TPU v7x, 32 devices: a whole 2x2x4 slice. The times are simulated.
32 devices in a mesh: dp: 8 (over z, x), tensor: 4 (over y, core).
Axes of the slice: x: 2, y: 2, z: 4, core: 2. Of those that a mesh axis runs over, the one named last changes fastest.
Arguments:
- bag_items: bfloat16 [16384, 64, 128], P('dp', 'tensor'), may hold values from -1.1953125 to 1.1953125
- bag_lengths: int32 [2048, 64], P('dp', 'tensor'), may hold values from 0 to 16, as said below
- send_counts: int32 [8, 8], P('dp'), may hold values from 0 to 48, as said below
- cross_weight: bfloat16 [1, 8192, 8192], P(None, 'tensor', 'dp'), may hold values from -0.0625 to 0.0625
- cross_bias: float32 [1, 8192], P(None, 'tensor'), may hold values from -3 to 3
Outputs:
- crossed: bfloat16 [2048, 8192], P('dp', 'tensor')
Inputs may be any that keep to these rules, and one draw needn't show every extreme that they name: `bag_lengths`: for every feature, the bags of the 256 rows of one aligned block hold 2048 items together; bags may be empty; in every aligned block and feature some bag holds exactly 16 items. `send_counts`: every row and every column sums to 256; each row has eight nonzero entries, one of them may be on the diagonal; no entry exceeds 48 and every row has an entry equal to 48.
All inputs are finite; a program needn't handle non-finite values.
Results may differ from a plain program's by a relative error of at most 0.0053.
Values may be sent and summed in bfloat16 or wider, within the bound.
No kernel may reach another device: no remote copies, remote signals or barrier semaphores. Data moves between devices by JAX's collectives and lax.ppermute only.
A program may use at most 128 MiB of HBM per device.

v0:
```python
import jax
import jax.numpy as jnp
from jax import lax
from jax.sharding import PartitionSpec as P

BAG = 8
CAP = 48


def shards(bag_items, bag_lengths, send_counts, cross_weight, cross_bias):
    row_count = bag_lengths.shape[0]
    feat_count = bag_lengths.shape[1]
    slot_count = bag_items.shape[0]
    embed_width = bag_items.shape[2]
    block_width = feat_count * embed_width
    bag_ends = jnp.cumsum(bag_lengths, axis=0)
    bag_starts = bag_ends - bag_lengths
    row_block = min(128, row_count)
    block_total = row_count // row_block
    window = min(slot_count, 2 * BAG * row_block)
    first_starts = bag_starts.reshape(block_total, row_block, feat_count)[:, 0, :]
    window_starts = jnp.clip(first_starts, 0, slot_count - window)
    feature_ids = jnp.arange(feat_count, dtype=jnp.int32)

    def take_window(start, feature):
        piece = lax.dynamic_slice(
            bag_items, (start, feature, jnp.int32(0)), (window, 1, embed_width)
        )
        return piece[:, 0, :]

    def pool_block(block_id):
        starts = window_starts[block_id]
        window_items = jax.vmap(take_window)(starts, feature_ids)
        row_first = (
            lax.dynamic_slice_in_dim(bag_starts, block_id * row_block, row_block, 0)
            - starts[None, :]
        )
        row_last = (
            lax.dynamic_slice_in_dim(bag_ends, block_id * row_block, row_block, 0) - starts[None, :]
        )
        positions = lax.broadcasted_iota(jnp.int32, (feat_count, row_block, window), 2)
        member = (positions >= row_first.T[:, :, None]) & (positions < row_last.T[:, :, None])
        one_hot = member.astype(jnp.bfloat16)
        return jnp.einsum("frs,fse->rfe", one_hot, window_items, preferred_element_type=jnp.float32)

    pooled_sum = lax.map(pool_block, jnp.arange(block_total, dtype=jnp.int32))
    pooled = pooled_sum.reshape(row_count, block_width).astype(jnp.bfloat16)
    device_count = lax.axis_size("dp")
    count_row = send_counts.reshape(-1)
    send_end = jnp.cumsum(count_row)
    send_start = send_end - count_row
    slot_ids = jnp.arange(CAP, dtype=jnp.int32)
    slot_index = jnp.minimum(send_start[:, None] + slot_ids[None, :], row_count - 1)
    slot_valid = slot_ids[None, :] < count_row[:, None]
    outgoing = jnp.where(slot_valid[:, :, None], pooled[slot_index], jnp.zeros((), jnp.bfloat16))
    received, recv_column = (
        lax.all_to_all(outgoing, "dp", split_axis=0, concat_axis=0, tiled=True),
        lax.all_to_all(
            count_row.reshape(device_count, 1), "dp", split_axis=0, concat_axis=0, tiled=True
        ),
    )
    recv_counts = recv_column.reshape(-1)
    recv_end = jnp.cumsum(recv_counts).astype(jnp.int32)
    recv_start = recv_end - recv_counts
    target_rows = jnp.arange(row_count, dtype=jnp.int32)
    source_block = jnp.sum((recv_end[None, :] <= target_rows[:, None]).astype(jnp.int32), axis=1)
    source_match = jnp.arange(device_count, dtype=jnp.int32)[None, :] == source_block[:, None]
    source_start = jnp.sum(jnp.where(source_match, recv_start[None, :], 0), axis=1)
    flat_index = source_block * CAP + target_rows - source_start
    cross_input = received.reshape(device_count * CAP, block_width)[flat_index]
    base_rows = cross_input.astype(jnp.float32)
    state = cross_input
    gathered = lax.all_gather(state, "tensor", axis=1, tiled=True)
    layer_weight = cross_weight[0]
    empty_sum = jnp.zeros((row_count, block_width), jnp.float32)
    w_piece = lax.all_gather(layer_weight, "dp", axis=1, tiled=True)
    columns = lax.slice_in_dim(gathered, 0, w_piece.shape[1], axis=1)
    product = empty_sum + lax.dot_general(
        columns, w_piece, (((1,), (1,)), ((), ())), preferred_element_type=jnp.float32
    )
    state = (base_rows * (product + cross_bias[0]) + state.astype(jnp.float32)).astype(jnp.bfloat16)
    return state


def solution(mesh):
    return jax.shard_map(
        shards,
        mesh=mesh,
        in_specs=(
            P("dp", "tensor", None),
            P("dp", "tensor"),
            P("dp", None),
            P(None, "tensor", "dp"),
            P(None, "tensor"),
        ),
        out_specs=P("dp", "tensor"),
        check_vma=False,
    )
```

profile of v0, /device:TPU:0, one launch (start us, length us, event | category | flops | bytes accessed | tf_op | source)
XLA Modules:
  0.0 814.9 jit_solution(1087858234139182849)
XLA Ops:
  6.5 1.3 copy.32
  7.9 7.3 all-to-all-start.1
  15.1 0.7 copy_bitcast_fusion.1
  15.8 0.6 reduce-window.25
  16.6 0.8 fusion.29
  17.6 12.3 %copy.30 = bf16[2048,16,128]{0,2,1:T(8,128)(2,1)} copy(bf16[2048,16,128]{2,1,0:T(8,128)(2,1)} %param.7) | data formatting | bytes 16777216
  29.9 37.9 %while.11 = (s32[]{:T(128)}, bf16[2,128,16,128]{1,3,2,0:T(8,128)(2,1)S(1)}, s32[2]{0:T(128)S(1)}, s32[2,16]{1,0:T(2,128)S(1)}, bf16[2048,16,128]{0,2,1:T(8,128)(...) while((s32[]{:T(128)}, ...), condition=%wide.region_3.4_spmd.clone, body=%wide.region_2.3_spmd.clone.sunk | while | flops 1086328960 | bytes 26264288 | solution.py:46
  29.9 0.6 dynamic_slice.31
  32.9 8.3 %gather_fusion = bf16[16,2048,128]{1,2,0:T(8,128)(2,1)} fusion(bf16[2048,16,128]{0,2,1:T(8,128)(2,1)} %get-tuple-element.190, s32[16]{0:T(128)S(1)} %fusion.40), kind=kCustom, calls=%fused_computation.clone.clone.1 | custom fusion | bytes 16777408 | tf_op jit(solution)/shard_map/while/body/eval_jaxpr/vmap()/gather | solution.py:26
  41.1 7.8 fusion.42
  48.9 0.6 dynamic_slice.31
  51.9 8.3 %gather_fusion = bf16[16,2048,128]{1,2,0:T(8,128)(2,1)} fusion(bf16[2048,16,128]{0,2,1:T(8,128)(2,1)} %get-tuple-element.190, s32[16]{0:T(128)S(1)} %fusion.40), kind=kCustom, calls=%fused_computation.clone.clone.1 | custom fusion | bytes 16777408 | tf_op jit(solution)/shard_map/while/body/eval_jaxpr/vmap()/gather | solution.py:26
  60.1 7.8 fusion.42
  67.9 1.0 copy.31
  68.9 0.3 copy.42
  69.6 2.4 gather_fusion.1
  72.0 1.3 broadcast_select_fusion
  73.4 6.0 all-to-all-start
  80.0 35.8 %all-to-all-done = bf16[8,48,2048]{2,1,0:T(8,128)(2,1)S(1)} async-done(((bf16[8,48,2048]{2,1,0:T(8,128)(2,1)}), bf16[8,48,2048]{2,1,0:T(8,128)(2,1)S(1)}, u32[]{:S(2)}, u32[]{:S(2)}) %all-to-all-start) | async-done | bytes 1572896 | tf_op jit(solution)/shard_map/all_to_all | solution.py:57
  115.8 2.3 gather_fusion.2
  118.2 0.7 all-gather.7.cloned.1.call-update
  118.9 33.0 %all-gather.5.cloned.1.call-done = bf16[256,8192]{1,0:T(8,128)(2,1)} async-done(((bf16[256,2048]{1,0:T(8,128)(2,1)}), bf16[256,8192]{1,0:T(8,128)(2,1)}) %all-gather.5.cloned.1.call-update) | async-done | bytes 4194320 | tf_op jit(solution)/shard_map/all_gather | solution.py:73
  151.9 639.3 %all-gather.7.cloned.1.call-done = bf16[1,2048,8192]{2,1,0:T(8,128)(2,1)} async-done(((bf16[1,2048,1024]{2,1,0:T(8,128)(2,1)}), bf16[1,2048,8192]{2,1,0:T(8,128)(2,1)}) %all-gather.7.cloned.1.call-update) | async-done | bytes 33554448 | tf_op jit(solution)/shard_map/all_gather | solution.py:76
  791.2 16.8 %fusion.26 = bf16[256,2048]{1,0:T(8,128)(2,1)} fusion(bf16[256,8192]{1,0:T(8,128)(2,1)} %all-gather.5.cloned.1.call-done, bf16[1,2048,8192]{2,1,0:T(8,128)(2,1)} %all-gather.7.cloned.1.call-done, bf16[256,2048]{1,0:T(8,128)(2,1)S(1)} %copy-done, f32[2048]{0:T(1024)S(1)} %bitcast.99), kind=kOutput, calls=%fused_computation.27 | convolution fusion | flops 8592556032 | bytes 39854080 | tf_op jit(solution)/shard_map/dot_general | solution.py:78
  (39 shorter events, 1.8 us)
Async XLA Ops:
  7.9 65.5 %all-to-all-start.1 = ((s32[8,1,1]{2,1,0:T(1,128)}), s32[8,1,1]{2,1,0:T(1,128)S(1)}, u32[]{:S(2)}, u32[]{:S(2)}) async-start(s32[8,1,1]{2,1,0:T(1,128)} %copy.32), calls=%async_computation.1 | async-start | bytes 8192 | tf_op jit(solution)/shard_map/all_to_all | solution.py:58
  67.9 1.3 copy-start.1
  73.4 42.4 %all-to-all-start = ((bf16[8,48,2048]{2,1,0:T(8,128)(2,1)}), bf16[8,48,2048]{2,1,0:T(8,128)(2,1)S(1)}, u32[]{:S(2)}, u32[]{:S(2)}) async-start(bf16[8,48,2048]{2,1,0:T(8,128)(2,1)} %broadcast_select_fusion), calls=%async_computation | async-start | bytes 3145728 | tf_op jit(solution)/shard_map/all_to_all | solution.py:57
  79.4 72.5 %all-gather.5.cloned.1.call-start = ((), (), s32[]{:S(2)}) async-start(), calls=%async_computation.2 | async-start | bytes 5242880 | tf_op jit(solution)/shard_map/all_gather | solution.py:73
  118.1 673.1 %copy-start = (bf16[256,2048]{1,0:T(8,128)(2,1)S(1)}, bf16[256,2048]{1,0:T(8,128)(2,1)}, u32[]{:S(2)}) copy-start(bf16[256,2048]{1,0:T(8,128)(2,1)} %gather_fusion.2) | copy-start | bytes 3145732
  118.1 673.1 %copy-start.2 = (f32[1,2048]{1,0:T(1,128)S(1)}, f32[1,2048]{1,0:T(1,128)}, u32[]{:S(2)}) copy-start(f32[1,2048]{1,0:T(1,128)} %param.11) | copy-start | bytes 24580
  118.2 673.0 %all-gather.7.cloned.1.call-start = ((), (), s32[]{:S(2)}) async-start(), calls=%async_computation.3 | async-start | bytes 37748736 | tf_op jit(solution)/shard_map/all_gather | solution.py:76
Sparse Core Ops, SparseCore 0:
  118.3 33.5 all-gather.4
  153.4 637.7 all-gather.6
where the time goes:
time: 816 us; the launch traced here: 815 us
  waiting for transfers between devices  709 us (87%)
  local copies, waits for them, and re-layouts  38.4 us (5%)
  matrix products  32.3 us (4%)
  between operations  13.5 us (2%)
  starting transfers between devices  13.3 us (2%)
    all_gather x1, waiting for transfers between devices, shards(): w_piece = lax.all_gather(layer_weight, 'dp', axis=1, tiled=True)  639 us
    all_to_all x1, waiting for transfers between devices, shards(): lax.all_to_all(outgoing, 'dp', split_axis=0, concat_axis=0, tiled=True)  35.8 us
    all_gather x1, waiting for transfers between devices, shards(): gathered = lax.all_gather(state, 'tensor', axis=1, tiled=True)  33 us
    dot_general x1, matrix products, shards(): lax.dot_general(columns, w_piece, (((1,), (1,)), ((), ())), preferred_ele...  16.8 us
    gather x2, local copies, waits for them, and re-layouts, take_window(): lax.dynamic_slice(bag_items, (start, feature, jnp.int32(0)), (window, 1,...  16.5 us
  transfers between devices with their start and end apart: 4, of which 3 were waited for; matrix products, arithmetic and copies ran while one was open for 7% of the time, Pallas kernels for 0%

commit v1 on v0

v1 whole, which is shorter than its diff:
```python
import functools

import jax
import jax.numpy as jnp
from jax import lax
from jax.experimental import pallas as pl
from jax.experimental.pallas import tpu as pltpu
from jax.sharding import Mesh
from jax.sharding import PartitionSpec as P

CAP = 48
BF16 = jnp.bfloat16
F32 = jnp.float32
I32 = jnp.int32
ANY = pl.ANY
VMEM = pltpu.VMEM
SMEM = pltpu.SMEM


def params(mib):
    return pltpu.CompilerParams(vmem_limit_bytes=mib << 20)


def pool_kernel(groups, share, quarter, count_ref, length_ref, items_ref, *rest):
    out_refs = rest[: len(groups)]
    items, wide, by_feat, first, last, pooled, sems = rest[len(groups) :]
    slots, feats, width = items.shape
    rows = length_ref.shape[1]
    step = slots // sems.shape[0]
    copies = []
    for k in range(sems.shape[0]):
        part = pl.ds(k * step, step)
        copy = pltpu.make_async_copy(items_ref.at[part], items.at[part], sems.at[k])
        copy.start()
        copies.append(copy)

    row_id = lax.broadcasted_iota(I32, (rows, rows), 0)
    col_id = lax.broadcasted_iota(I32, (rows, rows), 1)
    lower = jnp.where(col_id <= row_id, 1.0, 0.0).astype(BF16)
    strict = jnp.where(col_id < row_id, 1.0, 0.0).astype(BF16)
    lengths = length_ref[...].astype(F32).astype(BF16)
    dims = (((1,), (1,)), ((), ()))
    ends = lax.dot_general(lower, lengths, dims, preferred_element_type=F32).astype(I32)
    starts = lax.dot_general(strict, lengths, dims, preferred_element_type=F32).astype(I32)
    for f in range(feats):
        first[f] = jnp.broadcast_to(starts[:, f : f + 1], (rows, width))
        last[f] = jnp.broadcast_to(ends[:, f : f + 1], (rows, width))

    for k in range(sems.shape[0]):
        copies[k].wait()
        part = pl.ds(k * step, step)
        wide[...] = items[part].astype(F32).reshape(step * feats, width)
        for f in range(feats):
            by_feat[f, part, :] = wide[pl.ds(f, step, stride=feats), :].astype(BF16)

    lane = lax.broadcasted_iota(I32, (rows, width), 1)

    @pl.loop(0, feats)
    def _(f):
        low = first[f]
        high = last[f]
        total = jnp.zeros((rows, width), F32)
        for k in range(slots // (2 * width)):
            tiles = []
            for half in range(2):
                where = lane + (2 * k + half) * width
                inside = (where >= low) & (where < high)
                tiles.append(jnp.where(inside, 1.0, 0.0).astype(BF16))
            total += jnp.dot(
                jnp.concatenate(tiles, axis=1),
                by_feat[f, pl.ds(2 * k * width, 2 * width), :],
                preferred_element_type=F32,
            )
        pooled[:, pl.ds(pl.multiple_of(f * width, width), width)] = total.astype(BF16)

    slot = lax.broadcasted_iota(I32, (CAP, rows), 0)
    source = lax.broadcasted_iota(I32, (CAP, rows), 1)
    begin = []
    at = jnp.int32(0)
    for p in range(count_ref.shape[1]):
        begin.append(at)
        at = at + count_ref[0, p]
    for g, group in enumerate(groups):
        picks = []
        for b in range(share):
            for a in group:
                p = a * share + b
                hit = (source == slot + begin[p]) & (slot < count_ref[0, p])
                picks.append(jnp.where(hit, 1.0, 0.0).astype(BF16))
        pick = jnp.concatenate(picks, axis=0)
        for q in range(out_refs[g].shape[0]):
            moved = jnp.dot(
                pick, pooled[:, q * quarter : (q + 1) * quarter], preferred_element_type=F32
            )
            out_refs[g][q] = moved.astype(BF16)


def pool(bag_items, bag_lengths, send_counts, groups, share, quarters):
    slots, feats, width = bag_items.shape
    rows = bag_lengths.shape[0]
    quarter = feats * width // quarters
    chunks = 8
    return pl.pallas_call(
        functools.partial(pool_kernel, groups, share, quarter),
        out_shape=[
            jax.ShapeDtypeStruct((quarters, share * len(g) * CAP, quarter), BF16) for g in groups
        ],
        in_specs=[
            pl.BlockSpec(memory_space=SMEM),
            pl.BlockSpec(memory_space=VMEM),
            pl.BlockSpec(memory_space=ANY),
        ],
        out_specs=[pl.BlockSpec(memory_space=VMEM) for _ in groups],
        scratch_shapes=[
            VMEM((slots, feats, width), BF16),
            VMEM((slots // chunks * feats, width), F32),
            VMEM((feats, slots, width), BF16),
            VMEM((feats, rows, width), I32),
            VMEM((feats, rows, width), I32),
            VMEM((rows, feats * width), BF16),
            pltpu.SemaphoreType.DMA((chunks,)),
        ],
        compiler_params=params(48),
        cost_estimate=pl.CostEstimate(
            flops=2 * rows * slots * feats * width,
            bytes_accessed=2 * slots * feats * width,
            transcendentals=0,
        ),
        name="pool",
    )(send_counts, bag_lengths.T, bag_items)


def order_kernel(group, share, rows, place_ref, counts_ref, slots_ref, out_ref):
    sources = slots_ref.shape[0]
    lane = lax.broadcasted_iota(I32, (rows, sources * CAP), 1)
    place = lax.broadcasted_iota(I32, (rows, sources * CAP), 0)
    b = place_ref[0]
    for g, a in enumerate(group):
        want = jnp.full((rows, sources * CAP), -1, I32)
        at = jnp.int32(0)
        for k in range(sources):
            count = counts_ref[k, a * share + b]
            slot = lane - k * CAP
            want = jnp.where((slot >= 0) & (slot < count), slot + at, want)
            at = at + count
        pick = jnp.where(want == place, 1.0, 0.0).astype(BF16)
        got = slots_ref[:, g * CAP : (g + 1) * CAP, :].reshape(sources * CAP, slots_ref.shape[2])
        out_ref[g] = jnp.dot(pick, got, preferred_element_type=F32).astype(BF16)


def order(place, counts, slots, group, share, rows):
    quarter = slots.shape[2]
    return pl.pallas_call(
        functools.partial(order_kernel, group, share, rows),
        out_shape=jax.ShapeDtypeStruct((len(group), rows, quarter), BF16),
        in_specs=[
            pl.BlockSpec(memory_space=SMEM),
            pl.BlockSpec(memory_space=SMEM),
            pl.BlockSpec(memory_space=VMEM),
        ],
        out_specs=pl.BlockSpec(memory_space=VMEM),
        compiler_params=params(32),
        cost_estimate=pl.CostEstimate(
            flops=2 * len(group) * rows * slots.shape[0] * CAP * quarter,
            bytes_accessed=2 * slots.size,
            transcendentals=0,
        ),
        name="order",
    )(place, counts, slots)


def multiply_kernel(count, spot_ref, *refs):
    pieces = refs[:count]
    own_ref, other_ref, out_ref, held = refs[count:]

    @pl.when(pl.program_id(0) == 0)
    def _():
        for j in range(count):
            held[spot_ref[j]] = pieces[j][...].reshape(held.shape[1:])

    quarter = held.shape[2]
    half = count // 2
    total = None
    for j in range(count):
        weight = own_ref if j < half else other_ref
        part = lax.dot_general(
            held[j],
            weight[:, (j % half) * quarter : (j % half + 1) * quarter],
            (((1,), (1,)), ((), ())),
            preferred_element_type=F32,
        )
        total = part if total is None else total + part
    out_ref[...] = total.astype(BF16).reshape(out_ref.shape)


def multiply(spots, pieces, own, other, offset, tile):
    blocks, rows, quarter = pieces[0].shape
    count = len(pieces)
    outs, depth = other.shape
    base = offset // tile
    return pl.pallas_call(
        functools.partial(multiply_kernel, count),
        out_shape=jax.ShapeDtypeStruct((blocks, rows, outs), BF16),
        grid=(outs // tile,),
        in_specs=[pl.BlockSpec(memory_space=SMEM)]
        + [
            pl.BlockSpec((blocks, rows, quarter), lambda n: (0, 0, 0), pipeline_mode=pl.Buffered(1))
            for _ in pieces
        ]
        + [
            pl.BlockSpec((tile, depth), lambda n: (n + base, 0)),
            pl.BlockSpec((tile, depth), lambda n: (n, 0)),
        ],
        out_specs=pl.BlockSpec((blocks, rows, tile), lambda n: (0, 0, n)),
        scratch_shapes=[VMEM((count, blocks * rows, quarter), BF16)],
        compiler_params=params(32),
        cost_estimate=pl.CostEstimate(
            flops=4 * blocks * rows * outs * depth,
            bytes_accessed=2 * (2 * outs * depth + blocks * rows * (outs + count * quarter)),
            transcendentals=0,
        ),
        name="multiply",
    )(spots, *pieces, own, other)


def pick(index, options):
    value = options[0][1]
    for which, other in options[1:]:
        value = jnp.where(index == which, other, value)
    return value


def shards(bag_items, bag_lengths, send_counts, cross_weight, cross_bias):
    line, share = lax.axis_size("a"), lax.axis_size("b")
    tall = lax.axis_size("y")
    quarters = tall * 2
    rows = bag_lengths.shape[0]
    a, b = lax.axis_index("a"), lax.axis_index("b")
    y, c = lax.axis_index("y"), lax.axis_index("c")
    swap = [(0, 1), (1, 0)]
    edge = line // 4
    groups = [
        list(range(edge)) + list(range(line - edge, line)),
        list(range(edge, line - edge)),
    ]

    weight = cross_weight[0]
    outs = weight.shape[0]
    parts = 2
    each = outs // parts
    others = [
        lax.ppermute(weight[n * each : (n + 1) * each], "b", swap) for n in range(parts)
    ]
    counts = lax.all_gather(send_counts, ("a", "b"), axis=0, tiled=True)
    padded = pool(bag_items, bag_lengths, send_counts, groups, share, quarters)

    place = b.reshape(1).astype(I32)
    ordered, pieces = [], []
    for g, group in enumerate(groups):
        mixed = lax.all_to_all(padded[g], ("y", "c"), 0, 0, tiled=True)
        mixed = mixed.reshape(line * share, len(group) * CAP, mixed.shape[2])
        slots = lax.all_to_all(mixed, ("a", "b"), 0, 0, tiled=True)
        mine = order(place, counts, slots, group, share, rows)
        ordered.append(mine)
        if tall == 2:
            far = lax.ppermute(mine, "y", swap)
            near = [(y, mine), (1 - y, far)]
        else:
            every = lax.all_gather(mine, "y", axis=0)
            near = [(jnp.int32(k), every[k]) for k in range(tall)]
        found = [(k, c, piece) for k, piece in near]
        found += [(k, 1 - c, lax.ppermute(piece, "c", swap)) for k, piece in near]
        pieces.append(found)

    half = quarters // 2
    spots = []
    for k, core, _ in pieces[0]:
        quarter_id = k * 2 + core
        spots.append(jnp.where(quarter_id // half == b, 0, half) + quarter_id % half)
    spots = jnp.stack(spots).astype(I32)

    tile = min(512, each)
    columns = []
    for n in range(parts):
        block = {}
        for g, group in enumerate(groups):
            partial = multiply(
                spots, [piece for _, _, piece in pieces[g]], weight, others[n], n * each, tile
            )
            for k, which in enumerate(group):
                block[which] = partial[k]
        up = down = None
        for s in range(1, line):
            send_up = pick(a, [(i, block[line - s + i]) for i in range(s)])
            send_down = pick(a, [(line - 1 - i, block[s - 1 - i]) for i in range(s)])
            if up is not None:
                send_up = send_up + up
                send_down = send_down + down
            up = lax.ppermute(send_up, "a", [(i, i + 1) for i in range(s)])
            down = lax.ppermute(
                send_down, "a", [(line - 1 - i, line - 2 - i) for i in range(s)]
            )
        mine = pick(a, [(i, block[i]) for i in range(line)])
        columns.append(mine.astype(F32) + up.astype(F32) + down.astype(F32))
    product = jnp.concatenate(columns, axis=1)

    blocks = [None] * line
    for g, group in enumerate(groups):
        for k, which in enumerate(group):
            blocks[which] = ordered[g][k]
    back = lax.all_to_all(jnp.stack(blocks), "a", 0, 0, tiled=True)
    back = lax.all_to_all(back, ("y", "c"), 0, 0, tiled=True)
    base = jnp.transpose(back, (1, 0, 2)).reshape(rows, -1).astype(F32)
    return (base * (product + cross_bias[0]) + base).astype(BF16)


def solution(mesh):
    owners, tensor = mesh.devices.shape
    split = Mesh(
        mesh.devices.reshape(tensor, owners // tensor, tensor // 2, 2), ("a", "b", "y", "c")
    )
    dp, tp = ("a", "b"), ("y", "c")
    return jax.shard_map(
        shards,
        mesh=split,
        in_specs=(
            P(dp, tp, None),
            P(dp, tp),
            P(dp, None),
            P(None, tp, dp),
            P(None, tp),
        ),
        out_specs=P(dp, tp),
        check_vma=False,
    )
```

time: 816 us -> 317 us (0.39)
  waiting for transfers between devices: 709 us -> 57.7 us
  blocking collectives: 0 us -> 126 us
  starting transfers between devices: 13.3 us -> 59.2 us
  Pallas kernels: 0 us -> 39.8 us
  matrix products: 32.3 us -> 0 us
  local copies, waits for them, and re-layouts: 38.4 us -> 13.6 us
  other arithmetic: 3.95 us -> 19.7 us
  between operations: 13.5 us -> 0.31 us
    all_gather x2 -> x0, waiting for transfers between devices: 672 us -> none  [the longest x1 639 us: shards(): w_piece = lax.all_gather(layer_weight, 'dp', axis=1, tiled=True)]
    all_gather x0 -> x1, blocking collectives: none -> 95.1 us  [shards(): counts = lax.all_gather(send_counts, ('a', 'b'), axis=0, tiled=True)]
    ppermute x0 -> x20, waiting for transfers between devices: none -> 44.5 us  [the longest x6 19.1 us: shards(): lax.ppermute(send_down, 'a', [(line - 1 - i, line - 2 - i) for i in range...]
    ppermute x0 -> x20, starting transfers between devices: none -> 40.2 us  [the longest x6 25.2 us: shards(): up = lax.ppermute(send_up, 'a', [(i, i + 1) for i in range(s)])]
    pallas_call x0 -> x7, Pallas kernels: none -> 39.8 us  [the longest x1 19.7 us: pool(): pl.pallas_call(functools.partial(pool_kernel, groups, share, quarter), ou...]
    dot_general x3 -> x0, matrix products: 32.3 us -> none  [the longest x1 16.8 us: shards(): lax.dot_general(columns, w_piece, (((1,), (1,)), ((), ())), preferred_ele...]
    all_to_all x0 -> x2, blocking collectives: none -> 30.6 us  [shards(): mixed = lax.all_to_all(padded[g], ('y', 'c'), 0, 0, tiled=True)]
    all_to_all x2 -> x4, waiting for transfers between devices: 35.8 us -> 13.2 us  [the longest x2 13.2 us: shards(): slots = lax.all_to_all(mixed, ('a', 'b'), 0, 0, tiled=True)]
  transfers between devices with their start and end apart: 4 -> 24, of which waited for: 3 -> 8; matrix products, arithmetic and copies ran while one was open for 7% -> 7% of each run, Pallas kernels for 0% -> 6%
where the time goes in v1:
time: 317 us; the launch traced here: 316 us
  blocking collectives  126 us (40%)
  starting transfers between devices  59.2 us (19%)
  waiting for transfers between devices  57.7 us (18%)
  Pallas kernels  39.8 us (13%)
  other arithmetic  19.7 us (6%)
  local copies, waits for them, and re-layouts  13.6 us (4%)
    all_gather x1, blocking collectives, shards(): counts = lax.all_gather(send_counts, ('a', 'b'), axis=0, tiled=True)  95.1 us
    all_to_all x2, blocking collectives, shards(): mixed = lax.all_to_all(padded[g], ('y', 'c'), 0, 0, tiled=True)  30.6 us
    ppermute x6, starting transfers between devices, shards(): up = lax.ppermute(send_up, 'a', [(i, i + 1) for i in range(s)])  25.2 us
    pallas_call x1, Pallas kernels, pool(): pl.pallas_call(functools.partial(pool_kernel, groups, share, quarter), ou...  19.7 us
    ppermute x6, waiting for transfers between devices, shards(): lax.ppermute(send_down, 'a', [(line - 1 - i, line - 2 - i) for i in range...  19.1 us
    pallas_call x4, Pallas kernels, multiply(): pl.pallas_call(functools.partial(multiply_kernel, count), out_shape=jax.S...  16.7 us
    ppermute x6, waiting for transfers between devices, shards(): up = lax.ppermute(send_up, 'a', [(i, i + 1) for i in range(s)])  14.9 us
    all_to_all x2, waiting for transfers between devices, shards(): slots = lax.all_to_all(mixed, ('a', 'b'), 0, 0, tiled=True)  13.2 us
  transfers between devices with their start and end apart: 24, of which 8 were waited for; matrix products, arithmetic and copies ran while one was open for 7% of the time, Pallas kernels for 6%

profile of v1, /device:TPU:0, one launch (start us, length us, event | category | flops | bytes accessed | tf_op | source)
XLA Modules:
  0.0 315.9 jit_solution(13313244805520724578)
XLA Ops:
  1.4 19.7 %pool.1 = (bf16[4,192,512]{2,1,0:T(8,128)(2,1)S(1)}, bf16[4,192,512]{2,1,0:T(8,128)(2,1)S(1)}) custom-call(s32[1,8]{1,0:T(1,128)S(1)} %copy-done.14, s32[16,256]{1,0:T(8,128)S(1)} %bitcast.98, bf16[2048,16,128]{2,1,0:T(8,128)(2,1)} %items_ref.1), custom_call_target="tpu_custom_call" | custom-call | flops 2147483648 | bytes 8388608 | tf_op jit(solution)/shard_map/pool/pallas_call | solution.py:103
  21.1 15.8 %all_to_all.30 = bf16[4,192,512]{2,1,0:T(8,128)(2,1)} all-to-all(bf16[4,192,512]{2,1,0:T(8,128)(2,1)S(1)} %get-tuple-element.7), channel_id=1, replica_groups=mesh['a'=4,'b'=2,'y'=2,'c'=2] {'y','c'}, dimensions={0} | all-to-all | bytes 1572864 | tf_op jit(solution)/shard_map/all_to_all | solution.py:260
  36.9 14.8 %all_to_all.31 = bf16[4,192,512]{2,1,0:T(8,128)(2,1)} all-to-all(bf16[4,192,512]{2,1,0:T(8,128)(2,1)S(1)} %get-tuple-element.8), channel_id=1, replica_groups=mesh['a'=4,'b'=2,'y'=2,'c'=2] {'y','c'}, dimensions={0} | all-to-all | bytes 1572864 | tf_op jit(solution)/shard_map/all_to_all | solution.py:260
  51.6 6.2 %all-to-all-start.1 = ((bf16[8,96,512]{2,1,0:T(8,128)(2,1)}), bf16[8,96,512]{2,1,0:T(8,128)(2,1)S(1)}, u32[]{:S(2)}, u32[]{:S(2)}) async-start(bf16[8,96,512]{2,1,0:T(8,128)(2,1)} %bitcast.102), calls=%async_computation.1 | async-start | bytes 1572864 | tf_op jit(solution)/shard_map/all_to_all | solution.py:262
  57.9 4.7 %slice_bitcast_fusion.1 = (bf16[1024,1024]{1,0:T(8,128)(2,1)}, bf16[1024,1024]{1,0:T(8,128)(2,1)}) fusion(bf16[1,2048,1024]{2,1,0:T(8,128)(2,1)} %param.8), kind=kLoop, calls=%fused_computation.5 | loop fusion | bytes 8388608 | tf_op jit(solution)/shard_map/slice | solution.py:252
  64.6 13.2 %all-to-all-done.1.slots_ref = bf16[8,96,512]{2,1,0:T(8,128)(2,1)S(1)} async-done(((bf16[8,96,512]{2,1,0:T(8,128)(2,1)}), bf16[8,96,512]{2,1,0:T(8,128)(2,1)S(1)}, u32[]{:S(2)}, u32[]{:S(2)}) %all-to-all-start.1) | async-done | bytes 786464 | tf_op jit(solution)/shard_map/all_to_all | solution.py:262
  77.7 4.2 %all-to-all-start.3 = ((bf16[8,96,512]{2,1,0:T(8,128)(2,1)}), bf16[8,96,512]{2,1,0:T(8,128)(2,1)}, u32[]{:S(2)}, u32[]{:S(2)}) async-start(bf16[8,96,512]{2,1,0:T(8,128)(2,1)} %bitcast.101), calls=%async_computation.3 | async-start | bytes 1572864 | tf_op jit(solution)/shard_map/all_to_all | solution.py:262
  83.8 95.1 %all-gather = s32[8,1,8]{2,1,0:T(1,128)S(1)} all-gather(s32[1,1,8]{2,1,0:T(1,128)S(1)} %bitcast.99), channel_id=1, replica_groups=mesh['a'=4,'b'=2,'y'=2,'c'=2] {'a','b'}, dimensions={0}, use_global_device_ids=true | all-gather | bytes 288 | tf_op jit(solution)/shard_map/all_gather | solution.py:254
  185.6 10.4 %collective-permute-done.refs_1_ = bf16[2,256,512]{2,1,0:T(8,128)(2,1)S(1)} collective-permute-done((bf16[2,256,512]{2,1,0:T(8,128)(2,1)S(1)}, bf16[2,256,512]{2,1,0:T(8,128)(2,1)S(1)}, u32[]{:S(2)}, u32[]{:S(2)}) %collective-permute-start) | collective-permute-done | bytes 524320 | tf_op jit(solution)/shard_map/ppermute | solution.py:266
  198.4 4.3 %all-to-all-start.4 = ((bf16[4,256,512]{2,1,0:T(8,128)(2,1)}), bf16[4,256,512]{2,1,0:T(8,128)(2,1)}, u32[]{:S(2)}, u32[]{:S(2)}) async-start(bf16[4,256,512]{2,1,0:T(8,128)(2,1)} %pad_maximum_fusion), calls=%async_computation.4 | async-start | bytes 2097152 | tf_op jit(solution)/shard_map/all_to_all | solution.py:311
  207.7 4.0 %multiply.4 = bf16[2,256,1024]{2,1,0:T(8,128)(2,1)S(1)} custom-call(s32[4]{0:T(128)S(1)} %pad_add_fusion.spot_ref, bf16[2,256,512]{2,1,0:T(8,128)(2,1)S(1)} %copy-done.6, bf16[2,256,512]{2,1,0:T(8,128)(2,1)S(1)} %copy-done.11, bf16[2,256,512]{2,1,0:T(8,128)(2,1)} %collective-permute-done.1.refs_2_, bf16[2,256,512]{2,1,0:T(8,128)(2,1)} %collective-permute-done.2.refs_3_, ...), custom_call_target="tpu_custom_call" | custom-call | flops 2147483648 | bytes 7340032 | tf_op jit(solution)/shard_map/multiply/pallas_call | solution.py:201
  212.6 3.9 %collective-permute-start.7 = (bf16[256,1024]{1,0:T(8,128)(2,1)S(1)}, bf16[256,1024]{1,0:T(8,128)(2,1)S(1)}, u32[]{:S(2)}, u32[]{:S(2)}) collective-permute-start(bf16[256,1024]{1,0:T(8,128)(2,1)S(1)} %get-tuple-element.15), channel_id=1, source_target_pairs={{0,8},{1,9},{2,10},{3,11},{4,12},{5,13},{6,14},{7,15}} | collective-permute-start | bytes 1572872 | tf_op jit(solution)/shard_map/ppermute | solution.py:299
  217.9 4.3 %multiply.6 = bf16[2,256,1024]{2,1,0:T(8,128)(2,1)S(1)} custom-call(s32[4]{0:T(128)S(1)} %pad_add_fusion.spot_ref, bf16[2,256,512]{2,1,0:T(8,128)(2,1)S(1)} %copy-done.7, bf16[2,256,512]{2,1,0:T(8,128)(2,1)S(1)} %copy-done.12, bf16[2,256,512]{2,1,0:T(8,128)(2,1)} %collective-permute-done.1.refs_2_, bf16[2,256,512]{2,1,0:T(8,128)(2,1)} %collective-permute-done.2.refs_3_, ...), custom_call_target="tpu_custom_call" | custom-call | flops 2147483648 | bytes 7340032 | tf_op jit(solution)/shard_map/multiply/pallas_call | solution.py:201
  226.0 4.0 %multiply.5 = bf16[2,256,1024]{2,1,0:T(8,128)(2,1)S(1)} custom-call(s32[4]{0:T(128)S(1)} %pad_add_fusion.spot_ref, bf16[2,256,512]{2,1,0:T(8,128)(2,1)} %order.3.refs_0_, bf16[2,256,512]{2,1,0:T(8,128)(2,1)} %collective-permute-done.4.refs_1_, bf16[2,256,512]{2,1,0:T(8,128)(2,1)S(1)} %collective-permute-done.5.refs_2_, ...), custom_call_target="tpu_custom_call" | custom-call | flops 2147483648 | bytes 7340032 | tf_op jit(solution)/shard_map/multiply/pallas_call | solution.py:201
  232.9 5.2 %collective-permute-start.8 = (bf16[256,1024]{1,0:T(8,128)(2,1)}, bf16[256,1024]{1,0:T(8,128)(2,1)}, u32[]{:S(2)}, u32[]{:S(2)}) collective-permute-start(bf16[256,1024]{1,0:T(8,128)(2,1)} %select_add_fusion.6), channel_id=1, source_target_pairs={{0,8},{8,16},{1,9},{9,17},{2,10},{10,18},{3,11},{11,19},{4,12},{12... | collective-permute-start | bytes 1572872 | tf_op jit(solution)/shard_map/ppermute | solution.py:299
  238.1 4.3 %multiply.7 = bf16[2,256,1024]{2,1,0:T(8,128)(2,1)S(1)} custom-call(s32[4]{0:T(128)S(1)} %pad_add_fusion.spot_ref, bf16[2,256,512]{2,1,0:T(8,128)(2,1)} %order.3.refs_0_, bf16[2,256,512]{2,1,0:T(8,128)(2,1)} %collective-permute-done.4.refs_1_, bf16[2,256,512]{2,1,0:T(8,128)(2,1)S(1)} %collective-permute-done.5.refs_2_, ...), custom_call_target="tpu_custom_call" | custom-call | flops 2147483648 | bytes 7340032 | tf_op jit(solution)/shard_map/multiply/pallas_call | solution.py:201
  244.2 5.2 %collective-permute-start.15 = (bf16[256,1024]{1,0:T(8,128)(2,1)}, bf16[256,1024]{1,0:T(8,128)(2,1)}, u32[]{:S(2)}, u32[]{:S(2)}) collective-permute-start(bf16[256,1024]{1,0:T(8,128)(2,1)} %select_add_fusion.2), channel_id=1, source_target_pairs={{0,8},{8,16},{1,9},{9,17},{2,10},{10,18},{3,11},{11,19},{4,12},{12... | collective-permute-start | bytes 1572872 | tf_op jit(solution)/shard_map/ppermute | solution.py:299
  249.4 5.3 %collective-permute-done.8 = bf16[256,1024]{1,0:T(8,128)(2,1)} collective-permute-done((bf16[256,1024]{1,0:T(8,128)(2,1)}, bf16[256,1024]{1,0:T(8,128)(2,1)}, u32[]{:S(2)}, u32[]{:S(2)}) %collective-permute-start.8) | collective-permute-done | bytes 524320 | tf_op jit(solution)/shard_map/ppermute | solution.py:299
  258.8 6.8 %collective-permute-done.15 = bf16[256,1024]{1,0:T(8,128)(2,1)} collective-permute-done((bf16[256,1024]{1,0:T(8,128)(2,1)}, bf16[256,1024]{1,0:T(8,128)(2,1)}, u32[]{:S(2)}, u32[]{:S(2)}) %collective-permute-start.15) | collective-permute-done | bytes 524320 | tf_op jit(solution)/shard_map/ppermute | solution.py:299
  269.4 4.2 %all-to-all-start.5 = ((bf16[4,256,512]{2,1,0:T(8,128)(2,1)}), bf16[4,256,512]{2,1,0:T(8,128)(2,1)}, u32[]{:S(2)}, u32[]{:S(2)}) async-start(bf16[4,256,512]{2,1,0:T(8,128)(2,1)} %all-to-all-done.4), calls=%async_computation.5 | async-start | bytes 2097152 | tf_op jit(solution)/shard_map/all_to_all | solution.py:312
  273.6 5.0 %collective-permute-start.9 = (bf16[256,1024]{1,0:T(8,128)(2,1)}, bf16[256,1024]{1,0:T(8,128)(2,1)}, u32[]{:S(2)}, u32[]{:S(2)}) collective-permute-start(bf16[256,1024]{1,0:T(8,128)(2,1)} %get-tuple-element.11), channel_id=1, source_target_pairs={{0,8},{8,16},{16,24},{1,9},{9,17},{17,25},{2,10},{10,18},{18,26},{... | collective-permute-start | bytes 1572872 | tf_op jit(solution)/shard_map/ppermute | solution.py:299
  278.7 4.6 %collective-permute-start.16 = (bf16[256,1024]{1,0:T(8,128)(2,1)}, bf16[256,1024]{1,0:T(8,128)(2,1)}, u32[]{:S(2)}, u32[]{:S(2)}) collective-permute-start(bf16[256,1024]{1,0:T(8,128)(2,1)} %get-tuple-element.13), channel_id=1, source_target_pairs={{0,8},{8,16},{16,24},{1,9},{9,17},{17,25},{2,10},{10,18},{18,26},{... | collective-permute-start | bytes 1572872 | tf_op jit(solution)/shard_map/ppermute | solution.py:299
  291.8 10.8 %collective-permute-done.12 = bf16[256,1024]{1,0:T(8,128)(2,1)} collective-permute-done((bf16[256,1024]{1,0:T(8,128)(2,1)}, bf16[256,1024]{1,0:T(8,128)(2,1)}, u32[]{:S(2)}, u32[]{:S(2)}) %collective-permute-start.12) | collective-permute-done | bytes 524320 | tf_op jit(solution)/shard_map/ppermute | solution.py:300
  304.3 8.3 %collective-permute-done.19 = bf16[256,1024]{1,0:T(8,128)(2,1)} collective-permute-done((bf16[256,1024]{1,0:T(8,128)(2,1)}, bf16[256,1024]{1,0:T(8,128)(2,1)}, u32[]{:S(2)}, u32[]{:S(2)}) %collective-permute-start.19) | collective-permute-done | bytes 524320 | tf_op jit(solution)/shard_map/ppermute | solution.py:300
  (85 shorter events, 51.3 us)
Async XLA Ops:
  51.6 26.1 %all-to-all-start.1 = ((bf16[8,96,512]{2,1,0:T(8,128)(2,1)}), bf16[8,96,512]{2,1,0:T(8,128)(2,1)S(1)}, u32[]{:S(2)}, u32[]{:S(2)}) async-start(bf16[8,96,512]{2,1,0:T(8,128)(2,1)} %bitcast.102), calls=%async_computation.1 | async-start | bytes 1572864 | tf_op jit(solution)/shard_map/all_to_all | solution.py:262
  62.6 140.1 %collective-permute-start.3 = (bf16[1024,1024]{1,0:T(8,128)(2,1)}, bf16[1024,1024]{1,0:T(8,128)(2,1)S(1)}, u32[]{:S(2)}, u32[]{:S(2)}) collective-permute-start(bf16[1024,1024]{1,0:T(8,128)(2,1)} %get-tuple-element.9), channel_id=1, source_target_pairs={{0,4},{4,0},{1,5},{5,1},{2,6},{6,2},{3,7},{7,3},{8,12},{12,8},{9,1... | collective-permute-start | bytes 6291464 | tf_op jit(solution)/shard_map/ppermute | solution.py:252
  77.7 104.2 %all-to-all-start.3 = ((bf16[8,96,512]{2,1,0:T(8,128)(2,1)}), bf16[8,96,512]{2,1,0:T(8,128)(2,1)}, u32[]{:S(2)}, u32[]{:S(2)}) async-start(bf16[8,96,512]{2,1,0:T(8,128)(2,1)} %bitcast.101), calls=%async_computation.3 | async-start | bytes 1572864 | tf_op jit(solution)/shard_map/all_to_all | solution.py:262
  81.9 136.0 %collective-permute-start.13 = (bf16[1024,1024]{1,0:T(8,128)(2,1)}, bf16[1024,1024]{1,0:T(8,128)(2,1)}, u32[]{:S(2)}, u32[]{:S(2)}) collective-permute-start(bf16[1024,1024]{1,0:T(8,128)(2,1)} %get-tuple-element.10), channel_id=1, source_target_pairs={{0,4},{4,0},{1,5},{5,1},{2,6},{6,2},{3,7},{7,3},{8,12},{12,8},{9,1... | collective-permute-start | bytes 6291464 | tf_op jit(solution)/shard_map/ppermute | solution.py:252
  181.1 14.9 %collective-permute-start = (bf16[2,256,512]{2,1,0:T(8,128)(2,1)S(1)}, bf16[2,256,512]{2,1,0:T(8,128)(2,1)S(1)}, u32[]{:S(2)}, u32[]{:S(2)}) collective-permute-start(bf16[2,256,512]{2,1,0:T(8,128)(2,1)S(1)} %order.2.refs_0_), channel_id=1, source_target_pairs={{0,2},{2,0},{1,3},{3,1},{4,6},{6,4},{5,7},{7,5},{8,10},{10,8},{9,1... | collective-permute-start | bytes 1572872 | tf_op jit(solution)/shard_map/ppermute | solution.py:266
  184.4 18.8 %collective-permute-start.4 = (bf16[2,256,512]{2,1,0:T(8,128)(2,1)}, bf16[2,256,512]{2,1,0:T(8,128)(2,1)}, u32[]{:S(2)}, u32[]{:S(2)}) collective-permute-start(bf16[2,256,512]{2,1,0:T(8,128)(2,1)} %order.3.refs_0_), channel_id=1, source_target_pairs={{0,2},{2,0},{1,3},{3,1},{4,6},{6,4},{5,7},{7,5},{8,10},{10,8},{9,1... | collective-permute-start | bytes 1572872 | tf_op jit(solution)/shard_map/ppermute | solution.py:266
  185.6 17.6 %collective-permute-start.1 = (bf16[2,256,512]{2,1,0:T(8,128)(2,1)S(1)}, bf16[2,256,512]{2,1,0:T(8,128)(2,1)}, u32[]{:S(2)}, u32[]{:S(2)}) collective-permute-start(bf16[2,256,512]{2,1,0:T(8,128)(2,1)S(1)} %order.2.refs_0_), channel_id=1, source_target_pairs={{0,1},{1,0},{2,3},{3,2},{4,5},{5,4},{6,7},{7,6},{8,9},{9,8},{10,11... | collective-permute-start | bytes 1572872 | tf_op jit(solution)/shard_map/ppermute | solution.py:272
  196.1 7.2 %collective-permute-start.2 = (bf16[2,256,512]{2,1,0:T(8,128)(2,1)S(1)}, bf16[2,256,512]{2,1,0:T(8,128)(2,1)}, u32[]{:S(2)}, u32[]{:S(2)}) collective-permute-start(bf16[2,256,512]{2,1,0:T(8,128)(2,1)S(1)} %collective-permute-done.refs_1_), channel_id=1, source_target_pairs={{0,1},{1,0},{2,3},{3,2},{4,5},{5,4},{6,7},{7,6},{8,9},{9,8},{10,11... | collective-permute-start | bytes 1572872 | tf_op jit(solution)/shard_map/ppermute | solution.py:272
  198.4 71.0 %all-to-all-start.4 = ((bf16[4,256,512]{2,1,0:T(8,128)(2,1)}), bf16[4,256,512]{2,1,0:T(8,128)(2,1)}, u32[]{:S(2)}, u32[]{:S(2)}) async-start(bf16[4,256,512]{2,1,0:T(8,128)(2,1)} %pad_maximum_fusion), calls=%async_computation.4 | async-start | bytes 2097152 | tf_op jit(solution)/shard_map/all_to_all | solution.py:311
  202.7 21.8 %collective-permute-start.5 = (bf16[2,256,512]{2,1,0:T(8,128)(2,1)}, bf16[2,256,512]{2,1,0:T(8,128)(2,1)S(1)}, u32[]{:S(2)}, u32[]{:S(2)}) collective-permute-start(bf16[2,256,512]{2,1,0:T(8,128)(2,1)} %order.3.refs_0_), channel_id=1, source_target_pairs={{0,1},{1,0},{2,3},{3,2},{4,5},{5,4},{6,7},{7,6},{8,9},{9,8},{10,11... | collective-permute-start | bytes 1572872 | tf_op jit(solution)/shard_map/ppermute | solution.py:272
  203.2 22.8 %collective-permute-start.6 = (bf16[2,256,512]{2,1,0:T(8,128)(2,1)}, bf16[2,256,512]{2,1,0:T(8,128)(2,1)S(1)}, u32[]{:S(2)}, u32[]{:S(2)}) collective-permute-start(bf16[2,256,512]{2,1,0:T(8,128)(2,1)} %collective-permute-done.4.refs_1_), channel_id=1, source_target_pairs={{0,1},{1,0},{2,3},{3,2},{4,5},{5,4},{6,7},{7,6},{8,9},{9,8},{10,11... | collective-permute-start | bytes 1572872 | tf_op jit(solution)/shard_map/ppermute | solution.py:272
  212.6 19.5 %collective-permute-start.7 = (bf16[256,1024]{1,0:T(8,128)(2,1)S(1)}, bf16[256,1024]{1,0:T(8,128)(2,1)S(1)}, u32[]{:S(2)}, u32[]{:S(2)}) collective-permute-start(bf16[256,1024]{1,0:T(8,128)(2,1)S(1)} %get-tuple-element.15), channel_id=1, source_target_pairs={{0,8},{1,9},{2,10},{3,11},{4,12},{5,13},{6,14},{7,15}} | collective-permute-start | bytes 1572872 | tf_op jit(solution)/shard_map/ppermute | solution.py:299
  216.5 32.9 %collective-permute-start.10 = (bf16[256,1024]{1,0:T(8,128)(2,1)}, bf16[256,1024]{1,0:T(8,128)(2,1)}, u32[]{:S(2)}, u32[]{:S(2)}) collective-permute-start(bf16[256,1024]{1,0:T(8,128)(2,1)} %get-tuple-element.16), channel_id=1, source_target_pairs={{24,16},{25,17},{26,18},{27,19},{28,20},{29,21},{30,22},{31,23}} | collective-permute-start | bytes 1572872 | tf_op jit(solution)/shard_map/ppermute | solution.py:300
  223.2 20.1 %collective-permute-start.14 = (bf16[256,1024]{1,0:T(8,128)(2,1)S(1)}, bf16[256,1024]{1,0:T(8,128)(2,1)S(1)}, u32[]{:S(2)}, u32[]{:S(2)}) collective-permute-start(bf16[256,1024]{1,0:T(8,128)(2,1)S(1)} %get-tuple-element.17), channel_id=1, source_target_pairs={{0,8},{1,9},{2,10},{3,11},{4,12},{5,13},{6,14},{7,15}} | collective-permute-start | bytes 1572872 | tf_op jit(solution)/shard_map/ppermute | solution.py:299
  224.5 34.3 %collective-permute-start.17 = (bf16[256,1024]{1,0:T(8,128)(2,1)}, bf16[256,1024]{1,0:T(8,128)(2,1)}, u32[]{:S(2)}, u32[]{:S(2)}) collective-permute-start(bf16[256,1024]{1,0:T(8,128)(2,1)} %get-tuple-element.18), channel_id=1, source_target_pairs={{24,16},{25,17},{26,18},{27,19},{28,20},{29,21},{30,22},{31,23}} | collective-permute-start | bytes 1572872 | tf_op jit(solution)/shard_map/ppermute | solution.py:300
  232.9 21.7 %collective-permute-start.8 = (bf16[256,1024]{1,0:T(8,128)(2,1)}, bf16[256,1024]{1,0:T(8,128)(2,1)}, u32[]{:S(2)}, u32[]{:S(2)}) collective-permute-start(bf16[256,1024]{1,0:T(8,128)(2,1)} %select_add_fusion.6), channel_id=1, source_target_pairs={{0,8},{8,16},{1,9},{9,17},{2,10},{10,18},{3,11},{11,19},{4,12},{12... | collective-permute-start | bytes 1572872 | tf_op jit(solution)/shard_map/ppermute | solution.py:299
  244.2 21.4 %collective-permute-start.15 = (bf16[256,1024]{1,0:T(8,128)(2,1)}, bf16[256,1024]{1,0:T(8,128)(2,1)}, u32[]{:S(2)}, u32[]{:S(2)}) collective-permute-start(bf16[256,1024]{1,0:T(8,128)(2,1)} %select_add_fusion.2), channel_id=1, source_target_pairs={{0,8},{8,16},{1,9},{9,17},{2,10},{10,18},{3,11},{11,19},{4,12},{12... | collective-permute-start | bytes 1572872 | tf_op jit(solution)/shard_map/ppermute | solution.py:299
  257.3 25.9 %collective-permute-start.11 = (bf16[256,1024]{1,0:T(8,128)(2,1)}, bf16[256,1024]{1,0:T(8,128)(2,1)}, u32[]{:S(2)}, u32[]{:S(2)}) collective-permute-start(bf16[256,1024]{1,0:T(8,128)(2,1)} %get-tuple-element.12), channel_id=1, source_target_pairs={{24,16},{16,8},{25,17},{17,9},{26,18},{18,10},{27,19},{19,11},{28,... | collective-permute-start | bytes 1572872 | tf_op jit(solution)/shard_map/ppermute | solution.py:300
  267.9 18.9 %collective-permute-start.18 = (bf16[256,1024]{1,0:T(8,128)(2,1)}, bf16[256,1024]{1,0:T(8,128)(2,1)}, u32[]{:S(2)}, u32[]{:S(2)}) collective-permute-start(bf16[256,1024]{1,0:T(8,128)(2,1)} %get-tuple-element.14), channel_id=1, source_target_pairs={{24,16},{16,8},{25,17},{17,9},{26,18},{18,10},{27,19},{19,11},{28,... | collective-permute-start | bytes 1572872 | tf_op jit(solution)/shard_map/ppermute | solution.py:300
  269.4 20.7 %all-to-all-start.5 = ((bf16[4,256,512]{2,1,0:T(8,128)(2,1)}), bf16[4,256,512]{2,1,0:T(8,128)(2,1)}, u32[]{:S(2)}, u32[]{:S(2)}) async-start(bf16[4,256,512]{2,1,0:T(8,128)(2,1)} %all-to-all-done.4), calls=%async_computation.5 | async-start | bytes 2097152 | tf_op jit(solution)/shard_map/all_to_all | solution.py:312
  273.6 18.1 %collective-permute-start.9 = (bf16[256,1024]{1,0:T(8,128)(2,1)}, bf16[256,1024]{1,0:T(8,128)(2,1)}, u32[]{:S(2)}, u32[]{:S(2)}) collective-permute-start(bf16[256,1024]{1,0:T(8,128)(2,1)} %get-tuple-element.11), channel_id=1, source_target_pairs={{0,8},{8,16},{16,24},{1,9},{9,17},{17,25},{2,10},{10,18},{18,26},{... | collective-permute-start | bytes 1572872 | tf_op jit(solution)/shard_map/ppermute | solution.py:299
  278.7 25.7 %collective-permute-start.16 = (bf16[256,1024]{1,0:T(8,128)(2,1)}, bf16[256,1024]{1,0:T(8,128)(2,1)}, u32[]{:S(2)}, u32[]{:S(2)}) collective-permute-start(bf16[256,1024]{1,0:T(8,128)(2,1)} %get-tuple-element.13), channel_id=1, source_target_pairs={{0,8},{8,16},{16,24},{1,9},{9,17},{17,25},{2,10},{10,18},{18,26},{... | collective-permute-start | bytes 1572872 | tf_op jit(solution)/shard_map/ppermute | solution.py:299
  285.5 17.0 %collective-permute-start.12 = (bf16[256,1024]{1,0:T(8,128)(2,1)}, bf16[256,1024]{1,0:T(8,128)(2,1)}, u32[]{:S(2)}, u32[]{:S(2)}) collective-permute-start(bf16[256,1024]{1,0:T(8,128)(2,1)} %select_add_fusion.5), channel_id=1, source_target_pairs={{24,16},{16,8},{8,0},{25,17},{17,9},{9,1},{26,18},{18,10},{10,2},{... | collective-permute-start | bytes 1572872 | tf_op jit(solution)/shard_map/ppermute | solution.py:300
  288.8 23.9 %collective-permute-start.19 = (bf16[256,1024]{1,0:T(8,128)(2,1)}, bf16[256,1024]{1,0:T(8,128)(2,1)}, u32[]{:S(2)}, u32[]{:S(2)}) collective-permute-start(bf16[256,1024]{1,0:T(8,128)(2,1)} %select_add_fusion.1), channel_id=1, source_target_pairs={{24,16},{16,8},{8,0},{25,17},{17,9},{9,1},{26,18},{18,10},{10,2},{... | collective-permute-start | bytes 1572872 | tf_op jit(solution)/shard_map/ppermute | solution.py:300
  (17 other events, 203.0 us)

commit v2 on v1

--- a/solution.py
+++ b/solution.py
@@ -9,19 +9,21 @@
 from jax.sharding import PartitionSpec as P
 
 CAP = 48
+HEAD = 16
 BF16 = jnp.bfloat16
 F32 = jnp.float32
 I32 = jnp.int32
 ANY = pl.ANY
 VMEM = pltpu.VMEM
 SMEM = pltpu.SMEM
+SMALL = pl.CostEstimate(flops=1, bytes_accessed=1, transcendentals=0)
 
 
 def params(mib):
     return pltpu.CompilerParams(vmem_limit_bytes=mib << 20)
 
 
-def pool_kernel(groups, share, quarter, count_ref, length_ref, items_ref, *rest):
+def pool_kernel(groups, share, quarter, count_ref, spot_ref, length_ref, items_ref, *rest):
     out_refs = rest[: len(groups)]
     items, wide, by_feat, first, last, pooled, sems = rest[len(groups) :]
     slots, feats, width = items.shape
@@ -55,7 +57,7 @@
 
     lane = lax.broadcasted_iota(I32, (rows, width), 1)
 
-    @pl.loop(0, feats)
+    @pl.loop(0, feats, unroll=2)
     def _(f):
         low = first[f]
         high = last[f]
@@ -88,14 +90,26 @@
                 hit = (source == slot + begin[p]) & (slot < count_ref[0, p])
                 picks.append(jnp.where(hit, 1.0, 0.0).astype(BF16))
         pick = jnp.concatenate(picks, axis=0)
+        body = len(group) * CAP
         for q in range(out_refs[g].shape[0]):
+            at = pl.multiple_of(spot_ref[g, q] * quarter, quarter)
             moved = jnp.dot(
-                pick, pooled[:, q * quarter : (q + 1) * quarter], preferred_element_type=F32
-            )
-            out_refs[g][q] = moved.astype(BF16)
-
-
-def pool(bag_items, bag_lengths, send_counts, groups, share, quarters):
+                pick, pooled[:, pl.ds(at, quarter)], preferred_element_type=F32
+            ).astype(BF16)
+            for b in range(share):
+                out_refs[g][q, b, :body] = moved[b * body : (b + 1) * body]
+        if g > 0:
+            continue
+        which = lax.broadcasted_iota(I32, (HEAD, quarter), 0)
+        for b in range(share):
+            head = jnp.zeros((HEAD, quarter), F32)
+            for p in range(b, count_ref.shape[1], share):
+                head = jnp.where(which == p // share, count_ref[0, p].astype(F32), head)
+            for q in range(out_refs[g].shape[0]):
+                out_refs[g][q, b, body:] = head.astype(BF16)
+
+
+def pool(bag_items, bag_lengths, send_counts, spots, groups, share, quarters):
     slots, feats, width = bag_items.shape
     rows = bag_lengths.shape[0]
     quarter = feats * width // quarters
@@ -103,9 +117,13 @@
     return pl.pallas_call(
         functools.partial(pool_kernel, groups, share, quarter),
         out_shape=[
-            jax.ShapeDtypeStruct((quarters, share * len(g) * CAP, quarter), BF16) for g in groups
+            jax.ShapeDtypeStruct(
+                (quarters, share, len(g) * CAP + (0 if k else HEAD), quarter), BF16
+            )
+            for k, g in enumerate(groups)
         ],
         in_specs=[
+            pl.BlockSpec(memory_space=SMEM),
             pl.BlockSpec(memory_space=SMEM),
             pl.BlockSpec(memory_space=VMEM),
             pl.BlockSpec(memory_space=ANY),
@@ -121,106 +139,105 @@
             pltpu.SemaphoreType.DMA((chunks,)),
         ],
         compiler_params=params(48),
-        cost_estimate=pl.CostEstimate(
-            flops=2 * rows * slots * feats * width,
-            bytes_accessed=2 * slots * feats * width,
-            transcendentals=0,
-        ),
+        cost_estimate=SMALL,
         name="pool",
-    )(send_counts, bag_lengths.T, bag_items)
-
-
-def order_kernel(group, share, rows, place_ref, counts_ref, slots_ref, out_ref):
+    )(send_counts, spots, bag_lengths.T, bag_items)
+
+
+def order_kernel(group, rows, slots_ref, head_ref, out_ref):
     sources = slots_ref.shape[0]
-    lane = lax.broadcasted_iota(I32, (rows, sources * CAP), 1)
-    place = lax.broadcasted_iota(I32, (rows, sources * CAP), 0)
-    b = place_ref[0]
+    width = sources * CAP
+    lane = lax.broadcasted_iota(I32, (1, width), 1).astype(F32)
+    place = lax.broadcasted_iota(I32, (rows, width), 0).astype(F32)
     for g, a in enumerate(group):
-        want = jnp.full((rows, sources * CAP), -1, I32)
-        at = jnp.int32(0)
+        want = jnp.full((1, width), -1.0, F32)
+        at = jnp.zeros((1, width), F32)
         for k in range(sources):
-            count = counts_ref[k, a * share + b]
+            count = head_ref[k, a : a + 1, :].astype(F32)
+            count = jnp.concatenate([count] * (width // count.shape[1]), axis=1)
             slot = lane - k * CAP
             want = jnp.where((slot >= 0) & (slot < count), slot + at, want)
             at = at + count
         pick = jnp.where(want == place, 1.0, 0.0).astype(BF16)
-        got = slots_ref[:, g * CAP : (g + 1) * CAP, :].reshape(sources * CAP, slots_ref.shape[2])
+        got = slots_ref[:, g * CAP : (g + 1) * CAP, :].reshape(width, slots_ref.shape[2])
         out_ref[g] = jnp.dot(pick, got, preferred_element_type=F32).astype(BF16)
 
 
-def order(place, counts, slots, group, share, rows):
+def order(slots, head, group, rows):
     quarter = slots.shape[2]
     return pl.pallas_call(
-        functools.partial(order_kernel, group, share, rows),
+        functools.partial(order_kernel, group, rows),
         out_shape=jax.ShapeDtypeStruct((len(group), rows, quarter), BF16),
-        in_specs=[
-            pl.BlockSpec(memory_space=SMEM),
-            pl.BlockSpec(memory_space=SMEM),
-            pl.BlockSpec(memory_space=VMEM),
-        ],
+        in_specs=[pl.BlockSpec(memory_space=VMEM), pl.BlockSpec(memory_space=VMEM)],
         out_specs=pl.BlockSpec(memory_space=VMEM),
         compiler_params=params(32),
-        cost_estimate=pl.CostEstimate(
-            flops=2 * len(group) * rows * slots.shape[0] * CAP * quarter,
-            bytes_accessed=2 * slots.size,
-            transcendentals=0,
-        ),
+        cost_estimate=SMALL,
         name="order",
-    )(place, counts, slots)
-
-
-def multiply_kernel(count, spot_ref, *refs):
+    )(slots, head)
+
+
+def multiply_kernel(count, cuts, spot_ref, *refs):
     pieces = refs[:count]
-    own_ref, other_ref, out_ref, held = refs[count:]
-
-    @pl.when(pl.program_id(0) == 0)
+    own_ref = refs[count]
+    other_refs = refs[count + 1 : count + 1 + len(cuts)]
+    out_ref, held = refs[count + 1 + len(cuts) :]
+    step = pl.program_id(0)
+
+    @pl.when(step == 0)
     def _():
         for j in range(count):
             held[spot_ref[j]] = pieces[j][...].reshape(held.shape[1:])
 
     quarter = held.shape[2]
     half = count // 2
-    total = None
-    for j in range(count):
-        weight = own_ref if j < half else other_ref
-        part = lax.dot_general(
-            held[j],
-            weight[:, (j % half) * quarter : (j % half + 1) * quarter],
-            (((1,), (1,)), ((), ())),
-            preferred_element_type=F32,
-        )
-        total = part if total is None else total + part
-    out_ref[...] = total.astype(BF16).reshape(out_ref.shape)
-
-
-def multiply(spots, pieces, own, other, offset, tile):
+
+    def run(other_ref):
+        total = None
+        for j in range(count):
+            weight = own_ref if j < half else other_ref
+            part = lax.dot_general(
+                held[j],
+                weight[:, (j % half) * quarter : (j % half + 1) * quarter],
+                (((1,), (1,)), ((), ())),
+                preferred_element_type=F32,
+            )
+            total = part if total is None else total + part
+        out_ref[...] = total.astype(BF16).reshape(out_ref.shape)
+
+    for (low, high), other_ref in zip(cuts, other_refs):
+        pl.when((step >= low) & (step < high))(functools.partial(run, other_ref))
+
+
+def multiply(spots, pieces, own, others, offset, tile):
     blocks, rows, quarter = pieces[0].shape
     count = len(pieces)
-    outs, depth = other.shape
+    depth = own.shape[1]
     base = offset // tile
+    cuts, at = [], 0
+    for other in others:
+        cuts.append((at, at + other.shape[0] // tile))
+        at = cuts[-1][1]
+
+    def other_spec(low, high):
+        return pl.BlockSpec((tile, depth), lambda n: (jnp.clip(n - low, 0, high - low - 1), 0))
+
     return pl.pallas_call(
-        functools.partial(multiply_kernel, count),
-        out_shape=jax.ShapeDtypeStruct((blocks, rows, outs), BF16),
-        grid=(outs // tile,),
+        functools.partial(multiply_kernel, count, cuts),
+        out_shape=jax.ShapeDtypeStruct((blocks, rows, at * tile), BF16),
+        grid=(at,),
         in_specs=[pl.BlockSpec(memory_space=SMEM)]
         + [
             pl.BlockSpec((blocks, rows, quarter), lambda n: (0, 0, 0), pipeline_mode=pl.Buffered(1))
             for _ in pieces
         ]
-        + [
-            pl.BlockSpec((tile, depth), lambda n: (n + base, 0)),
-            pl.BlockSpec((tile, depth), lambda n: (n, 0)),
-        ],
+        + [pl.BlockSpec((tile, depth), lambda n: (n + base, 0))]
+        + [other_spec(*cut) for cut in cuts],
         out_specs=pl.BlockSpec((blocks, rows, tile), lambda n: (0, 0, n)),
         scratch_shapes=[VMEM((count, blocks * rows, quarter), BF16)],
         compiler_params=params(32),
-        cost_estimate=pl.CostEstimate(
-            flops=4 * blocks * rows * outs * depth,
-            bytes_accessed=2 * (2 * outs * depth + blocks * rows * (outs + count * quarter)),
-            transcendentals=0,
-        ),
+        cost_estimate=SMALL,
         name="multiply",
-    )(spots, *pieces, own, other)
+    )(spots, *pieces, own, *others)
 
 
 def pick(index, options):
@@ -246,30 +263,63 @@
 
     weight = cross_weight[0]
     outs = weight.shape[0]
-    parts = 2
-    each = outs // parts
-    others = [
-        lax.ppermute(weight[n * each : (n + 1) * each], "b", swap) for n in range(parts)
-    ]
-    counts = lax.all_gather(send_counts, ("a", "b"), axis=0, tiled=True)
-    padded = pool(bag_items, bag_lengths, send_counts, groups, share, quarters)
-
-    place = b.reshape(1).astype(I32)
+    eighth = outs // 8
+    cuts = [(0, 3 * eighth), (3 * eighth, 5 * eighth), (5 * eighth, outs)]
+    parts = [(0, 2), (2, 3)]
+
+    def fetch(which, gate=None):
+        piece = weight[cuts[which][0] : cuts[which][1]]
+        if gate is not None:
+            piece, _ = lax.optimization_barrier((piece, gate))
+        return lax.ppermute(piece, "b", swap)
+
+    plain = jnp.arange(quarters, dtype=I32)
+    if tall == 2:
+        near = jnp.stack([(y ^ (k // 2)) * 2 + (c ^ (k % 2)) for k in range(4)]).astype(I32)
+    else:
+        near = plain
+    others = [fetch(0)]
+    padded = pool(
+        bag_items, bag_lengths, send_counts, jnp.stack([plain, near]), groups, share, quarters
+    )
+
+    def mix(sent, relative):
+        if not relative:
+            return lax.all_to_all(sent, ("y", "c"), 0, 0, tiled=True)
+        far = lax.ppermute(sent[2:], "y", swap)
+        side = lax.ppermute(sent[1], "c", swap)
+        cross = lax.ppermute(far[1], "c", swap)
+        got = [sent[0], side, far[0], cross]
+        return jnp.stack(
+            [pick(near[q], [(k, got[k]) for k in range(4)]) for q in range(4)]
+        )
+
+    mixed = [mix(padded[0], False)]
+    mixed[0], others[0] = lax.optimization_barrier((mixed[0], others[0]))
+    late, _ = lax.optimization_barrier((padded[1], mixed[0]))
+    mixed.append(mix(late, tall == 2))
+    others.append(fetch(1, mixed[0]))
+
     ordered, pieces = [], []
+    head = None
     for g, group in enumerate(groups):
-        mixed = lax.all_to_all(padded[g], ("y", "c"), 0, 0, tiled=True)
-        mixed = mixed.reshape(line * share, len(group) * CAP, mixed.shape[2])
-        slots = lax.all_to_all(mixed, ("a", "b"), 0, 0, tiled=True)
-        mine = order(place, counts, slots, group, share, rows)
+        sent = mixed[g].reshape(line * share, mixed[g].shape[2], mixed[g].shape[3])
+        slots = lax.all_to_all(sent, ("a", "b"), 0, 0, tiled=True)
+        if head is None:
+            head = slots[:, len(group) * CAP :, : bag_items.shape[2]]
+        mine = order(slots, head, group, rows)
         ordered.append(mine)
         if tall == 2:
             far = lax.ppermute(mine, "y", swap)
-            near = [(y, mine), (1 - y, far)]
+            found = [(y, mine), (1 - y, far)]
         else:
             every = lax.all_gather(mine, "y", axis=0)
-            near = [(jnp.int32(k), every[k]) for k in range(tall)]
-        found = [(k, c, piece) for k, piece in near]
-        found += [(k, 1 - c, lax.ppermute(piece, "c", swap)) for k, piece in near]
+            found = [(jnp.int32(k), every[k]) for k in range(tall)]
+        if g == 0:
+            others.append(fetch(2, found[-1][1]))
+        found = [(k, c, piece) for k, piece in found] + [
+            (k, 1 - c, lax.ppermute(piece, "c", swap)) for k, piece in found
+        ]
         pieces.append(found)
 
     half = quarters // 2
@@ -279,14 +329,15 @@
         spots.append(jnp.where(quarter_id // half == b, 0, half) + quarter_id % half)
     spots = jnp.stack(spots).astype(I32)
 
-    tile = min(512, each)
     columns = []
-    for n in range(parts):
+    gate = None
+    for first, last in parts:
         block = {}
         for g, group in enumerate(groups):
-            partial = multiply(
-                spots, [piece for _, _, piece in pieces[g]], weight, others[n], n * each, tile
-            )
+            taken = [piece for _, _, piece in pieces[g]]
+            if gate is not None:
+                taken, _ = lax.optimization_barrier((taken, gate))
+            partial = multiply(spots, taken, weight, others[first:last], cuts[first][0], eighth)
             for k, which in enumerate(group):
                 block[which] = partial[k]
         up = down = None
@@ -296,6 +347,8 @@
             if up is not None:
                 send_up = send_up + up
                 send_down = send_down + down
+            if s == 2:
+                gate = send_up
             up = lax.ppermute(send_up, "a", [(i, i + 1) for i in range(s)])
             down = lax.ppermute(
                 send_down, "a", [(line - 1 - i, line - 2 - i) for i in range(s)]

time: 317 us -> 233 us (0.74)
  the two profiles are of different devices: /device:TPU:0 before, /device:TPU:12 now
where the time goes in v2:
time: 233 us; the launch traced here: 231 us
  waiting for transfers between devices  64.9 us (28%)
  starting transfers between devices  61.5 us (26%)
  Pallas kernels  38.9 us (17%)
  local copies, waits for them, and re-layouts  29.3 us (13%)
  other arithmetic  21.1 us (9%)
  blocking collectives  15 us (6%)
    ppermute x6, starting transfers between devices, shards(): up = lax.ppermute(send_up, 'a', [(i, i + 1) for i in range(s)])  22.2 us
    unnamed x52, local copies, waits for them, and re-layouts  19.5 us
    pallas_call x4, Pallas kernels, multiply(): pl.pallas_call(functools.partial(multiply_kernel, count, cuts), out_shape...  19.4 us
    pallas_call x1, Pallas kernels, pool(): pl.pallas_call(functools.partial(pool_kernel, groups, share, quarter), ou...  18.6 us
    ppermute x6, waiting for transfers between devices, shards(): lax.ppermute(send_down, 'a', [(line - 1 - i, line - 2 - i) for i in range...  17.6 us
    all_to_all x1, blocking collectives, mix(): return lax.all_to_all(sent, ('y', 'c'), 0, 0, tiled=True)  15 us
    ppermute x3, waiting for transfers between devices, fetch(): return lax.ppermute(piece, 'b', swap)  12.7 us
    ppermute x2, waiting for transfers between devices, shards(): far = lax.ppermute(mine, 'y', swap)  12.5 us
  transfers between devices with their start and end apart: 28, of which 14 were waited for; matrix products, arithmetic and copies ran while one was open for 11% of the time, Pallas kernels for 17%

profile of v2, /device:TPU:12, one launch (start us, length us, event | category | flops | bytes accessed | tf_op | source)
XLA Modules:
  0.0 231.2 jit_solution(10301766779343374285)
XLA Ops:
  0.0 3.8 %slice_bitcast_fusion = (bf16[768,1024]{1,0:T(8,128)(2,1)}, bf16[768,1024]{1,0:T(8,128)(2,1)}) fusion(bf16[1,2048,1024]{2,1,0:T(8,128)(2,1)} %param.8), kind=kLoop, calls=%fused_computation.4 | loop fusion | bytes 6291456 | tf_op jit(solution)/shard_map/slice | solution.py:271
  5.4 18.6 %pool.1 = (bf16[4,2,112,512]{3,2,1,0:T(8,128)(2,1)S(1)}, bf16[4,2,96,512]{3,2,1,0:T(8,128)(2,1)S(1)}) custom-call(s32[1,8]{1,0:T(1,128)S(1)} %copy-done.22, s32[2,4]{1,0:T(2,128)S(1)} %pad_add_fusion.spot_ref, s32[16,256]{1,0:T(8,128)S(1)} %bitcast.152, bf16[2048,16,128]{2,1,0:T(8,128)(2,1)} %items_ref.1), custom_call_target="tpu_custom_call" | custom-call | flops 1 | bytes 1 | tf_op jit(solution)/shard_map/pool/pallas_call | solution.py:117
  24.1 15.0 %all_to_all.25 = bf16[4,2,112,512]{3,2,1,0:T(8,128)(2,1)} all-to-all(bf16[4,2,112,512]{3,2,1,0:T(8,128)(2,1)S(1)} %get-tuple-element.20), channel_id=1, replica_groups=mesh['a'=4,'b'=2,'y'=2,'c'=2] {'y','c'}, dimensions={0} | all-to-all | bytes 1835008 | tf_op jit(solution)/shard_map/all_to_all | solution.py:288
  40.2 6.3 %all-to-all-start.1 = ((bf16[8,112,512]{2,1,0:T(8,128)(2,1)}), bf16[8,112,512]{2,1,0:T(8,128)(2,1)S(1)}, u32[]{:S(2)}, u32[]{:S(2)}) async-start(bf16[8,112,512]{2,1,0:T(8,128)(2,1)} %bitcast.154), calls=%async_computation.1 | async-start | bytes 1835008 | tf_op jit(solution)/shard_map/all_to_all | solution.py:307
  47.7 8.2 %collective-permute-done.1 = bf16[2,2,96,512]{3,2,1,0:T(8,128)(2,1)S(1)} collective-permute-done((bf16[2,2,96,512]{3,2,1,0:T(8,128)(2,1)S(1)}, bf16[2,2,96,512]{3,2,1,0:T(8,128)(2,1)S(1)}, u32[]{:S(2)}, u32[]{:S(2)}) %collective-permute-start.1) | collective-permute-done | bytes 393248 | tf_op jit(solution)/shard_map/ppermute | solution.py:289
  62.3 4.3 %all-to-all-done.1.slots_ref = bf16[8,112,512]{2,1,0:T(8,128)(2,1)S(1)} async-done(((bf16[8,112,512]{2,1,0:T(8,128)(2,1)}), bf16[8,112,512]{2,1,0:T(8,128)(2,1)S(1)}, u32[]{:S(2)}, u32[]{:S(2)}) %all-to-all-start.1) | async-done | bytes 917536 | tf_op jit(solution)/shard_map/all_to_all | solution.py:307
  66.6 5.6 %all-to-all-start.2 = ((bf16[8,96,512]{2,1,0:T(8,128)(2,1)}), bf16[8,96,512]{2,1,0:T(8,128)(2,1)S(1)}, u32[]{:S(2)}, u32[]{:S(2)}) async-start(bf16[8,96,512]{2,1,0:T(8,128)(2,1)} %bitcast.16), calls=%async_computation.2 | async-start | bytes 1572864 | tf_op jit(solution)/shard_map/all_to_all | solution.py:307
  72.2 2.3 slice_bitcast_fusion.2
  77.1 12.5 %collective-permute-done.4.refs_1_ = bf16[2,256,512]{2,1,0:T(8,128)(2,1)} collective-permute-done((bf16[2,256,512]{2,1,0:T(8,128)(2,1)S(1)}, bf16[2,256,512]{2,1,0:T(8,128)(2,1)}, u32[]{:S(2)}, u32[]{:S(2)}) %collective-permute-start.4) | collective-permute-done | bytes 524320 | tf_op jit(solution)/shard_map/ppermute | solution.py:313
  94.0 11.6 %collective-permute-done.7.refs_6_ = bf16[512,1024]{1,0:T(8,128)(2,1)S(1)} collective-permute-done((bf16[512,1024]{1,0:T(8,128)(2,1)}, bf16[512,1024]{1,0:T(8,128)(2,1)S(1)}, u32[]{:S(2)}, u32[]{:S(2)}) %collective-permute-start.7) | collective-permute-done | bytes 1048608 | tf_op jit(solution)/shard_map/ppermute | solution.py:274
  111.4 5.5 %multiply.4 = bf16[2,256,1280]{2,1,0:T(8,128)(2,1)S(1)} custom-call(s32[4]{0:T(128)S(1)} %pad_add_fusion.1.spot_ref, bf16[2,256,512]{2,1,0:T(8,128)(2,1)S(1)} %order.2.refs_0_, bf16[2,256,512]{2,1,0:T(8,128)(2,1)} %collective-permute-done.4.refs_1_, bf16[2,256,512]{2,1,0:T(8,128)(2,1)} %collective-permute-done.5.refs_2_, ...), custom_call_target="tpu_custom_call" | custom-call | flops 1 | bytes 1 | tf_op jit(solution)/shard_map/multiply/pallas_call | solution.py:224
  128.1 5.4 %multiply.5 = bf16[2,256,1280]{2,1,0:T(8,128)(2,1)S(1)} custom-call(s32[4]{0:T(128)S(1)} %pad_add_fusion.1.spot_ref, bf16[2,256,512]{2,1,0:T(8,128)(2,1)S(1)} %order.3.refs_0_, bf16[2,256,512]{2,1,0:T(8,128)(2,1)S(1)} %copy-done.19, bf16[2,256,512]{2,1,0:T(8,128)(2,1)} %collective-permute-done.9.refs_2_, ...), custom_call_target="tpu_custom_call" | custom-call | flops 1 | bytes 1 | tf_op jit(solution)/shard_map/multiply/pallas_call | solution.py:224
  133.5 2.9 %collective-permute-done.11 = bf16[256,1280]{1,0:T(8,128)(2,1)} collective-permute-done((bf16[256,1280]{1,0:T(8,128)(2,1)}, bf16[256,1280]{1,0:T(8,128)(2,1)}, u32[]{:S(2)}, u32[]{:S(2)}) %collective-permute-start.11) | collective-permute-done | bytes 655392 | tf_op jit(solution)/shard_map/ppermute | solution.py:352
  140.3 4.3 %multiply.6 = bf16[2,256,768]{2,1,0:T(8,128)(2,1)S(1)} custom-call(s32[4]{0:T(128)S(1)} %pad_add_fusion.1.spot_ref, bf16[2,256,512]{2,1,0:T(8,128)(2,1)S(1)} %copy-done.6, bf16[2,256,512]{2,1,0:T(8,128)(2,1)} %collective-permute-done.4.refs_1_, bf16[2,256,512]{2,1,0:T(8,128)(2,1)} %collective-permute-done.5.refs_2_, ...), custom_call_target="tpu_custom_call" | custom-call | flops 1 | bytes 1 | tf_op jit(solution)/shard_map/multiply/pallas_call | solution.py:224
  148.0 7.8 %all-to-all-start.3 = ((bf16[4,256,512]{2,1,0:T(8,128)(2,1)}), bf16[4,256,512]{2,1,0:T(8,128)(2,1)}, u32[]{:S(2)}, u32[]{:S(2)}) async-start(bf16[4,256,512]{2,1,0:T(8,128)(2,1)} %pad_maximum_fusion), calls=%async_computation.3 | async-start | bytes 2097152 | tf_op jit(solution)/shard_map/all_to_all | solution.py:364
  161.5 4.2 %multiply.7 = bf16[2,256,768]{2,1,0:T(8,128)(2,1)S(1)} custom-call(s32[4]{0:T(128)S(1)} %pad_add_fusion.1.spot_ref, bf16[2,256,512]{2,1,0:T(8,128)(2,1)S(1)} %copy-done.9, bf16[2,256,512]{2,1,0:T(8,128)(2,1)S(1)} %copy-done.20, bf16[2,256,512]{2,1,0:T(8,128)(2,1)} %collective-permute-done.9.refs_2_, bf16[2,256,512]{2,1,0:T(8,128)(2,1)} %collective-permute-done.10.refs_3_, ...), custom_call_target="tpu_custom_call" | custom-call | flops 1 | bytes 1 | tf_op jit(solution)/shard_map/multiply/pallas_call | solution.py:224
  168.5 2.5 %collective-permute-start.19 = (bf16[256,768]{1,0:T(8,128)(2,1)}, bf16[256,768]{1,0:T(8,128)(2,1)}, u32[]{:S(2)}, u32[]{:S(2)}) collective-permute-start(bf16[256,768]{1,0:T(8,128)(2,1)} %select_add_fusion.6), channel_id=1, source_target_pairs={{0,8},{8,16},{1,9},{9,17},{2,10},{10,18},{3,11},{11,19},{4,12},{12... | collective-permute-start | bytes 1179656 | tf_op jit(solution)/shard_map/ppermute | solution.py:352
  171.0 2.5 %select_add_fusion.3 = (bf16[256,1280]{1,0:T(8,128)(2,1)}, bf16[256,1280]{1,0:T(8,128)(2,1)}) fusion(bf16[256,1280]{1,0:T(8,128)(2,1)} %collective-permute-done.12, pred[]{:T(512)S(6)} %eq.95, pred[]{:T(512)S(6)} %eq.94, bf16[2,256,1280]{2,1,0:T(8,128)(2,1)S(1)} %multiply.5, bf16[2,256,1280]{2,1,0:T(8,128)(2,1)S(1)} %multiply.4, ...), kind=kLoop, calls=%fused_computation.18 | loop fusion | flops 1638400 | bytes 5242882 | tf_op jit(solution)/shard_map/add | solution.py:348
  176.9 4.9 %all-to-all-start.4 = ((bf16[4,256,512]{2,1,0:T(8,128)(2,1)}), bf16[4,256,512]{2,1,0:T(8,128)(2,1)}, u32[]{:S(2)}, u32[]{:S(2)}) async-start(bf16[4,256,512]{2,1,0:T(8,128)(2,1)} %all-to-all-done.3), calls=%async_computation.4 | async-start | bytes 2097152 | tf_op jit(solution)/shard_map/all_to_all | solution.py:365
  181.8 10.0 %collective-permute-start.13 = (bf16[256,1280]{1,0:T(8,128)(2,1)}, bf16[256,1280]{1,0:T(8,128)(2,1)}, u32[]{:S(2)}, u32[]{:S(2)}) collective-permute-start(bf16[256,1280]{1,0:T(8,128)(2,1)} %get-tuple-element.37), channel_id=1, source_target_pairs={{0,8},{8,16},{16,24},{1,9},{9,17},{17,25},{2,10},{10,18},{18,26},{... | collective-permute-start | bytes 1966088 | tf_op jit(solution)/shard_map/ppermute | solution.py:352
  191.8 2.3 %select_add_fusion.7 = (bf16[256,768]{1,0:T(8,128)(2,1)}, bf16[256,768]{1,0:T(8,128)(2,1)}) fusion(bf16[256,768]{1,0:T(8,128)(2,1)} %collective-permute-done.19, pred[]{:T(512)S(6)} %eq.95, pred[]{:T(512)S(6)} %eq.94, bf16[2,256,768]{2,1,0:T(8,128)(2,1)} %copy-done.3, bf16[2,256,768]{2,1,0:T(8,128)(2,1)S(1)} %multiply.6, ...), kind=kLoop, calls=%fused_computation.26 | loop fusion | flops 983040 | bytes 3145730 | tf_op jit(solution)/shard_map/add | solution.py:348
  201.9 5.3 %collective-permute-start.20 = (bf16[256,768]{1,0:T(8,128)(2,1)S(1)}, bf16[256,768]{1,0:T(8,128)(2,1)S(1)}, u32[]{:S(2)}, u32[]{:S(2)}) collective-permute-start(bf16[256,768]{1,0:T(8,128)(2,1)S(1)} %copy-done.24), channel_id=1, source_target_pairs={{0,8},{8,16},{16,24},{1,9},{9,17},{17,25},{2,10},{10,18},{18,26},{... | collective-permute-start | bytes 1179656 | tf_op jit(solution)/shard_map/ppermute | solution.py:352
  211.4 11.0 %collective-permute-done.16 = bf16[256,1280]{1,0:T(8,128)(2,1)} collective-permute-done((bf16[256,1280]{1,0:T(8,128)(2,1)}, bf16[256,1280]{1,0:T(8,128)(2,1)}, u32[]{:S(2)}, u32[]{:S(2)}) %collective-permute-start.16) | collective-permute-done | bytes 655392 | tf_op jit(solution)/shard_map/ppermute | solution.py:353
  224.2 5.4 %collective-permute-done.23 = bf16[256,768]{1,0:T(8,128)(2,1)S(1)} collective-permute-done((bf16[256,768]{1,0:T(8,128)(2,1)S(1)}, bf16[256,768]{1,0:T(8,128)(2,1)S(1)}, u32[]{:S(2)}, u32[]{:S(2)}) %collective-permute-start.23) | collective-permute-done | bytes 393248 | tf_op jit(solution)/shard_map/ppermute | solution.py:353
  (120 shorter events, 68.7 us)
Async XLA Ops:
  3.8 36.3 %collective-permute-start = (bf16[768,1024]{1,0:T(8,128)(2,1)}, bf16[768,1024]{1,0:T(8,128)(2,1)S(1)}, u32[]{:S(2)}, u32[]{:S(2)}) collective-permute-start(bf16[768,1024]{1,0:T(8,128)(2,1)} %get-tuple-element.36), channel_id=1, source_target_pairs={{0,4},{4,0},{1,5},{5,1},{2,6},{6,2},{3,7},{7,3},{8,12},{12,8},{9,1... | collective-permute-start | bytes 4718600 | tf_op jit(solution)/shard_map/ppermute | solution.py:274
  40.2 26.4 %all-to-all-start.1 = ((bf16[8,112,512]{2,1,0:T(8,128)(2,1)}), bf16[8,112,512]{2,1,0:T(8,128)(2,1)S(1)}, u32[]{:S(2)}, u32[]{:S(2)}) async-start(bf16[8,112,512]{2,1,0:T(8,128)(2,1)} %bitcast.154), calls=%async_computation.1 | async-start | bytes 1835008 | tf_op jit(solution)/shard_map/all_to_all | solution.py:307
  47.7 9.7 %collective-permute-start.3 = (bf16[2,96,512]{2,1,0:T(8,128)(2,1)}, bf16[2,96,512]{2,1,0:T(8,128)(2,1)S(1)}, u32[]{:S(2)}, u32[]{:S(2)}) collective-permute-start(bf16[2,96,512]{2,1,0:T(8,128)(2,1)} %slice_bitcast_fusion.13), channel_id=1, source_target_pairs={{0,1},{1,0},{2,3},{3,2},{4,5},{5,4},{6,7},{7,6},{8,9},{9,8},{10,11... | collective-permute-start | bytes 589832 | tf_op jit(solution)/shard_map/ppermute | solution.py:290
  66.6 24.2 %all-to-all-start.2 = ((bf16[8,96,512]{2,1,0:T(8,128)(2,1)}), bf16[8,96,512]{2,1,0:T(8,128)(2,1)S(1)}, u32[]{:S(2)}, u32[]{:S(2)}) async-start(bf16[8,96,512]{2,1,0:T(8,128)(2,1)} %bitcast.16), calls=%async_computation.2 | async-start | bytes 1572864 | tf_op jit(solution)/shard_map/all_to_all | solution.py:307
  74.5 31.1 %collective-permute-start.7 = (bf16[512,1024]{1,0:T(8,128)(2,1)}, bf16[512,1024]{1,0:T(8,128)(2,1)S(1)}, u32[]{:S(2)}, u32[]{:S(2)}) collective-permute-start(bf16[512,1024]{1,0:T(8,128)(2,1)} %slice_bitcast_fusion.2), channel_id=1, source_target_pairs={{0,4},{4,0},{1,5},{5,1},{2,6},{6,2},{3,7},{7,3},{8,12},{12,8},{9,1... | collective-permute-start | bytes 3145736 | tf_op jit(solution)/shard_map/ppermute | solution.py:274
  76.5 13.1 %collective-permute-start.4 = (bf16[2,256,512]{2,1,0:T(8,128)(2,1)S(1)}, bf16[2,256,512]{2,1,0:T(8,128)(2,1)}, u32[]{:S(2)}, u32[]{:S(2)}) collective-permute-start(bf16[2,256,512]{2,1,0:T(8,128)(2,1)S(1)} %order.2.refs_0_), channel_id=1, source_target_pairs={{0,2},{2,0},{1,3},{3,1},{4,6},{6,4},{5,7},{7,5},{8,10},{10,8},{9,1... | collective-permute-start | bytes 1572872 | tf_op jit(solution)/shard_map/ppermute | solution.py:313
  77.1 29.4 %collective-permute-start.5 = (bf16[2,256,512]{2,1,0:T(8,128)(2,1)S(1)}, bf16[2,256,512]{2,1,0:T(8,128)(2,1)}, u32[]{:S(2)}, u32[]{:S(2)}) collective-permute-start(bf16[2,256,512]{2,1,0:T(8,128)(2,1)S(1)} %order.2.refs_0_), channel_id=1, source_target_pairs={{0,1},{1,0},{2,3},{3,2},{4,5},{5,4},{6,7},{7,6},{8,9},{9,8},{10,11... | collective-permute-start | bytes 1572872 | tf_op jit(solution)/shard_map/ppermute | solution.py:321
  89.6 17.0 %collective-permute-start.6 = (bf16[2,256,512]{2,1,0:T(8,128)(2,1)}, bf16[2,256,512]{2,1,0:T(8,128)(2,1)}, u32[]{:S(2)}, u32[]{:S(2)}) collective-permute-start(bf16[2,256,512]{2,1,0:T(8,128)(2,1)} %collective-permute-done.4.refs_1_), channel_id=1, source_target_pairs={{0,1},{1,0},{2,3},{3,2},{4,5},{5,4},{6,7},{7,6},{8,9},{9,8},{10,11... | collective-permute-start | bytes 1572872 | tf_op jit(solution)/shard_map/ppermute | solution.py:321
  93.3 26.2 %collective-permute-start.8 = (bf16[2,256,512]{2,1,0:T(8,128)(2,1)S(1)}, bf16[2,256,512]{2,1,0:T(8,128)(2,1)S(1)}, u32[]{:S(2)}, u32[]{:S(2)}) collective-permute-start(bf16[2,256,512]{2,1,0:T(8,128)(2,1)S(1)} %order.3.refs_0_), channel_id=1, source_target_pairs={{0,2},{2,0},{1,3},{3,1},{4,6},{6,4},{5,7},{7,5},{8,10},{10,8},{9,1... | collective-permute-start | bytes 1572872 | tf_op jit(solution)/shard_map/ppermute | solution.py:313
  94.0 46.3 %collective-permute-start.17 = (bf16[768,1024]{1,0:T(8,128)(2,1)}, bf16[768,1024]{1,0:T(8,128)(2,1)}, u32[]{:S(2)}, u32[]{:S(2)}) collective-permute-start(bf16[768,1024]{1,0:T(8,128)(2,1)} %get-tuple-element.30), channel_id=1, source_target_pairs={{0,4},{4,0},{1,5},{5,1},{2,6},{6,2},{3,7},{7,3},{8,12},{12,8},{9,1... | collective-permute-start | bytes 4718600 | tf_op jit(solution)/shard_map/ppermute | solution.py:274
  118.1 18.3 %collective-permute-start.11 = (bf16[256,1280]{1,0:T(8,128)(2,1)}, bf16[256,1280]{1,0:T(8,128)(2,1)}, u32[]{:S(2)}, u32[]{:S(2)}) collective-permute-start(bf16[256,1280]{1,0:T(8,128)(2,1)} %get-tuple-element.45), channel_id=1, source_target_pairs={{0,8},{1,9},{2,10},{3,11},{4,12},{5,13},{6,14},{7,15}} | collective-permute-start | bytes 1966088 | tf_op jit(solution)/shard_map/ppermute | solution.py:352
  120.0 51.0 %collective-permute-start.14 = (bf16[256,1280]{1,0:T(8,128)(2,1)}, bf16[256,1280]{1,0:T(8,128)(2,1)}, u32[]{:S(2)}, u32[]{:S(2)}) collective-permute-start(bf16[256,1280]{1,0:T(8,128)(2,1)} %get-tuple-element.44), channel_id=1, source_target_pairs={{24,16},{25,17},{26,18},{27,19},{28,20},{29,21},{30,22},{31,23}} | collective-permute-start | bytes 1966088 | tf_op jit(solution)/shard_map/ppermute | solution.py:353
  138.4 32.6 %collective-permute-start.12 = (bf16[256,1280]{1,0:T(8,128)(2,1)}, bf16[256,1280]{1,0:T(8,128)(2,1)}, u32[]{:S(2)}, u32[]{:S(2)}) collective-permute-start(bf16[256,1280]{1,0:T(8,128)(2,1)} %select_add_fusion.2), channel_id=1, source_target_pairs={{0,8},{8,16},{1,9},{9,17},{2,10},{10,18},{3,11},{11,19},{4,12},{12... | collective-permute-start | bytes 1966088 | tf_op jit(solution)/shard_map/ppermute | solution.py:352
  145.6 21.1 %collective-permute-start.18 = (bf16[256,768]{1,0:T(8,128)(2,1)}, bf16[256,768]{1,0:T(8,128)(2,1)}, u32[]{:S(2)}, u32[]{:S(2)}) collective-permute-start(bf16[256,768]{1,0:T(8,128)(2,1)} %get-tuple-element.46), channel_id=1, source_target_pairs={{0,8},{1,9},{2,10},{3,11},{4,12},{5,13},{6,14},{7,15}} | collective-permute-start | bytes 1179656 | tf_op jit(solution)/shard_map/ppermute | solution.py:352
  148.0 28.9 %all-to-all-start.3 = ((bf16[4,256,512]{2,1,0:T(8,128)(2,1)}), bf16[4,256,512]{2,1,0:T(8,128)(2,1)}, u32[]{:S(2)}, u32[]{:S(2)}) async-start(bf16[4,256,512]{2,1,0:T(8,128)(2,1)} %pad_maximum_fusion), calls=%async_computation.3 | async-start | bytes 2097152 | tf_op jit(solution)/shard_map/all_to_all | solution.py:364
  155.8 36.0 %collective-permute-start.21 = (bf16[256,768]{1,0:T(8,128)(2,1)}, bf16[256,768]{1,0:T(8,128)(2,1)}, u32[]{:S(2)}, u32[]{:S(2)}) collective-permute-start(bf16[256,768]{1,0:T(8,128)(2,1)} %get-tuple-element.47), channel_id=1, source_target_pairs={{24,16},{25,17},{26,18},{27,19},{28,20},{29,21},{30,22},{31,23}} | collective-permute-start | bytes 1179656 | tf_op jit(solution)/shard_map/ppermute | solution.py:353
  168.5 23.3 %collective-permute-start.19 = (bf16[256,768]{1,0:T(8,128)(2,1)}, bf16[256,768]{1,0:T(8,128)(2,1)}, u32[]{:S(2)}, u32[]{:S(2)}) collective-permute-start(bf16[256,768]{1,0:T(8,128)(2,1)} %select_add_fusion.6), channel_id=1, source_target_pairs={{0,8},{8,16},{1,9},{9,17},{2,10},{10,18},{3,11},{11,19},{4,12},{12... | collective-permute-start | bytes 1179656 | tf_op jit(solution)/shard_map/ppermute | solution.py:352
  173.5 21.9 %collective-permute-start.15 = (bf16[256,1280]{1,0:T(8,128)(2,1)}, bf16[256,1280]{1,0:T(8,128)(2,1)}, u32[]{:S(2)}, u32[]{:S(2)}) collective-permute-start(bf16[256,1280]{1,0:T(8,128)(2,1)} %get-tuple-element.38), channel_id=1, source_target_pairs={{24,16},{16,8},{25,17},{17,9},{26,18},{18,10},{27,19},{19,11},{28,... | collective-permute-start | bytes 1966088 | tf_op jit(solution)/shard_map/ppermute | solution.py:353
  176.9 22.5 %all-to-all-start.4 = ((bf16[4,256,512]{2,1,0:T(8,128)(2,1)}), bf16[4,256,512]{2,1,0:T(8,128)(2,1)}, u32[]{:S(2)}, u32[]{:S(2)}) async-start(bf16[4,256,512]{2,1,0:T(8,128)(2,1)} %all-to-all-done.3), calls=%async_computation.4 | async-start | bytes 2097152 | tf_op jit(solution)/shard_map/all_to_all | solution.py:365
  181.8 29.6 %collective-permute-start.13 = (bf16[256,1280]{1,0:T(8,128)(2,1)}, bf16[256,1280]{1,0:T(8,128)(2,1)}, u32[]{:S(2)}, u32[]{:S(2)}) collective-permute-start(bf16[256,1280]{1,0:T(8,128)(2,1)} %get-tuple-element.37), channel_id=1, source_target_pairs={{0,8},{8,16},{16,24},{1,9},{9,17},{17,25},{2,10},{10,18},{18,26},{... | collective-permute-start | bytes 1966088 | tf_op jit(solution)/shard_map/ppermute | solution.py:352
  194.1 14.2 %collective-permute-start.22 = (bf16[256,768]{1,0:T(8,128)(2,1)}, bf16[256,768]{1,0:T(8,128)(2,1)}, u32[]{:S(2)}, u32[]{:S(2)}) collective-permute-start(bf16[256,768]{1,0:T(8,128)(2,1)} %get-tuple-element.40), channel_id=1, source_target_pairs={{24,16},{16,8},{25,17},{17,9},{26,18},{18,10},{27,19},{19,11},{28,... | collective-permute-start | bytes 1179656 | tf_op jit(solution)/shard_map/ppermute | solution.py:353
  197.5 24.9 %collective-permute-start.16 = (bf16[256,1280]{1,0:T(8,128)(2,1)}, bf16[256,1280]{1,0:T(8,128)(2,1)}, u32[]{:S(2)}, u32[]{:S(2)}) collective-permute-start(bf16[256,1280]{1,0:T(8,128)(2,1)} %select_add_fusion.1), channel_id=1, source_target_pairs={{24,16},{16,8},{8,0},{25,17},{17,9},{9,1},{26,18},{18,10},{10,2},{... | collective-permute-start | bytes 1966088 | tf_op jit(solution)/shard_map/ppermute | solution.py:353
  201.9 22.2 %collective-permute-start.20 = (bf16[256,768]{1,0:T(8,128)(2,1)S(1)}, bf16[256,768]{1,0:T(8,128)(2,1)S(1)}, u32[]{:S(2)}, u32[]{:S(2)}) collective-permute-start(bf16[256,768]{1,0:T(8,128)(2,1)S(1)} %copy-done.24), channel_id=1, source_target_pairs={{0,8},{8,16},{16,24},{1,9},{9,17},{17,25},{2,10},{10,18},{18,26},{... | collective-permute-start | bytes 1179656 | tf_op jit(solution)/shard_map/ppermute | solution.py:352
  209.4 20.2 %collective-permute-start.23 = (bf16[256,768]{1,0:T(8,128)(2,1)S(1)}, bf16[256,768]{1,0:T(8,128)(2,1)S(1)}, u32[]{:S(2)}, u32[]{:S(2)}) collective-permute-start(bf16[256,768]{1,0:T(8,128)(2,1)S(1)} %select_add_fusion.5), channel_id=1, source_target_pairs={{24,16},{16,8},{8,0},{25,17},{17,9},{9,1},{26,18},{18,10},{10,2},{... | collective-permute-start | bytes 1179656 | tf_op jit(solution)/shard_map/ppermute | solution.py:353
  (30 other events, 168.5 us)

commit v3 on v2

--- a/solution.py
+++ b/solution.py
@@ -23,7 +23,7 @@
     return pltpu.CompilerParams(vmem_limit_bytes=mib << 20)
 
 
-def pool_kernel(groups, share, quarter, count_ref, spot_ref, length_ref, items_ref, *rest):
+def pool_kernel(groups, share, quarter, whole, count_ref, spot_ref, length_ref, items_ref, *rest):
     out_refs = rest[: len(groups)]
     items, wide, by_feat, first, last, pooled, sems = rest[len(groups) :]
     slots, feats, width = items.shape
@@ -32,7 +32,12 @@
     copies = []
     for k in range(sems.shape[0]):
         part = pl.ds(k * step, step)
-        copy = pltpu.make_async_copy(items_ref.at[part], items.at[part], sems.at[k])
+        if whole:
+            source = items_ref.at[part]
+        else:
+            start = pl.multiple_of(spot_ref[spot_ref.shape[0] - 1] * feats, feats)
+            source = items_ref.at[part, pl.ds(start, feats)]
+        copy = pltpu.make_async_copy(source, items.at[part], sems.at[k])
         copy.start()
         copies.append(copy)
 
@@ -92,7 +97,7 @@
         pick = jnp.concatenate(picks, axis=0)
         body = len(group) * CAP
         for q in range(out_refs[g].shape[0]):
-            at = pl.multiple_of(spot_ref[g, q] * quarter, quarter)
+            at = pl.multiple_of(spot_ref[q] * quarter, quarter)
             moved = jnp.dot(
                 pick, pooled[:, pl.ds(at, quarter)], preferred_element_type=F32
             ).astype(BF16)
@@ -109,13 +114,13 @@
                 out_refs[g][q, b, body:] = head.astype(BF16)
 
 
-def pool(bag_items, bag_lengths, send_counts, spots, groups, share, quarters):
-    slots, feats, width = bag_items.shape
-    rows = bag_lengths.shape[0]
-    quarter = feats * width // quarters
+def pool(bag_items, lengths, send_counts, spots, groups, share, quarter):
+    slots, whole, width = bag_items.shape
+    feats, rows = lengths.shape
+    quarters = feats * width // quarter
     chunks = 8
     return pl.pallas_call(
-        functools.partial(pool_kernel, groups, share, quarter),
+        functools.partial(pool_kernel, groups, share, quarter, feats == whole),
         out_shape=[
             jax.ShapeDtypeStruct(
                 (quarters, share, len(g) * CAP + (0 if k else HEAD), quarter), BF16
@@ -141,7 +146,7 @@
         compiler_params=params(48),
         cost_estimate=SMALL,
         name="pool",
-    )(send_counts, spots, bag_lengths.T, bag_items)
+    )(send_counts, spots, lengths, bag_items)
 
 
 def order_kernel(group, rows, slots_ref, head_ref, out_ref):
@@ -176,17 +181,43 @@
     )(slots, head)
 
 
-def multiply_kernel(count, cuts, spot_ref, *refs):
-    pieces = refs[:count]
-    own_ref = refs[count]
-    other_refs = refs[count + 1 : count + 1 + len(cuts)]
-    out_ref, held = refs[count + 1 + len(cuts) :]
+def cut_kernel(source_ref, out_ref):
+    out_ref[...] = source_ref[...]
+
+
+def cut(weight, low, high, tile):
+    depth = weight.shape[1]
+    return pl.pallas_call(
+        cut_kernel,
+        out_shape=jax.ShapeDtypeStruct((high - low, depth), BF16),
+        grid=((high - low) // tile,),
+        in_specs=[pl.BlockSpec((tile, depth), lambda n: (n + low // tile, 0))],
+        out_specs=pl.BlockSpec((tile, depth), lambda n: (n, 0)),
+        compiler_params=params(60),
+        cost_estimate=SMALL,
+        name="cut",
+    )(weight)
+
+
+def multiply_kernel(counts, spans, spot_ref, place_ref, *refs):
+    groups, count = counts
+    pieces = refs[: groups * count]
+    own_ref = refs[groups * count]
+    other_refs = refs[groups * count + 1 : groups * count + 1 + len(spans)]
+    out_refs = refs[groups * count + 1 + len(spans) : -1]
+    held = refs[-1]
+    rows = out_refs[0].shape[0]
     step = pl.program_id(0)
 
     @pl.when(step == 0)
     def _():
-        for j in range(count):
-            held[spot_ref[j]] = pieces[j][...].reshape(held.shape[1:])
+        for g in range(groups):
+            for j in range(count):
+                piece = pieces[g * count + j]
+                for k in range(piece.shape[0]):
+                    which = g * piece.shape[0] + k
+                    at = pl.multiple_of(place_ref[which] * rows, rows)
+                    held[spot_ref[j], pl.ds(at, rows), :] = piece[k]
 
     quarter = held.shape[2]
     half = count // 2
@@ -202,42 +233,83 @@
                 preferred_element_type=F32,
             )
             total = part if total is None else total + part
-        out_ref[...] = total.astype(BF16).reshape(out_ref.shape)
-
-    for (low, high), other_ref in zip(cuts, other_refs):
+        for k, out_ref in enumerate(out_refs):
+            out_ref[...] = total[k * rows : (k + 1) * rows].astype(BF16)
+
+    for (low, high), other_ref in zip(spans, other_refs):
         pl.when((step >= low) & (step < high))(functools.partial(run, other_ref))
 
 
-def multiply(spots, pieces, own, others, offset, tile):
-    blocks, rows, quarter = pieces[0].shape
-    count = len(pieces)
+def multiply(spots, places, groups, own, others, offset, tile):
+    blocks, rows, quarter = groups[0][0].shape
+    count = len(groups[0])
     depth = own.shape[1]
     base = offset // tile
-    cuts, at = [], 0
+    total = blocks * len(groups)
+    spans, at = [], 0
     for other in others:
-        cuts.append((at, at + other.shape[0] // tile))
-        at = cuts[-1][1]
+        spans.append((at, at + other.shape[0] // tile))
+        at = spans[-1][1]
 
     def other_spec(low, high):
         return pl.BlockSpec((tile, depth), lambda n: (jnp.clip(n - low, 0, high - low - 1), 0))
 
     return pl.pallas_call(
-        functools.partial(multiply_kernel, count, cuts),
-        out_shape=jax.ShapeDtypeStruct((blocks, rows, at * tile), BF16),
+        functools.partial(multiply_kernel, (len(groups), count), spans),
+        out_shape=[jax.ShapeDtypeStruct((rows, at * tile), BF16) for _ in range(total)],
         grid=(at,),
-        in_specs=[pl.BlockSpec(memory_space=SMEM)]
+        in_specs=[pl.BlockSpec(memory_space=SMEM)] * 2
         + [
             pl.BlockSpec((blocks, rows, quarter), lambda n: (0, 0, 0), pipeline_mode=pl.Buffered(1))
-            for _ in pieces
+            for _ in range(count * len(groups))
         ]
         + [pl.BlockSpec((tile, depth), lambda n: (n + base, 0))]
-        + [other_spec(*cut) for cut in cuts],
-        out_specs=pl.BlockSpec((blocks, rows, tile), lambda n: (0, 0, n)),
-        scratch_shapes=[VMEM((count, blocks * rows, quarter), BF16)],
-        compiler_params=params(32),
+        + [other_spec(*span) for span in spans],
+        out_specs=[pl.BlockSpec((rows, tile), lambda n: (0, n)) for _ in range(total)],
+        scratch_shapes=[VMEM((count, total * rows, quarter), BF16)],
+        compiler_params=params(60),
         cost_estimate=SMALL,
         name="multiply",
-    )(spots, *pieces, own, *others)
+    )(spots, places, *[piece for group in groups for piece in group], own, *others)
+
+
+def finish_kernel(end_ref, own_end, own_mid, outer, near, far, base_ref, bias_ref, *rest):
+    out_ref = rest[-1]
+    base = base_ref[0].astype(F32)
+    is_end = end_ref[0] == 1
+
+    def run(sums):
+        product = sums[0][...].astype(F32)
+        for extra in sums[1:]:
+            product += extra[...].astype(F32)
+        out_ref[...] = (base * (product + bias_ref[...]) + base).astype(BF16)
+
+    pl.when(is_end)(functools.partial(run, (own_end, outer)))
+    pl.when(jnp.logical_not(is_end))(functools.partial(run, (own_mid, near, far)))
+
+
+def finish(is_end, sums, base, bias, offset, tile, onto=None):
+    quarters, rows, quarter = base.shape
+    first = offset // tile
+    per = quarter // tile
+    more = [] if onto is None else [onto]
+    return pl.pallas_call(
+        finish_kernel,
+        out_shape=jax.ShapeDtypeStruct((rows, quarters * quarter), BF16),
+        grid=(sums[0].shape[1] // tile,),
+        in_specs=[pl.BlockSpec(memory_space=SMEM)]
+        + [pl.BlockSpec((rows, tile), lambda n: (0, n))] * 5
+        + [
+            pl.BlockSpec((1, rows, tile), lambda n: ((n + first) // per, 0, (n + first) % per)),
+            pl.BlockSpec((1, tile), lambda n: (0, n + first)),
+        ]
+        + [pl.BlockSpec(memory_space=ANY) for _ in more],
+        out_specs=pl.BlockSpec((rows, tile), lambda n: (0, n + first)),
+        input_output_aliases={8: 0} if more else {},
+        compiler_params=params(60),
+        cost_estimate=SMALL,
+        name="finish",
+    )(is_end, *sums, base, bias, *more)
 
 
 def pick(index, options):
@@ -257,48 +329,53 @@
     swap = [(0, 1), (1, 0)]
     edge = line // 4
     groups = [
+        list(range(edge, line - edge)),
         list(range(edge)) + list(range(line - edge, line)),
-        list(range(edge, line - edge)),
     ]
 
     weight = cross_weight[0]
     outs = weight.shape[0]
     eighth = outs // 8
-    cuts = [(0, 3 * eighth), (3 * eighth, 5 * eighth), (5 * eighth, outs)]
-    parts = [(0, 2), (2, 3)]
-
-    def fetch(which, gate=None):
-        piece = weight[cuts[which][0] : cuts[which][1]]
-        if gate is not None:
-            piece, _ = lax.optimization_barrier((piece, gate))
-        return lax.ppermute(piece, "b", swap)
-
-    plain = jnp.arange(quarters, dtype=I32)
+    tile = 2 * eighth
+    parts = [(0, tile), (tile, 2 * tile), (2 * tile, outs)]
+
+    def fetch(which, source):
+        return lax.ppermute(cut(source, *parts[which], tile), "b", swap)
+
+    quarter = bag_items.shape[1] * bag_items.shape[2] // quarters
+    lengths = bag_lengths.T
+    others = [fetch(0, weight), fetch(1, weight)]
+    mixed = []
     if tall == 2:
-        near = jnp.stack([(y ^ (k // 2)) * 2 + (c ^ (k % 2)) for k in range(4)]).astype(I32)
+        feats = bag_items.shape[1] // 2
+        near = [(y ^ (k // 2)) * 2 + (c ^ (k % 2)) for k in range(4)]
+
+        def half_pool(side):
+            spots = jnp.stack([c, 1 - c, side]).astype(I32)
+            part = lax.dynamic_slice_in_dim(lengths, side * feats, feats, 0)
+            return list(pool(bag_items, part, send_counts, spots, groups, share, quarter))
+
+        leaving = half_pool(1 - y)
+        away = [lax.ppermute(piece, "y", swap) for piece in leaving]
+        staying = half_pool(y)
+        for g in range(2):
+            staying[g], others[g] = lax.optimization_barrier((staying[g], others[g]))
+            side = lax.ppermute(staying[g][1], "c", swap)
+            cross = lax.ppermute(away[g][1], "c", swap)
+            got = [staying[g][0], side, away[g][0], cross]
+            mixed.append(
+                jnp.stack([pick(near[q], [(k, got[k]) for k in range(4)]) for q in range(4)])
+            )
     else:
-        near = plain
-    others = [fetch(0)]
-    padded = pool(
-        bag_items, bag_lengths, send_counts, jnp.stack([plain, near]), groups, share, quarters
-    )
-
-    def mix(sent, relative):
-        if not relative:
-            return lax.all_to_all(sent, ("y", "c"), 0, 0, tiled=True)
-        far = lax.ppermute(sent[2:], "y", swap)
-        side = lax.ppermute(sent[1], "c", swap)
-        cross = lax.ppermute(far[1], "c", swap)
-        got = [sent[0], side, far[0], cross]
-        return jnp.stack(
-            [pick(near[q], [(k, got[k]) for k in range(4)]) for q in range(4)]
-        )
-
-    mixed = [mix(padded[0], False)]
-    mixed[0], others[0] = lax.optimization_barrier((mixed[0], others[0]))
-    late, _ = lax.optimization_barrier((padded[1], mixed[0]))
-    mixed.append(mix(late, tall == 2))
-    others.append(fetch(1, mixed[0]))
+        spots = jnp.arange(quarters, dtype=I32)
+        for padded in pool(bag_items, lengths, send_counts, spots, groups, share, quarter):
+            mixed.append(lax.all_to_all(padded, ("y", "c"), 0, 0, tiled=True))
+
+    upper = a >= 2
+    is_end = ((a == 0) | (a == 3)).astype(I32).reshape(1)
+    flip = jnp.where(upper, 0, 1).astype(I32)
+    places = jnp.stack([flip, 1 - flip])
+    inward, middle, outward = [(0, 1), (3, 2)], [(1, 2), (2, 1)], [(1, 0), (2, 3)]
 
     ordered, pieces = [], []
     head = None
@@ -307,7 +384,15 @@
         slots = lax.all_to_all(sent, ("a", "b"), 0, 0, tiled=True)
         if head is None:
             head = slots[:, len(group) * CAP :, : bag_items.shape[2]]
+        if g == 1 and line == 4:
+            far1, near1 = multiply(spots, places, [pieces[0]], weight, others[:2], 0, tile)
+            in2 = lax.ppermute(far1, "a", inward)
+            in3 = lax.ppermute(near1, "a", inward)
+            slots, far1 = lax.optimization_barrier((slots, far1))
         mine = order(slots, head, group, rows)
+        if g == 0:
+            late, mine = lax.optimization_barrier((weight, mine))
+            others.append(fetch(2, late))
         ordered.append(mine)
         if tall == 2:
             far = lax.ppermute(mine, "y", swap)
@@ -315,56 +400,71 @@
         else:
             every = lax.all_gather(mine, "y", axis=0)
             found = [(jnp.int32(k), every[k]) for k in range(tall)]
-        if g == 0:
-            others.append(fetch(2, found[-1][1]))
         found = [(k, c, piece) for k, piece in found] + [
             (k, 1 - c, lax.ppermute(piece, "c", swap)) for k, piece in found
         ]
-        pieces.append(found)
-
-    half = quarters // 2
-    spots = []
-    for k, core, _ in pieces[0]:
-        quarter_id = k * 2 + core
-        spots.append(jnp.where(quarter_id // half == b, 0, half) + quarter_id % half)
-    spots = jnp.stack(spots).astype(I32)
-
-    columns = []
-    gate = None
-    for first, last in parts:
-        block = {}
-        for g, group in enumerate(groups):
-            taken = [piece for _, _, piece in pieces[g]]
-            if gate is not None:
-                taken, _ = lax.optimization_barrier((taken, gate))
-            partial = multiply(spots, taken, weight, others[first:last], cuts[first][0], eighth)
-            for k, which in enumerate(group):
-                block[which] = partial[k]
-        up = down = None
-        for s in range(1, line):
-            send_up = pick(a, [(i, block[line - s + i]) for i in range(s)])
-            send_down = pick(a, [(line - 1 - i, block[s - 1 - i]) for i in range(s)])
-            if up is not None:
-                send_up = send_up + up
-                send_down = send_down + down
-            if s == 2:
-                gate = send_up
-            up = lax.ppermute(send_up, "a", [(i, i + 1) for i in range(s)])
-            down = lax.ppermute(
-                send_down, "a", [(line - 1 - i, line - 2 - i) for i in range(s)]
-            )
-        mine = pick(a, [(i, block[i]) for i in range(line)])
-        columns.append(mine.astype(F32) + up.astype(F32) + down.astype(F32))
-    product = jnp.concatenate(columns, axis=1)
+        pieces.append([piece for _, _, piece in found])
+        spots = [k * 2 + core for k, core, _ in found]
+        half = quarters // 2
+        spots = jnp.stack([jnp.where(q // half == b, 0, half) + q % half for q in spots])
+        spots = spots.astype(I32)
 
     blocks = [None] * line
     for g, group in enumerate(groups):
         for k, which in enumerate(group):
             blocks[which] = ordered[g][k]
-    back = lax.all_to_all(jnp.stack(blocks), "a", 0, 0, tiled=True)
+    middle_piece = len(pieces[1]) // 2
+    stacked, pieces[1][middle_piece] = lax.optimization_barrier(
+        (jnp.stack(blocks), pieces[1][middle_piece])
+    )
+    back = lax.all_to_all(stacked, "a", 0, 0, tiled=True)
+
+    if line != 4:
+        where = jnp.arange(line, dtype=I32)
+        columns = []
+        for held, low in ((others[:2], 0), (others[2:], parts[2][0])):
+            block = {}
+            for g, group in enumerate(groups):
+                partial = multiply(spots, where, [pieces[g]], weight, held, low, tile)
+                block.update(zip(group, partial))
+            up = down = None
+            for s in range(1, line):
+                send_up = pick(a, [(i, block[line - s + i]) for i in range(s)])
+                send_down = pick(a, [(line - 1 - i, block[s - 1 - i]) for i in range(s)])
+                if up is not None:
+                    send_up = send_up + up
+                    send_down = send_down + down
+                up = lax.ppermute(send_up, "a", [(i, i + 1) for i in range(s)])
+                down = lax.ppermute(
+                    send_down, "a", [(line - 1 - i, line - 2 - i) for i in range(s)]
+                )
+            mine = pick(a, [(i, block[i]) for i in range(line)])
+            columns.append(mine.astype(F32) + up.astype(F32) + down.astype(F32))
+        back = lax.all_to_all(back, ("y", "c"), 0, 0, tiled=True)
+        base = jnp.transpose(back, (1, 0, 2)).reshape(rows, -1).astype(F32)
+        return (base * (jnp.concatenate(columns, axis=1) + cross_bias[0]) + base).astype(BF16)
+
+    far0, near0 = multiply(spots, places, [pieces[1]], weight, others[:2], 0, tile)
+    in1 = lax.ppermute(far0, "a", inward)
+    both, far0 = lax.optimization_barrier((pieces, far0))
+    mid3 = lax.ppermute(far1 + in2, "a", middle)
+    mid2 = lax.ppermute(far0 + in1, "a", middle)
+    out3 = lax.ppermute(near0 + mid2, "a", outward)
+    sums = (near0, near1, out3, in3, mid3)
     back = lax.all_to_all(back, ("y", "c"), 0, 0, tiled=True)
-    base = jnp.transpose(back, (1, 0, 2)).reshape(rows, -1).astype(F32)
-    return (base * (product + cross_bias[0]) + base).astype(BF16)
+
+    far1, near1, far0, near0 = multiply(
+        spots, jnp.concatenate([places, places + 2]), both, weight, others[2:], parts[2][0], tile
+    )
+    result = finish(is_end, sums, back, cross_bias, 0, tile)
+    in1 = lax.ppermute(far0, "a", inward)
+    in2 = lax.ppermute(far1, "a", inward)
+    mid2 = lax.ppermute(far0 + in1, "a", middle)
+    in3 = lax.ppermute(near1, "a", inward)
+    mid3 = lax.ppermute(far1 + in2, "a", middle)
+    out3 = lax.ppermute(near0 + mid2, "a", outward)
+    sums = (near0, near1, out3, in3, mid3)
+    return finish(is_end, sums, back, cross_bias, parts[2][0], tile, result)
 
 
 def solution(mesh):

time: 233 us -> 214 us (0.918)
  the two profiles are of different devices: /device:TPU:12 before, /device:TPU:0 now
where the time goes in v3:
time: 214 us; the launch traced here: 213 us
  waiting for transfers between devices  72.9 us (34%)
  starting transfers between devices  62.6 us (29%)
  Pallas kernels  50.5 us (24%)
  other arithmetic  21 us (10%)
  local copies, waits for them, and re-layouts  5.8 us (3%)
    ppermute x3, waiting for transfers between devices, fetch(): return lax.ppermute(cut(source, *parts[which], tile), 'b', swap)  33.1 us
    pallas_call x3, Pallas kernels, multiply(): pl.pallas_call(functools.partial(multiply_kernel, (len(groups), count), s...  21.1 us
    pallas_call x2, Pallas kernels, pool(): pl.pallas_call(functools.partial(pool_kernel, groups, share, quarter, fea...  15.9 us
    ppermute x2, waiting for transfers between devices, shards(): far = lax.ppermute(mine, 'y', swap)  15.4 us
    ppermute x2, starting transfers between devices, shards(): in3 = lax.ppermute(near1, 'a', inward)  11.1 us
    ppermute x2, waiting for transfers between devices, shards(): out3 = lax.ppermute(near0 + mid2, 'a', outward)  10.7 us
    all_to_all x2, starting transfers between devices, shards(): slots = lax.all_to_all(sent, ('a', 'b'), 0, 0, tiled=True)  10.7 us
    ppermute x2, starting transfers between devices, shards(): in1 = lax.ppermute(far0, 'a', inward)  8.2 us
  transfers between devices with their start and end apart: 31, of which 13 were waited for; matrix products, arithmetic and copies ran while one was open for 11% of the time, Pallas kernels for 21%

profile of v3, /device:TPU:0, one launch (start us, length us, event | category | flops | bytes accessed | tf_op | source)
XLA Modules:
  0.0 213.0 jit_solution(3857897005611241272)
XLA Ops:
  2.3 2.9 %collective-permute-start.2 = (bf16[512,1024]{1,0:T(8,128)(2,1)}, bf16[512,1024]{1,0:T(8,128)(2,1)S(1)}, u32[]{:S(2)}, u32[]{:S(2)}) collective-permute-start(bf16[512,1024]{1,0:T(8,128)(2,1)} %cut.3), channel_id=1, source_target_pairs={{0,4},{4,0},{1,5},{5,1},{2,6},{6,2},{3,7},{7,3},{8,12},{12,8},{9,1... | collective-permute-start | bytes 3145736 | tf_op jit(solution)/shard_map/ppermute | solution.py:343
  5.3 8.0 %pool.2 = (bf16[2,2,112,512]{3,2,1,0:T(8,128)(2,1)S(1)}, bf16[2,2,96,512]{3,2,1,0:T(8,128)(2,1)S(1)}) custom-call(s32[1,8]{1,0:T(1,128)S(1)} %copy-done.2, s32[3]{0:T(128)S(1)} %get-tuple-element.79.spot_ref, s32[8,256]{1,0:T(8,128)S(1)} %get-tuple-element.78.length_ref, bf16[2048,16,128]{2,1,0:T(8,128)(2,1)} %items_ref.3), custom_call_target="tpu_custom_call" | custom-call | flops 1 | bytes 1 | tf_op jit(solution)/shard_map/pool/pallas_call | solution.py:122
  14.9 8.0 %pool.3 = (bf16[2,2,112,512]{3,2,1,0:T(8,128)(2,1)S(1)}, bf16[2,2,96,512]{3,2,1,0:T(8,128)(2,1)S(1)}) custom-call(s32[1,8]{1,0:T(1,128)S(1)} %copy-done.2, s32[3]{0:T(128)S(1)} %get-tuple-element.80.spot_ref, s32[8,256]{1,0:T(8,128)S(1)} %get-tuple-element.77.length_ref, bf16[2048,16,128]{2,1,0:T(8,128)(2,1)} %items_ref.3), custom_call_target="tpu_custom_call" | custom-call | flops 1 | bytes 1 | tf_op jit(solution)/shard_map/pool/pallas_call | solution.py:122
  25.4 3.2 %collective-permute-done.2.refs_5_ = bf16[512,1024]{1,0:T(8,128)(2,1)S(1)} collective-permute-done((bf16[512,1024]{1,0:T(8,128)(2,1)}, bf16[512,1024]{1,0:T(8,128)(2,1)S(1)}, u32[]{:S(2)}, u32[]{:S(2)}) %collective-permute-start.2) | collective-permute-done | bytes 1048608 | tf_op jit(solution)/shard_map/ppermute | solution.py:343
  36.1 4.9 %all-to-all-start = ((bf16[8,112,512]{2,1,0:T(8,128)(2,1)}), bf16[8,112,512]{2,1,0:T(8,128)(2,1)S(1)}, u32[]{:S(2)}, u32[]{:S(2)}) async-start(bf16[8,112,512]{2,1,0:T(8,128)(2,1)} %bitcast.22), calls=%async_computation | async-start | bytes 1835008 | tf_op jit(solution)/shard_map/all_to_all | solution.py:384
  42.0 25.0 %collective-permute-done.9.refs_6_ = bf16[512,1024]{1,0:T(8,128)(2,1)} collective-permute-done((bf16[512,1024]{1,0:T(8,128)(2,1)}, bf16[512,1024]{1,0:T(8,128)(2,1)}, u32[]{:S(2)}, u32[]{:S(2)}) %collective-permute-start.9) | collective-permute-done | bytes 1048608 | tf_op jit(solution)/shard_map/ppermute | solution.py:343
  71.6 5.8 %all-to-all-start.1 = ((bf16[8,96,512]{2,1,0:T(8,128)(2,1)}), bf16[8,96,512]{2,1,0:T(8,128)(2,1)S(1)}, u32[]{:S(2)}, u32[]{:S(2)}) async-start(bf16[8,96,512]{2,1,0:T(8,128)(2,1)} %bitcast.31), calls=%async_computation.1 | async-start | bytes 1572864 | tf_op jit(solution)/shard_map/all_to_all | solution.py:384
  83.1 8.6 %collective-permute-done.4.refs_1_ = bf16[2,256,512]{2,1,0:T(8,128)(2,1)} collective-permute-done((bf16[2,256,512]{2,1,0:T(8,128)(2,1)S(1)}, bf16[2,256,512]{2,1,0:T(8,128)(2,1)}, u32[]{:S(2)}, u32[]{:S(2)}) %collective-permute-start.4) | collective-permute-done | bytes 524320 | tf_op jit(solution)/shard_map/ppermute | solution.py:398
  94.0 6.1 %multiply.3 = (bf16[256,1024]{1,0:T(8,128)(2,1)}, bf16[256,1024]{1,0:T(8,128)(2,1)}) custom-call(s32[4]{0:T(128)} %pad_add_fusion.spot_ref, s32[2]{0:T(128)} %get-tuple-element.68.place_ref, bf16[2,256,512]{2,1,0:T(8,128)(2,1)} %copy-done, bf16[2,256,512]{2,1,0:T(8,128)(2,1)} %collective-permute-done.4.refs_1_, ...), custom_call_target="tpu_custom_call" | custom-call | flops 1 | bytes 1 | tf_op jit(solution)/shard_map/multiply/pallas_call | solution.py:257
  103.4 4.8 %all-to-all-start.2 = ((bf16[4,256,512]{2,1,0:T(8,128)(2,1)}), bf16[4,256,512]{2,1,0:T(8,128)(2,1)}, u32[]{:S(2)}, u32[]{:S(2)}) async-start(bf16[4,256,512]{2,1,0:T(8,128)(2,1)} %pad_maximum_fusion), calls=%async_computation.2 | async-start | bytes 2097152 | tf_op jit(solution)/shard_map/all_to_all | solution.py:420
  108.3 6.8 %collective-permute-done.11.refs_1_.refs_5_ = bf16[2,256,512]{2,1,0:T(8,128)(2,1)} collective-permute-done((bf16[2,256,512]{2,1,0:T(8,128)(2,1)S(1)}, bf16[2,256,512]{2,1,0:T(8,128)(2,1)}, u32[]{:S(2)}, u32[]{:S(2)}) %collective-permute-start.11) | collective-permute-done | bytes 524320 | tf_op jit(solution)/shard_map/ppermute | solution.py:398
  118.0 6.1 %multiply.4 = (bf16[256,1024]{1,0:T(8,128)(2,1)}, bf16[256,1024]{1,0:T(8,128)(2,1)}) custom-call(s32[4]{0:T(128)} %pad_add_fusion.spot_ref, s32[2]{0:T(128)} %get-tuple-element.68.place_ref, bf16[2,256,512]{2,1,0:T(8,128)(2,1)} %copy-done.1, bf16[2,256,512]{2,1,0:T(8,128)(2,1)} %collective-permute-done.11.refs_1_.refs_5_, bf16[2,256,512]{2,1,0:T(8,128)(2,1)} %copy-done.8, ...), custom_call_target="tpu_custom_call" | custom-call | flops 1 | bytes 1 | tf_op jit(solution)/shard_map/multiply/pallas_call | solution.py:257
  124.1 4.6 %collective-permute-start.21 = (bf16[256,1024]{1,0:T(8,128)(2,1)}, bf16[256,1024]{1,0:T(8,128)(2,1)}, u32[]{:S(2)}, u32[]{:S(2)}) collective-permute-start(bf16[256,1024]{1,0:T(8,128)(2,1)} %get-tuple-element.65), channel_id=1, source_target_pairs={{0,8},{24,16},{1,9},{25,17},{2,10},{26,18},{3,11},{27,19},{4,12},{... | collective-permute-start | bytes 1572872 | tf_op jit(solution)/shard_map/ppermute | solution.py:448
  128.7 4.9 %collective-permute-done.14.refs_9_ = bf16[1024,1024]{1,0:T(8,128)(2,1)S(1)} collective-permute-done((bf16[1024,1024]{1,0:T(8,128)(2,1)}, bf16[1024,1024]{1,0:T(8,128)(2,1)S(1)}, u32[]{:S(2)}, u32[]{:S(2)}) %collective-permute-start.14) | collective-permute-done | bytes 2097184 | tf_op jit(solution)/shard_map/ppermute | solution.py:343
  134.9 9.0 %multiply.5 = (bf16[256,1024]{1,0:T(8,128)(2,1)}, bf16[256,1024]{1,0:T(8,128)(2,1)}, bf16[256,1024]{1,0:T(8,128)(2,1)}, bf16[256,1024]{1,0:T(8,128)(2,1)}) custom-call(s32[4]{0:T(128)} %pad_add_fusion.spot_ref, s32[4]{0:T(128)} %pad_add_fusion.2.place_ref, bf16[2,256,512]{2,1,0:T(8,128)(2,1)} %copy-done, ...), custom_call_target="tpu_custom_call" | custom-call | flops 1 | bytes 1 | tf_op jit(solution)/shard_map/multiply/pallas_call | solution.py:257
  143.9 3.6 %collective-permute-start.15 = (bf16[256,1024]{1,0:T(8,128)(2,1)}, bf16[256,1024]{1,0:T(8,128)(2,1)S(1)}, u32[]{:S(2)}, u32[]{:S(2)}) collective-permute-start(bf16[256,1024]{1,0:T(8,128)(2,1)} %get-tuple-element.60), channel_id=1, source_target_pairs={{0,8},{24,16},{1,9},{25,17},{2,10},{26,18},{3,11},{27,19},{4,12},{... | collective-permute-start | bytes 1572872 | tf_op jit(solution)/shard_map/ppermute | solution.py:460
  153.1 3.2 %collective-permute-start.19 = (bf16[256,1024]{1,0:T(8,128)(2,1)}, bf16[256,1024]{1,0:T(8,128)(2,1)}, u32[]{:S(2)}, u32[]{:S(2)}) collective-permute-start(bf16[256,1024]{1,0:T(8,128)(2,1)} %get-tuple-element.61), channel_id=1, source_target_pairs={{0,8},{24,16},{1,9},{25,17},{2,10},{26,18},{3,11},{27,19},{4,12},{... | collective-permute-start | bytes 1572872 | tf_op jit(solution)/shard_map/ppermute | solution.py:461
  156.3 3.8 %collective-permute-done.15 = bf16[256,1024]{1,0:T(8,128)(2,1)S(1)} collective-permute-done((bf16[256,1024]{1,0:T(8,128)(2,1)}, bf16[256,1024]{1,0:T(8,128)(2,1)S(1)}, u32[]{:S(2)}, u32[]{:S(2)}) %collective-permute-start.15) | collective-permute-done | bytes 524320 | tf_op jit(solution)/shard_map/ppermute | solution.py:460
  163.6 6.9 %collective-permute-start.24 = (bf16[256,1024]{1,0:T(8,128)(2,1)S(1)}, bf16[256,1024]{1,0:T(8,128)(2,1)}, u32[]{:S(2)}, u32[]{:S(2)}) collective-permute-start(bf16[256,1024]{1,0:T(8,128)(2,1)S(1)} %copy-done.10), channel_id=1, source_target_pairs={{0,8},{24,16},{1,9},{25,17},{2,10},{26,18},{3,11},{27,19},{4,12},{... | collective-permute-start | bytes 1572872 | tf_op jit(solution)/shard_map/ppermute | solution.py:390
  170.5 3.5 %all-to-all-start.3 = ((bf16[4,256,512]{2,1,0:T(8,128)(2,1)}), bf16[4,256,512]{2,1,0:T(8,128)(2,1)S(1)}, u32[]{:S(2)}, u32[]{:S(2)}) async-start(bf16[4,256,512]{2,1,0:T(8,128)(2,1)} %all-to-all-done.2), calls=%async_computation.3 | async-start | bytes 2097152 | tf_op jit(solution)/shard_map/all_to_all | solution.py:454
  177.8 4.3 %collective-permute-start.18 = (bf16[256,1024]{1,0:T(8,128)(2,1)S(1)}, bf16[256,1024]{1,0:T(8,128)(2,1)}, u32[]{:S(2)}, u32[]{:S(2)}) collective-permute-start(bf16[256,1024]{1,0:T(8,128)(2,1)S(1)} %copy-done.11), channel_id=1, source_target_pairs={{0,8},{24,16},{1,9},{25,17},{2,10},{26,18},{3,11},{27,19},{4,12},{... | collective-permute-start | bytes 1572872 | tf_op jit(solution)/shard_map/ppermute | solution.py:463
  190.3 3.4 %collective-permute-done.24.near = bf16[256,1024]{1,0:T(8,128)(2,1)} collective-permute-done((bf16[256,1024]{1,0:T(8,128)(2,1)S(1)}, bf16[256,1024]{1,0:T(8,128)(2,1)}, u32[]{:S(2)}, u32[]{:S(2)}) %collective-permute-start.24) | collective-permute-done | bytes 524320 | tf_op jit(solution)/shard_map/ppermute | solution.py:390
  195.0 5.4 %collective-permute-done.23.outer = bf16[256,1024]{1,0:T(8,128)(2,1)} collective-permute-done((bf16[256,1024]{1,0:T(8,128)(2,1)}, bf16[256,1024]{1,0:T(8,128)(2,1)}, u32[]{:S(2)}, u32[]{:S(2)}) %collective-permute-start.23) | collective-permute-done | bytes 524320 | tf_op jit(solution)/shard_map/ppermute | solution.py:452
  204.1 5.4 %collective-permute-done.17.outer = bf16[256,1024]{1,0:T(8,128)(2,1)S(1)} collective-permute-done((bf16[256,1024]{1,0:T(8,128)(2,1)}, bf16[256,1024]{1,0:T(8,128)(2,1)S(1)}, u32[]{:S(2)}, u32[]{:S(2)}) %collective-permute-start.17) | collective-permute-done | bytes 524320 | tf_op jit(solution)/shard_map/ppermute | solution.py:465
  (106 shorter events, 64.8 us)
Async XLA Ops:
  2.3 26.3 %collective-permute-start.2 = (bf16[512,1024]{1,0:T(8,128)(2,1)}, bf16[512,1024]{1,0:T(8,128)(2,1)S(1)}, u32[]{:S(2)}, u32[]{:S(2)}) collective-permute-start(bf16[512,1024]{1,0:T(8,128)(2,1)} %cut.3), channel_id=1, source_target_pairs={{0,4},{4,0},{1,5},{5,1},{2,6},{6,2},{3,7},{7,3},{8,12},{12,8},{9,1... | collective-permute-start | bytes 3145736 | tf_op jit(solution)/shard_map/ppermute | solution.py:343
  13.3 12.0 %collective-permute-start = (bf16[2,2,112,512]{3,2,1,0:T(8,128)(2,1)S(1)}, bf16[2,2,112,512]{3,2,1,0:T(8,128)(2,1)S(1)}, u32[]{:S(2)}, u32[]{:S(2)}) collective-permute-start(bf16[2,2,112,512]{3,2,1,0:T(8,128)(2,1)S(1)} %get-tuple-element.36), channel_id=1, source_target_pairs={{0,2},{2,0},{1,3},{3,1},{4,6},{6,4},{5,7},{7,5},{8,10},{10,8},{9,1... | collective-permute-start | bytes 1376264 | tf_op jit(solution)/shard_map/ppermute | solution.py:359
  29.4 11.7 %collective-permute-start.7 = (bf16[2,2,96,512]{3,2,1,0:T(8,128)(2,1)S(1)}, bf16[2,2,96,512]{3,2,1,0:T(8,128)(2,1)}, u32[]{:S(2)}, u32[]{:S(2)}) collective-permute-start(bf16[2,2,96,512]{3,2,1,0:T(8,128)(2,1)S(1)} %get-tuple-element.40), channel_id=1, source_target_pairs={{0,2},{2,0},{1,3},{3,1},{4,6},{6,4},{5,7},{7,5},{8,10},{10,8},{9,1... | collective-permute-start | bytes 1179656 | tf_op jit(solution)/shard_map/ppermute | solution.py:359
  33.4 33.7 %collective-permute-start.9 = (bf16[512,1024]{1,0:T(8,128)(2,1)}, bf16[512,1024]{1,0:T(8,128)(2,1)}, u32[]{:S(2)}, u32[]{:S(2)}) collective-permute-start(bf16[512,1024]{1,0:T(8,128)(2,1)} %cut.4), channel_id=1, source_target_pairs={{0,4},{4,0},{1,5},{5,1},{2,6},{6,2},{3,7},{7,3},{8,12},{12,8},{9,1... | collective-permute-start | bytes 3145736 | tf_op jit(solution)/shard_map/ppermute | solution.py:343
  36.1 35.5 %all-to-all-start = ((bf16[8,112,512]{2,1,0:T(8,128)(2,1)}), bf16[8,112,512]{2,1,0:T(8,128)(2,1)S(1)}, u32[]{:S(2)}, u32[]{:S(2)}) async-start(bf16[8,112,512]{2,1,0:T(8,128)(2,1)} %bitcast.22), calls=%async_computation | async-start | bytes 1835008 | tf_op jit(solution)/shard_map/all_to_all | solution.py:384
  42.0 25.2 %collective-permute-start.8 = (bf16[2,96,512]{2,1,0:T(8,128)(2,1)S(1)}, bf16[2,96,512]{2,1,0:T(8,128)(2,1)S(1)}, u32[]{:S(2)}, u32[]{:S(2)}) collective-permute-start(bf16[2,96,512]{2,1,0:T(8,128)(2,1)S(1)} %slice_bitcast_fusion.4), channel_id=1, source_target_pairs={{0,1},{1,0},{2,3},{3,2},{4,5},{5,4},{6,7},{7,6},{8,9},{9,8},{10,11... | collective-permute-start | bytes 589832 | tf_op jit(solution)/shard_map/ppermute | solution.py:364
  71.6 28.5 %all-to-all-start.1 = ((bf16[8,96,512]{2,1,0:T(8,128)(2,1)}), bf16[8,96,512]{2,1,0:T(8,128)(2,1)S(1)}, u32[]{:S(2)}, u32[]{:S(2)}) async-start(bf16[8,96,512]{2,1,0:T(8,128)(2,1)} %bitcast.31), calls=%async_computation.1 | async-start | bytes 1572864 | tf_op jit(solution)/shard_map/all_to_all | solution.py:384
  77.9 13.9 %collective-permute-start.4 = (bf16[2,256,512]{2,1,0:T(8,128)(2,1)S(1)}, bf16[2,256,512]{2,1,0:T(8,128)(2,1)}, u32[]{:S(2)}, u32[]{:S(2)}) collective-permute-start(bf16[2,256,512]{2,1,0:T(8,128)(2,1)S(1)} %order.2.refs_0_), channel_id=1, source_target_pairs={{0,2},{2,0},{1,3},{3,1},{4,6},{6,4},{5,7},{7,5},{8,10},{10,8},{9,1... | collective-permute-start | bytes 1572872 | tf_op jit(solution)/shard_map/ppermute | solution.py:398
  81.1 52.4 %collective-permute-start.14 = (bf16[1024,1024]{1,0:T(8,128)(2,1)}, bf16[1024,1024]{1,0:T(8,128)(2,1)S(1)}, u32[]{:S(2)}, u32[]{:S(2)}) collective-permute-start(bf16[1024,1024]{1,0:T(8,128)(2,1)} %cut.5), channel_id=1, source_target_pairs={{0,4},{4,0},{1,5},{5,1},{2,6},{6,2},{3,7},{7,3},{8,12},{12,8},{9,1... | collective-permute-start | bytes 6291464 | tf_op jit(solution)/shard_map/ppermute | solution.py:343
  100.8 14.3 %collective-permute-start.11 = (bf16[2,256,512]{2,1,0:T(8,128)(2,1)S(1)}, bf16[2,256,512]{2,1,0:T(8,128)(2,1)}, u32[]{:S(2)}, u32[]{:S(2)}) collective-permute-start(bf16[2,256,512]{2,1,0:T(8,128)(2,1)S(1)} %order.3.refs_0_.refs_4_), channel_id=1, source_target_pairs={{0,2},{2,0},{1,3},{3,1},{4,6},{6,4},{5,7},{7,5},{8,10},{10,8},{9,1... | collective-permute-start | bytes 1572872 | tf_op jit(solution)/shard_map/ppermute | solution.py:398
  103.4 67.0 %all-to-all-start.2 = ((bf16[4,256,512]{2,1,0:T(8,128)(2,1)}), bf16[4,256,512]{2,1,0:T(8,128)(2,1)}, u32[]{:S(2)}, u32[]{:S(2)}) async-start(bf16[4,256,512]{2,1,0:T(8,128)(2,1)} %pad_maximum_fusion), calls=%async_computation.2 | async-start | bytes 2097152 | tf_op jit(solution)/shard_map/all_to_all | solution.py:420
  124.1 25.5 %collective-permute-start.21 = (bf16[256,1024]{1,0:T(8,128)(2,1)}, bf16[256,1024]{1,0:T(8,128)(2,1)}, u32[]{:S(2)}, u32[]{:S(2)}) collective-permute-start(bf16[256,1024]{1,0:T(8,128)(2,1)} %get-tuple-element.65), channel_id=1, source_target_pairs={{0,8},{24,16},{1,9},{25,17},{2,10},{26,18},{3,11},{27,19},{4,12},{... | collective-permute-start | bytes 1572872 | tf_op jit(solution)/shard_map/ppermute | solution.py:448
  143.9 16.2 %collective-permute-start.15 = (bf16[256,1024]{1,0:T(8,128)(2,1)}, bf16[256,1024]{1,0:T(8,128)(2,1)S(1)}, u32[]{:S(2)}, u32[]{:S(2)}) collective-permute-start(bf16[256,1024]{1,0:T(8,128)(2,1)} %get-tuple-element.60), channel_id=1, source_target_pairs={{0,8},{24,16},{1,9},{25,17},{2,10},{26,18},{3,11},{27,19},{4,12},{... | collective-permute-start | bytes 1572872 | tf_op jit(solution)/shard_map/ppermute | solution.py:460
  147.5 26.5 %collective-permute-start.25 = (bf16[256,1024]{1,0:T(8,128)(2,1)}, bf16[256,1024]{1,0:T(8,128)(2,1)}, u32[]{:S(2)}, u32[]{:S(2)}) collective-permute-start(bf16[256,1024]{1,0:T(8,128)(2,1)} %get-tuple-element.66), channel_id=1, source_target_pairs={{0,8},{24,16},{1,9},{25,17},{2,10},{26,18},{3,11},{27,19},{4,12},{... | collective-permute-start | bytes 1572872 | tf_op jit(solution)/shard_map/ppermute | solution.py:389
  151.7 26.1 %collective-permute-start.22 = (bf16[256,1024]{1,0:T(8,128)(2,1)}, bf16[256,1024]{1,0:T(8,128)(2,1)}, u32[]{:S(2)}, u32[]{:S(2)}) collective-permute-start(bf16[256,1024]{1,0:T(8,128)(2,1)} %add.111), channel_id=1, source_target_pairs={{8,16},{16,8},{9,17},{17,9},{10,18},{18,10},{11,19},{19,11},{12,20... | collective-permute-start | bytes 1572872 | tf_op jit(solution)/shard_map/ppermute | solution.py:451
  153.1 31.0 %collective-permute-start.19 = (bf16[256,1024]{1,0:T(8,128)(2,1)}, bf16[256,1024]{1,0:T(8,128)(2,1)}, u32[]{:S(2)}, u32[]{:S(2)}) collective-permute-start(bf16[256,1024]{1,0:T(8,128)(2,1)} %get-tuple-element.61), channel_id=1, source_target_pairs={{0,8},{24,16},{1,9},{25,17},{2,10},{26,18},{3,11},{27,19},{4,12},{... | collective-permute-start | bytes 1572872 | tf_op jit(solution)/shard_map/ppermute | solution.py:461
  162.2 25.4 %collective-permute-start.16 = (bf16[256,1024]{1,0:T(8,128)(2,1)}, bf16[256,1024]{1,0:T(8,128)(2,1)}, u32[]{:S(2)}, u32[]{:S(2)}) collective-permute-start(bf16[256,1024]{1,0:T(8,128)(2,1)} %add.108), channel_id=1, source_target_pairs={{8,16},{16,8},{9,17},{17,9},{10,18},{18,10},{11,19},{19,11},{12,20... | collective-permute-start | bytes 1572872 | tf_op jit(solution)/shard_map/ppermute | solution.py:462
  163.6 30.1 %collective-permute-start.24 = (bf16[256,1024]{1,0:T(8,128)(2,1)S(1)}, bf16[256,1024]{1,0:T(8,128)(2,1)}, u32[]{:S(2)}, u32[]{:S(2)}) collective-permute-start(bf16[256,1024]{1,0:T(8,128)(2,1)S(1)} %copy-done.10), channel_id=1, source_target_pairs={{0,8},{24,16},{1,9},{25,17},{2,10},{26,18},{3,11},{27,19},{4,12},{... | collective-permute-start | bytes 1572872 | tf_op jit(solution)/shard_map/ppermute | solution.py:390
  170.5 29.9 %all-to-all-start.3 = ((bf16[4,256,512]{2,1,0:T(8,128)(2,1)}), bf16[4,256,512]{2,1,0:T(8,128)(2,1)S(1)}, u32[]{:S(2)}, u32[]{:S(2)}) async-start(bf16[4,256,512]{2,1,0:T(8,128)(2,1)} %all-to-all-done.2), calls=%async_computation.3 | async-start | bytes 2097152 | tf_op jit(solution)/shard_map/all_to_all | solution.py:454
  176.3 18.7 %collective-permute-start.26 = (bf16[256,1024]{1,0:T(8,128)(2,1)}, bf16[256,1024]{1,0:T(8,128)(2,1)}, u32[]{:S(2)}, u32[]{:S(2)}) collective-permute-start(bf16[256,1024]{1,0:T(8,128)(2,1)} %add.113), channel_id=1, source_target_pairs={{8,16},{16,8},{9,17},{17,9},{10,18},{18,10},{11,19},{19,11},{12,20... | collective-permute-start | bytes 1572872 | tf_op jit(solution)/shard_map/ppermute | solution.py:450
  177.8 26.3 %collective-permute-start.18 = (bf16[256,1024]{1,0:T(8,128)(2,1)S(1)}, bf16[256,1024]{1,0:T(8,128)(2,1)}, u32[]{:S(2)}, u32[]{:S(2)}) collective-permute-start(bf16[256,1024]{1,0:T(8,128)(2,1)S(1)} %copy-done.11), channel_id=1, source_target_pairs={{0,8},{24,16},{1,9},{25,17},{2,10},{26,18},{3,11},{27,19},{4,12},{... | collective-permute-start | bytes 1572872 | tf_op jit(solution)/shard_map/ppermute | solution.py:463
  184.1 16.3 %collective-permute-start.23 = (bf16[256,1024]{1,0:T(8,128)(2,1)}, bf16[256,1024]{1,0:T(8,128)(2,1)}, u32[]{:S(2)}, u32[]{:S(2)}) collective-permute-start(bf16[256,1024]{1,0:T(8,128)(2,1)} %add.112), channel_id=1, source_target_pairs={{8,0},{16,24},{9,1},{17,25},{10,2},{18,26},{11,3},{19,27},{12,4},{... | collective-permute-start | bytes 1572872 | tf_op jit(solution)/shard_map/ppermute | solution.py:452
  187.6 16.5 %collective-permute-start.20 = (bf16[256,1024]{1,0:T(8,128)(2,1)}, bf16[256,1024]{1,0:T(8,128)(2,1)S(1)}, u32[]{:S(2)}, u32[]{:S(2)}) collective-permute-start(bf16[256,1024]{1,0:T(8,128)(2,1)} %add.110), channel_id=1, source_target_pairs={{8,16},{16,8},{9,17},{17,9},{10,18},{18,10},{11,19},{19,11},{12,20... | collective-permute-start | bytes 1572872 | tf_op jit(solution)/shard_map/ppermute | solution.py:464
  193.7 15.8 %collective-permute-start.17 = (bf16[256,1024]{1,0:T(8,128)(2,1)}, bf16[256,1024]{1,0:T(8,128)(2,1)S(1)}, u32[]{:S(2)}, u32[]{:S(2)}) collective-permute-start(bf16[256,1024]{1,0:T(8,128)(2,1)} %add.109), channel_id=1, source_target_pairs={{8,0},{16,24},{9,1},{17,25},{10,2},{18,26},{11,3},{19,27},{12,4},{... | collective-permute-start | bytes 1572872 | tf_op jit(solution)/shard_map/ppermute | solution.py:465
  (23 other events, 279.0 us)

commit v4 on v3

--- a/solution.py
+++ b/solution.py
@@ -25,7 +25,7 @@
 
 def pool_kernel(groups, share, quarter, whole, count_ref, spot_ref, length_ref, items_ref, *rest):
     out_refs = rest[: len(groups)]
-    items, wide, by_feat, first, last, pooled, sems = rest[len(groups) :]
+    items, wide, by_feat, last, pooled, sems = rest[len(groups) :]
     slots, feats, width = items.shape
     rows = length_ref.shape[1]
     step = slots // sems.shape[0]
@@ -44,13 +44,10 @@
     row_id = lax.broadcasted_iota(I32, (rows, rows), 0)
     col_id = lax.broadcasted_iota(I32, (rows, rows), 1)
     lower = jnp.where(col_id <= row_id, 1.0, 0.0).astype(BF16)
-    strict = jnp.where(col_id < row_id, 1.0, 0.0).astype(BF16)
     lengths = length_ref[...].astype(F32).astype(BF16)
     dims = (((1,), (1,)), ((), ()))
     ends = lax.dot_general(lower, lengths, dims, preferred_element_type=F32).astype(I32)
-    starts = lax.dot_general(strict, lengths, dims, preferred_element_type=F32).astype(I32)
     for f in range(feats):
-        first[f] = jnp.broadcast_to(starts[:, f : f + 1], (rows, width))
         last[f] = jnp.broadcast_to(ends[:, f : f + 1], (rows, width))
 
     for k in range(sems.shape[0]):
@@ -60,25 +57,18 @@
         for f in range(feats):
             by_feat[f, part, :] = wide[pl.ds(f, step, stride=feats), :].astype(BF16)
 
-    lane = lax.broadcasted_iota(I32, (rows, width), 1)
+    lane = lax.broadcasted_iota(I32, (1, width), 1)
+    top = lax.broadcasted_iota(I32, (rows, width), 0) == 0
 
     @pl.loop(0, feats, unroll=2)
     def _(f):
-        low = first[f]
         high = last[f]
-        total = jnp.zeros((rows, width), F32)
-        for k in range(slots // (2 * width)):
-            tiles = []
-            for half in range(2):
-                where = lane + (2 * k + half) * width
-                inside = (where >= low) & (where < high)
-                tiles.append(jnp.where(inside, 1.0, 0.0).astype(BF16))
-            total += jnp.dot(
-                jnp.concatenate(tiles, axis=1),
-                by_feat[f, pl.ds(2 * k * width, 2 * width), :],
-                preferred_element_type=F32,
-            )
-        pooled[:, pl.ds(pl.multiple_of(f * width, width), width)] = total.astype(BF16)
+        tiles = []
+        for k in range(slots // width):
+            tiles.append(jnp.where(lane + k * width < high, 1.0, 0.0).astype(BF16))
+        total = jnp.dot(jnp.concatenate(tiles, axis=1), by_feat[f], preferred_element_type=F32)
+        above = jnp.where(top, 0.0, pltpu.roll(total, 1, 0))
+        pooled[:, pl.ds(pl.multiple_of(f * width, width), width)] = (total - above).astype(BF16)
 
     slot = lax.broadcasted_iota(I32, (CAP, rows), 0)
     source = lax.broadcasted_iota(I32, (CAP, rows), 1)
@@ -139,7 +129,6 @@
             VMEM((slots // chunks * feats, width), F32),
             VMEM((feats, slots, width), BF16),
             VMEM((feats, rows, width), I32),
-            VMEM((feats, rows, width), I32),
             VMEM((rows, feats * width), BF16),
             pltpu.SemaphoreType.DMA((chunks,)),
         ],
@@ -193,7 +182,7 @@
         grid=((high - low) // tile,),
         in_specs=[pl.BlockSpec((tile, depth), lambda n: (n + low // tile, 0))],
         out_specs=pl.BlockSpec((tile, depth), lambda n: (n, 0)),
-        compiler_params=params(60),
+        compiler_params=params(12),
         cost_estimate=SMALL,
         name="cut",
     )(weight)
@@ -267,7 +256,7 @@
         + [other_spec(*span) for span in spans],
         out_specs=[pl.BlockSpec((rows, tile), lambda n: (0, n)) for _ in range(total)],
         scratch_shapes=[VMEM((count, total * rows, quarter), BF16)],
-        compiler_params=params(60),
+        compiler_params=params(40),
         cost_estimate=SMALL,
         name="multiply",
     )(spots, places, *[piece for group in groups for piece in group], own, *others)
@@ -306,7 +295,7 @@
         + [pl.BlockSpec(memory_space=ANY) for _ in more],
         out_specs=pl.BlockSpec((rows, tile), lambda n: (0, n + first)),
         input_output_aliases={8: 0} if more else {},
-        compiler_params=params(60),
+        compiler_params=params(12),
         cost_estimate=SMALL,
         name="finish",
     )(is_end, *sums, base, bias, *more)

time: 214 us -> 210 us (0.981)
  Pallas kernels: 50.5 us -> 40.2 us
  local copies, waits for them, and re-layouts: 5.8 us -> 14.3 us
  other arithmetic: 21 us -> 18.2 us
    unnamed x32 -> x42, local copies, waits for them, and re-layouts: 4.04 us -> 12.6 us
    pallas_call x3, Pallas kernels: 7.21 us -> 2.53 us  [cut(): pl.pallas_call(cut_kernel, out_shape=jax.ShapeDtypeStruct((high - low, de...]
    pallas_call x3, Pallas kernels: 21.1 us -> 16.5 us  [multiply(): pl.pallas_call(functools.partial(multiply_kernel, (len(groups), count), s...]
    ppermute x3, waiting for transfers between devices: 33.1 us -> 29.5 us  [fetch(): return lax.ppermute(cut(source, *parts[which], tile), 'b', swap)]
    another operation x6, other arithmetic: 4.21 us -> 6.37 us  [shards(): jnp.stack([pick(near[q], [(k, got[k]) for k in range(4)]) for q in range(...]
    add x2, other arithmetic: 4.15 us -> 1.99 us  [shards(): mid2 = lax.ppermute(far0 + in1, 'a', middle)]
  transfers between devices with their start and end apart: 31 -> 31, of which waited for: 13 -> 15; matrix products, arithmetic and copies ran while one was open for 11% -> 10% of each run, Pallas kernels for 21% -> 18%
where the time goes in v4:
time: 210 us; the launch traced here: 209 us
  waiting for transfers between devices  71.1 us (34%)
  starting transfers between devices  64.4 us (31%)
  Pallas kernels  40.2 us (19%)
  other arithmetic  18.2 us (9%)
  local copies, waits for them, and re-layouts  14.3 us (7%)
    ppermute x3, waiting for transfers between devices, fetch(): return lax.ppermute(cut(source, *parts[which], tile), 'b', swap)  29.5 us
    pallas_call x3, Pallas kernels, multiply(): pl.pallas_call(functools.partial(multiply_kernel, (len(groups), count), s...  16.5 us
    pallas_call x2, Pallas kernels, pool(): pl.pallas_call(functools.partial(pool_kernel, groups, share, quarter, fea...  14.7 us
    ppermute x2, waiting for transfers between devices, shards(): far = lax.ppermute(mine, 'y', swap)  14.5 us
    unnamed x42, local copies, waits for them, and re-layouts  12.6 us
    ppermute x2, starting transfers between devices, shards(): in3 = lax.ppermute(near1, 'a', inward)  12.3 us
    all_to_all x2, starting transfers between devices, shards(): slots = lax.all_to_all(sent, ('a', 'b'), 0, 0, tiled=True)  10.7 us
    ppermute x2, waiting for transfers between devices, shards(): out3 = lax.ppermute(near0 + mid2, 'a', outward)  9.76 us
  transfers between devices with their start and end apart: 31, of which 15 were waited for; matrix products, arithmetic and copies ran while one was open for 10% of the time, Pallas kernels for 18%

profile of v4, /device:TPU:0, one launch (start us, length us, event | category | flops | bytes accessed | tf_op | source)
XLA Modules:
  0.0 208.5 jit_solution(13992451266504423183)
XLA Ops:
  2.3 3.0 %collective-permute-start.2 = (bf16[512,1024]{1,0:T(8,128)(2,1)S(1)}, bf16[512,1024]{1,0:T(8,128)(2,1)S(1)}, u32[]{:S(2)}, u32[]{:S(2)}) collective-permute-start(bf16[512,1024]{1,0:T(8,128)(2,1)S(1)} %cut.3), channel_id=1, source_target_pairs={{0,4},{4,0},{1,5},{5,1},{2,6},{6,2},{3,7},{7,3},{8,12},{12,8},{9,1... | collective-permute-start | bytes 3145736 | tf_op jit(solution)/shard_map/ppermute | solution.py:332
  5.4 7.6 %pool.2 = (bf16[2,2,112,512]{3,2,1,0:T(8,128)(2,1)S(1)}, bf16[2,2,96,512]{3,2,1,0:T(8,128)(2,1)}) custom-call(s32[1,8]{1,0:T(1,128)S(1)} %copy-done.18, s32[3]{0:T(128)S(1)} %get-tuple-element.79.spot_ref, s32[8,256]{1,0:T(8,128)S(1)} %get-tuple-element.78.length_ref, bf16[2048,16,128]{2,1,0:T(8,128)(2,1)} %items_ref.3), custom_call_target="tpu_custom_call" | custom-call | flops 1 | bytes 1 | tf_op jit(solution)/shard_map/pool/pallas_call | solution.py:112
  14.6 7.1 %pool.3 = (bf16[2,2,112,512]{3,2,1,0:T(8,128)(2,1)S(1)}, bf16[2,2,96,512]{3,2,1,0:T(8,128)(2,1)S(1)}) custom-call(s32[1,8]{1,0:T(1,128)S(1)} %copy-done.18, s32[3]{0:T(128)S(1)} %get-tuple-element.80.spot_ref, s32[8,256]{1,0:T(8,128)S(1)} %get-tuple-element.77.length_ref, bf16[2048,16,128]{2,1,0:T(8,128)(2,1)} %items_ref.3), custom_call_target="tpu_custom_call" | custom-call | flops 1 | bytes 1 | tf_op jit(solution)/shard_map/pool/pallas_call | solution.py:112
  21.7 3.3 %collective-permute-done = bf16[2,2,112,512]{3,2,1,0:T(8,128)(2,1)S(1)} collective-permute-done((bf16[2,2,112,512]{3,2,1,0:T(8,128)(2,1)S(1)}, bf16[2,2,112,512]{3,2,1,0:T(8,128)(2,1)S(1)}, u32[]{:S(2)}, u32[]{:S(2)}) %collective-permute-start) | collective-permute-done | bytes 458784 | tf_op jit(solution)/shard_map/ppermute | solution.py:348
  25.1 3.3 %collective-permute-done.2.refs_5_ = bf16[512,1024]{1,0:T(8,128)(2,1)S(1)} collective-permute-done((bf16[512,1024]{1,0:T(8,128)(2,1)S(1)}, bf16[512,1024]{1,0:T(8,128)(2,1)S(1)}, u32[]{:S(2)}, u32[]{:S(2)}) %collective-permute-start.2) | collective-permute-done | bytes 1048608 | tf_op jit(solution)/shard_map/ppermute | solution.py:332
  36.8 4.9 %all-to-all-start = ((bf16[8,112,512]{2,1,0:T(8,128)(2,1)}), bf16[8,112,512]{2,1,0:T(8,128)(2,1)S(1)}, u32[]{:S(2)}, u32[]{:S(2)}) async-start(bf16[8,112,512]{2,1,0:T(8,128)(2,1)} %bitcast.126), calls=%async_computation | async-start | bytes 1835008 | tf_op jit(solution)/shard_map/all_to_all | solution.py:373
  42.7 22.8 %collective-permute-done.9.refs_6_ = bf16[512,1024]{1,0:T(8,128)(2,1)S(1)} collective-permute-done((bf16[512,1024]{1,0:T(8,128)(2,1)}, bf16[512,1024]{1,0:T(8,128)(2,1)S(1)}, u32[]{:S(2)}, u32[]{:S(2)}) %collective-permute-start.9) | collective-permute-done | bytes 1048608 | tf_op jit(solution)/shard_map/ppermute | solution.py:332
  70.1 5.8 %all-to-all-start.1 = ((bf16[8,96,512]{2,1,0:T(8,128)(2,1)}), bf16[8,96,512]{2,1,0:T(8,128)(2,1)}, u32[]{:S(2)}, u32[]{:S(2)}) async-start(bf16[8,96,512]{2,1,0:T(8,128)(2,1)} %bitcast.127), calls=%async_computation.1 | async-start | bytes 1572864 | tf_op jit(solution)/shard_map/all_to_all | solution.py:373
  83.8 7.6 %collective-permute-done.4.refs_1_ = bf16[2,256,512]{2,1,0:T(8,128)(2,1)S(1)} collective-permute-done((bf16[2,256,512]{2,1,0:T(8,128)(2,1)S(1)}, bf16[2,256,512]{2,1,0:T(8,128)(2,1)S(1)}, u32[]{:S(2)}, u32[]{:S(2)}) %collective-permute-start.4) | collective-permute-done | bytes 524320 | tf_op jit(solution)/shard_map/ppermute | solution.py:387
  95.6 4.8 %multiply.3 = (bf16[256,1024]{1,0:T(8,128)(2,1)}, bf16[256,1024]{1,0:T(8,128)(2,1)}) custom-call(s32[4]{0:T(128)S(1)} %pad_add_fusion.spot_ref, s32[2]{0:T(128)S(1)} %get-tuple-element.68.place_ref, bf16[2,256,512]{2,1,0:T(8,128)(2,1)S(1)} %order.2.refs_0_, bf16[2,256,512]{2,1,0:T(8,128)(2,1)S(1)} %collective-permute-done.4.refs_1_, ...), custom_call_target="tpu_custom_call" | custom-call | flops 1 | bytes 1 | tf_op jit(solution)/shard_map/multiply/pallas_call | solution.py:246
  104.7 4.8 %all-to-all-start.2 = ((bf16[4,256,512]{2,1,0:T(8,128)(2,1)}), bf16[4,256,512]{2,1,0:T(8,128)(2,1)}, u32[]{:S(2)}, u32[]{:S(2)}) async-start(bf16[4,256,512]{2,1,0:T(8,128)(2,1)} %pad_maximum_fusion), calls=%async_computation.2 | async-start | bytes 2097152 | tf_op jit(solution)/shard_map/all_to_all | solution.py:409
  109.5 6.9 %collective-permute-done.11.refs_1_.refs_5_ = bf16[2,256,512]{2,1,0:T(8,128)(2,1)} collective-permute-done((bf16[2,256,512]{2,1,0:T(8,128)(2,1)S(1)}, bf16[2,256,512]{2,1,0:T(8,128)(2,1)}, u32[]{:S(2)}, u32[]{:S(2)}) %collective-permute-start.11) | collective-permute-done | bytes 524320 | tf_op jit(solution)/shard_map/ppermute | solution.py:387
  121.8 4.1 %multiply.4 = (bf16[256,1024]{1,0:T(8,128)(2,1)S(1)}, bf16[256,1024]{1,0:T(8,128)(2,1)S(1)}) custom-call(s32[4]{0:T(128)S(1)} %pad_add_fusion.spot_ref, s32[2]{0:T(128)S(1)} %get-tuple-element.68.place_ref, bf16[2,256,512]{2,1,0:T(8,128)(2,1)S(1)} %order.3.refs_0_.refs_4_, bf16[2,256,512]{2,1,0:T(8,128)(2,1)} %collective-permute-done.11.refs_1_.refs_5_, ...), custom_call_target="tpu_custom_call" | custom-call | flops 1 | bytes 1 | tf_op jit(solution)/shard_map/multiply/pallas_call | solution.py:246
  125.9 3.7 %collective-permute-start.21 = (bf16[256,1024]{1,0:T(8,128)(2,1)S(1)}, bf16[256,1024]{1,0:T(8,128)(2,1)S(1)}, u32[]{:S(2)}, u32[]{:S(2)}) collective-permute-start(bf16[256,1024]{1,0:T(8,128)(2,1)S(1)} %get-tuple-element.65), channel_id=1, source_target_pairs={{0,8},{24,16},{1,9},{25,17},{2,10},{26,18},{3,11},{27,19},{4,12},{... | collective-permute-start | bytes 1572872 | tf_op jit(solution)/shard_map/ppermute | solution.py:437
  129.6 3.4 %collective-permute-done.14.refs_9_ = bf16[1024,1024]{1,0:T(8,128)(2,1)} collective-permute-done((bf16[1024,1024]{1,0:T(8,128)(2,1)}, bf16[1024,1024]{1,0:T(8,128)(2,1)}, u32[]{:S(2)}, u32[]{:S(2)}) %collective-permute-start.14) | collective-permute-done | bytes 2097184 | tf_op jit(solution)/shard_map/ppermute | solution.py:332
  133.0 7.6 %multiply.5 = (bf16[256,1024]{1,0:T(8,128)(2,1)}, bf16[256,1024]{1,0:T(8,128)(2,1)S(1)}, bf16[256,1024]{1,0:T(8,128)(2,1)S(1)}, bf16[256,1024]{1,0:T(8,128)(2,1)S(1)}) custom-call(s32[4]{0:T(128)S(1)} %pad_add_fusion.spot_ref, s32[4]{0:T(128)S(1)} %pad_add_fusion.2.place_ref, bf16[2,256,512]{2,1,0:T(8,128)(2,1)S(1)} %order.2.refs_0_, ...), custom_call_target="tpu_custom_call" | custom-call | flops 1 | bytes 1 | tf_op jit(solution)/shard_map/multiply/pallas_call | solution.py:246
  141.4 4.2 %collective-permute-start.15 = (bf16[256,1024]{1,0:T(8,128)(2,1)S(1)}, bf16[256,1024]{1,0:T(8,128)(2,1)S(1)}, u32[]{:S(2)}, u32[]{:S(2)}) collective-permute-start(bf16[256,1024]{1,0:T(8,128)(2,1)S(1)} %get-tuple-element.60), channel_id=1, source_target_pairs={{0,8},{24,16},{1,9},{25,17},{2,10},{26,18},{3,11},{27,19},{4,12},{... | collective-permute-start | bytes 1572872 | tf_op jit(solution)/shard_map/ppermute | solution.py:449
  150.1 3.2 %collective-permute-start.19 = (bf16[256,1024]{1,0:T(8,128)(2,1)}, bf16[256,1024]{1,0:T(8,128)(2,1)}, u32[]{:S(2)}, u32[]{:S(2)}) collective-permute-start(bf16[256,1024]{1,0:T(8,128)(2,1)} %get-tuple-element.61), channel_id=1, source_target_pairs={{0,8},{24,16},{1,9},{25,17},{2,10},{26,18},{3,11},{27,19},{4,12},{... | collective-permute-start | bytes 1572872 | tf_op jit(solution)/shard_map/ppermute | solution.py:450
  153.3 4.6 %collective-permute-done.15 = bf16[256,1024]{1,0:T(8,128)(2,1)S(1)} collective-permute-done((bf16[256,1024]{1,0:T(8,128)(2,1)S(1)}, bf16[256,1024]{1,0:T(8,128)(2,1)S(1)}, u32[]{:S(2)}, u32[]{:S(2)}) %collective-permute-start.15) | collective-permute-done | bytes 524320 | tf_op jit(solution)/shard_map/ppermute | solution.py:449
  160.4 6.3 %collective-permute-start.24 = (bf16[256,1024]{1,0:T(8,128)(2,1)}, bf16[256,1024]{1,0:T(8,128)(2,1)S(1)}, u32[]{:S(2)}, u32[]{:S(2)}) collective-permute-start(bf16[256,1024]{1,0:T(8,128)(2,1)} %get-tuple-element.64.own_mid), channel_id=1, source_target_pairs={{0,8},{24,16},{1,9},{25,17},{2,10},{26,18},{3,11},{27,19},{4,12},{... | collective-permute-start | bytes 1572872 | tf_op jit(solution)/shard_map/ppermute | solution.py:379
  166.7 3.5 %all-to-all-start.3 = ((bf16[4,256,512]{2,1,0:T(8,128)(2,1)}), bf16[4,256,512]{2,1,0:T(8,128)(2,1)S(1)}, u32[]{:S(2)}, u32[]{:S(2)}) async-start(bf16[4,256,512]{2,1,0:T(8,128)(2,1)} %all-to-all-done.2), calls=%async_computation.3 | async-start | bytes 2097152 | tf_op jit(solution)/shard_map/all_to_all | solution.py:443
  174.0 6.0 %collective-permute-start.18 = (bf16[256,1024]{1,0:T(8,128)(2,1)S(1)}, bf16[256,1024]{1,0:T(8,128)(2,1)}, u32[]{:S(2)}, u32[]{:S(2)}) collective-permute-start(bf16[256,1024]{1,0:T(8,128)(2,1)S(1)} %copy-done.16), channel_id=1, source_target_pairs={{0,8},{24,16},{1,9},{25,17},{2,10},{26,18},{3,11},{27,19},{4,12},{... | collective-permute-start | bytes 1572872 | tf_op jit(solution)/shard_map/ppermute | solution.py:452
  193.1 3.7 %collective-permute-done.23.outer = bf16[256,1024]{1,0:T(8,128)(2,1)} collective-permute-done((bf16[256,1024]{1,0:T(8,128)(2,1)}, bf16[256,1024]{1,0:T(8,128)(2,1)}, u32[]{:S(2)}, u32[]{:S(2)}) %collective-permute-start.23) | collective-permute-done | bytes 524320 | tf_op jit(solution)/shard_map/ppermute | solution.py:441
  200.3 6.0 %collective-permute-done.17.outer = bf16[256,1024]{1,0:T(8,128)(2,1)} collective-permute-done((bf16[256,1024]{1,0:T(8,128)(2,1)}, bf16[256,1024]{1,0:T(8,128)(2,1)}, u32[]{:S(2)}, u32[]{:S(2)}) %collective-permute-start.17) | collective-permute-done | bytes 524320 | tf_op jit(solution)/shard_map/ppermute | solution.py:454
  (116 shorter events, 69.9 us)
Async XLA Ops:
  2.3 26.2 %collective-permute-start.2 = (bf16[512,1024]{1,0:T(8,128)(2,1)S(1)}, bf16[512,1024]{1,0:T(8,128)(2,1)S(1)}, u32[]{:S(2)}, u32[]{:S(2)}) collective-permute-start(bf16[512,1024]{1,0:T(8,128)(2,1)S(1)} %cut.3), channel_id=1, source_target_pairs={{0,4},{4,0},{1,5},{5,1},{2,6},{6,2},{3,7},{7,3},{8,12},{12,8},{9,1... | collective-permute-start | bytes 3145736 | tf_op jit(solution)/shard_map/ppermute | solution.py:332
  13.0 12.1 %collective-permute-start = (bf16[2,2,112,512]{3,2,1,0:T(8,128)(2,1)S(1)}, bf16[2,2,112,512]{3,2,1,0:T(8,128)(2,1)S(1)}, u32[]{:S(2)}, u32[]{:S(2)}) collective-permute-start(bf16[2,2,112,512]{3,2,1,0:T(8,128)(2,1)S(1)} %get-tuple-element.36), channel_id=1, source_target_pairs={{0,2},{2,0},{1,3},{3,1},{4,6},{6,4},{5,7},{7,5},{8,10},{10,8},{9,1... | collective-permute-start | bytes 1376264 | tf_op jit(solution)/shard_map/ppermute | solution.py:348
  29.2 12.5 %collective-permute-start.7 = (bf16[2,2,96,512]{3,2,1,0:T(8,128)(2,1)}, bf16[2,2,96,512]{3,2,1,0:T(8,128)(2,1)}, u32[]{:S(2)}, u32[]{:S(2)}) collective-permute-start(bf16[2,2,96,512]{3,2,1,0:T(8,128)(2,1)} %get-tuple-element.40), channel_id=1, source_target_pairs={{0,2},{2,0},{1,3},{3,1},{4,6},{6,4},{5,7},{7,5},{8,10},{10,8},{9,1... | collective-permute-start | bytes 1179656 | tf_op jit(solution)/shard_map/ppermute | solution.py:348
  32.0 33.6 %collective-permute-start.9 = (bf16[512,1024]{1,0:T(8,128)(2,1)}, bf16[512,1024]{1,0:T(8,128)(2,1)S(1)}, u32[]{:S(2)}, u32[]{:S(2)}) collective-permute-start(bf16[512,1024]{1,0:T(8,128)(2,1)} %cut.4), channel_id=1, source_target_pairs={{0,4},{4,0},{1,5},{5,1},{2,6},{6,2},{3,7},{7,3},{8,12},{12,8},{9,1... | collective-permute-start | bytes 3145736 | tf_op jit(solution)/shard_map/ppermute | solution.py:332
  36.8 33.3 %all-to-all-start = ((bf16[8,112,512]{2,1,0:T(8,128)(2,1)}), bf16[8,112,512]{2,1,0:T(8,128)(2,1)S(1)}, u32[]{:S(2)}, u32[]{:S(2)}) async-start(bf16[8,112,512]{2,1,0:T(8,128)(2,1)} %bitcast.126), calls=%async_computation | async-start | bytes 1835008 | tf_op jit(solution)/shard_map/all_to_all | solution.py:373
  42.6 23.0 %collective-permute-start.8 = (bf16[2,96,512]{2,1,0:T(8,128)(2,1)S(1)}, bf16[2,96,512]{2,1,0:T(8,128)(2,1)S(1)}, u32[]{:S(2)}, u32[]{:S(2)}) collective-permute-start(bf16[2,96,512]{2,1,0:T(8,128)(2,1)S(1)} %slice_bitcast_fusion.4), channel_id=1, source_target_pairs={{0,1},{1,0},{2,3},{3,2},{4,5},{5,4},{6,7},{7,6},{8,9},{9,8},{10,11... | collective-permute-start | bytes 589832 | tf_op jit(solution)/shard_map/ppermute | solution.py:353
  70.1 30.3 %all-to-all-start.1 = ((bf16[8,96,512]{2,1,0:T(8,128)(2,1)}), bf16[8,96,512]{2,1,0:T(8,128)(2,1)}, u32[]{:S(2)}, u32[]{:S(2)}) async-start(bf16[8,96,512]{2,1,0:T(8,128)(2,1)} %bitcast.127), calls=%async_computation.1 | async-start | bytes 1572864 | tf_op jit(solution)/shard_map/all_to_all | solution.py:373
  77.6 13.8 %collective-permute-start.4 = (bf16[2,256,512]{2,1,0:T(8,128)(2,1)S(1)}, bf16[2,256,512]{2,1,0:T(8,128)(2,1)S(1)}, u32[]{:S(2)}, u32[]{:S(2)}) collective-permute-start(bf16[2,256,512]{2,1,0:T(8,128)(2,1)S(1)} %order.2.refs_0_), channel_id=1, source_target_pairs={{0,2},{2,0},{1,3},{3,1},{4,6},{6,4},{5,7},{7,5},{8,10},{10,8},{9,1... | collective-permute-start | bytes 1572872 | tf_op jit(solution)/shard_map/ppermute | solution.py:387
  81.8 51.2 %collective-permute-start.14 = (bf16[1024,1024]{1,0:T(8,128)(2,1)}, bf16[1024,1024]{1,0:T(8,128)(2,1)}, u32[]{:S(2)}, u32[]{:S(2)}) collective-permute-start(bf16[1024,1024]{1,0:T(8,128)(2,1)} %cut.5), channel_id=1, source_target_pairs={{0,4},{4,0},{1,5},{5,1},{2,6},{6,2},{3,7},{7,3},{8,12},{12,8},{9,1... | collective-permute-start | bytes 6291464 | tf_op jit(solution)/shard_map/ppermute | solution.py:332
  102.2 14.3 %collective-permute-start.11 = (bf16[2,256,512]{2,1,0:T(8,128)(2,1)S(1)}, bf16[2,256,512]{2,1,0:T(8,128)(2,1)}, u32[]{:S(2)}, u32[]{:S(2)}) collective-permute-start(bf16[2,256,512]{2,1,0:T(8,128)(2,1)S(1)} %order.3.refs_0_.refs_4_), channel_id=1, source_target_pairs={{0,2},{2,0},{1,3},{3,1},{4,6},{6,4},{5,7},{7,5},{8,10},{10,8},{9,1... | collective-permute-start | bytes 1572872 | tf_op jit(solution)/shard_map/ppermute | solution.py:387
  104.7 62.0 %all-to-all-start.2 = ((bf16[4,256,512]{2,1,0:T(8,128)(2,1)}), bf16[4,256,512]{2,1,0:T(8,128)(2,1)}, u32[]{:S(2)}, u32[]{:S(2)}) async-start(bf16[4,256,512]{2,1,0:T(8,128)(2,1)} %pad_maximum_fusion), calls=%async_computation.2 | async-start | bytes 2097152 | tf_op jit(solution)/shard_map/all_to_all | solution.py:409
  125.9 21.8 %collective-permute-start.21 = (bf16[256,1024]{1,0:T(8,128)(2,1)S(1)}, bf16[256,1024]{1,0:T(8,128)(2,1)S(1)}, u32[]{:S(2)}, u32[]{:S(2)}) collective-permute-start(bf16[256,1024]{1,0:T(8,128)(2,1)S(1)} %get-tuple-element.65), channel_id=1, source_target_pairs={{0,8},{24,16},{1,9},{25,17},{2,10},{26,18},{3,11},{27,19},{4,12},{... | collective-permute-start | bytes 1572872 | tf_op jit(solution)/shard_map/ppermute | solution.py:437
  141.4 16.6 %collective-permute-start.15 = (bf16[256,1024]{1,0:T(8,128)(2,1)S(1)}, bf16[256,1024]{1,0:T(8,128)(2,1)S(1)}, u32[]{:S(2)}, u32[]{:S(2)}) collective-permute-start(bf16[256,1024]{1,0:T(8,128)(2,1)S(1)} %get-tuple-element.60), channel_id=1, source_target_pairs={{0,8},{24,16},{1,9},{25,17},{2,10},{26,18},{3,11},{27,19},{4,12},{... | collective-permute-start | bytes 1572872 | tf_op jit(solution)/shard_map/ppermute | solution.py:449
  145.6 24.7 %collective-permute-start.25 = (bf16[256,1024]{1,0:T(8,128)(2,1)}, bf16[256,1024]{1,0:T(8,128)(2,1)}, u32[]{:S(2)}, u32[]{:S(2)}) collective-permute-start(bf16[256,1024]{1,0:T(8,128)(2,1)} %get-tuple-element.66), channel_id=1, source_target_pairs={{0,8},{24,16},{1,9},{25,17},{2,10},{26,18},{3,11},{27,19},{4,12},{... | collective-permute-start | bytes 1572872 | tf_op jit(solution)/shard_map/ppermute | solution.py:378
  148.7 25.3 %collective-permute-start.22 = (bf16[256,1024]{1,0:T(8,128)(2,1)}, bf16[256,1024]{1,0:T(8,128)(2,1)}, u32[]{:S(2)}, u32[]{:S(2)}) collective-permute-start(bf16[256,1024]{1,0:T(8,128)(2,1)} %add.111), channel_id=1, source_target_pairs={{8,16},{16,8},{9,17},{17,9},{10,18},{18,10},{11,19},{19,11},{12,20... | collective-permute-start | bytes 1572872 | tf_op jit(solution)/shard_map/ppermute | solution.py:440
  150.1 32.0 %collective-permute-start.19 = (bf16[256,1024]{1,0:T(8,128)(2,1)}, bf16[256,1024]{1,0:T(8,128)(2,1)}, u32[]{:S(2)}, u32[]{:S(2)}) collective-permute-start(bf16[256,1024]{1,0:T(8,128)(2,1)} %get-tuple-element.61), channel_id=1, source_target_pairs={{0,8},{24,16},{1,9},{25,17},{2,10},{26,18},{3,11},{27,19},{4,12},{... | collective-permute-start | bytes 1572872 | tf_op jit(solution)/shard_map/ppermute | solution.py:450
  158.9 26.7 %collective-permute-start.16 = (bf16[256,1024]{1,0:T(8,128)(2,1)}, bf16[256,1024]{1,0:T(8,128)(2,1)}, u32[]{:S(2)}, u32[]{:S(2)}) collective-permute-start(bf16[256,1024]{1,0:T(8,128)(2,1)} %add.108), channel_id=1, source_target_pairs={{8,16},{16,8},{9,17},{17,9},{10,18},{18,10},{11,19},{19,11},{12,20... | collective-permute-start | bytes 1572872 | tf_op jit(solution)/shard_map/ppermute | solution.py:451
  160.4 31.3 %collective-permute-start.24 = (bf16[256,1024]{1,0:T(8,128)(2,1)}, bf16[256,1024]{1,0:T(8,128)(2,1)S(1)}, u32[]{:S(2)}, u32[]{:S(2)}) collective-permute-start(bf16[256,1024]{1,0:T(8,128)(2,1)} %get-tuple-element.64.own_mid), channel_id=1, source_target_pairs={{0,8},{24,16},{1,9},{25,17},{2,10},{26,18},{3,11},{27,19},{4,12},{... | collective-permute-start | bytes 1572872 | tf_op jit(solution)/shard_map/ppermute | solution.py:379
  166.7 30.1 %all-to-all-start.3 = ((bf16[4,256,512]{2,1,0:T(8,128)(2,1)}), bf16[4,256,512]{2,1,0:T(8,128)(2,1)S(1)}, u32[]{:S(2)}, u32[]{:S(2)}) async-start(bf16[4,256,512]{2,1,0:T(8,128)(2,1)} %all-to-all-done.2), calls=%async_computation.3 | async-start | bytes 2097152 | tf_op jit(solution)/shard_map/all_to_all | solution.py:443
  172.5 20.5 %collective-permute-start.26 = (bf16[256,1024]{1,0:T(8,128)(2,1)}, bf16[256,1024]{1,0:T(8,128)(2,1)}, u32[]{:S(2)}, u32[]{:S(2)}) collective-permute-start(bf16[256,1024]{1,0:T(8,128)(2,1)} %add.113), channel_id=1, source_target_pairs={{8,16},{16,8},{9,17},{17,9},{10,18},{18,10},{11,19},{19,11},{12,20... | collective-permute-start | bytes 1572872 | tf_op jit(solution)/shard_map/ppermute | solution.py:439
  174.0 26.2 %collective-permute-start.18 = (bf16[256,1024]{1,0:T(8,128)(2,1)S(1)}, bf16[256,1024]{1,0:T(8,128)(2,1)}, u32[]{:S(2)}, u32[]{:S(2)}) collective-permute-start(bf16[256,1024]{1,0:T(8,128)(2,1)S(1)} %copy-done.16), channel_id=1, source_target_pairs={{0,8},{24,16},{1,9},{25,17},{2,10},{26,18},{3,11},{27,19},{4,12},{... | collective-permute-start | bytes 1572872 | tf_op jit(solution)/shard_map/ppermute | solution.py:452
  182.1 14.7 %collective-permute-start.23 = (bf16[256,1024]{1,0:T(8,128)(2,1)}, bf16[256,1024]{1,0:T(8,128)(2,1)}, u32[]{:S(2)}, u32[]{:S(2)}) collective-permute-start(bf16[256,1024]{1,0:T(8,128)(2,1)} %add.112), channel_id=1, source_target_pairs={{8,0},{16,24},{9,1},{17,25},{10,2},{18,26},{11,3},{19,27},{12,4},{... | collective-permute-start | bytes 1572872 | tf_op jit(solution)/shard_map/ppermute | solution.py:441
  185.6 14.7 %collective-permute-start.20 = (bf16[256,1024]{1,0:T(8,128)(2,1)}, bf16[256,1024]{1,0:T(8,128)(2,1)}, u32[]{:S(2)}, u32[]{:S(2)}) collective-permute-start(bf16[256,1024]{1,0:T(8,128)(2,1)} %add.110), channel_id=1, source_target_pairs={{8,16},{16,8},{9,17},{17,9},{10,18},{18,10},{11,19},{19,11},{12,20... | collective-permute-start | bytes 1572872 | tf_op jit(solution)/shard_map/ppermute | solution.py:453
  191.7 14.5 %collective-permute-start.17 = (bf16[256,1024]{1,0:T(8,128)(2,1)}, bf16[256,1024]{1,0:T(8,128)(2,1)}, u32[]{:S(2)}, u32[]{:S(2)}) collective-permute-start(bf16[256,1024]{1,0:T(8,128)(2,1)} %add.109), channel_id=1, source_target_pairs={{8,0},{16,24},{9,1},{17,25},{10,2},{18,26},{11,3},{19,27},{12,4},{... | collective-permute-start | bytes 1572872 | tf_op jit(solution)/shard_map/ppermute | solution.py:454
  (28 other events, 243.2 us)

commit v5 on v4

--- a/solution.py
+++ b/solution.py
@@ -53,7 +53,7 @@
     for k in range(sems.shape[0]):
         copies[k].wait()
         part = pl.ds(k * step, step)
-        wide[...] = items[part].astype(F32).reshape(step * feats, width)
+        wide[: step * feats] = items[part].astype(F32).reshape(step * feats, width)
         for f in range(feats):
             by_feat[f, part, :] = wide[pl.ds(f, step, stride=feats), :].astype(BF16)
 
@@ -126,7 +126,7 @@
         out_specs=[pl.BlockSpec(memory_space=VMEM) for _ in groups],
         scratch_shapes=[
             VMEM((slots, feats, width), BF16),
-            VMEM((slots // chunks * feats, width), F32),
+            VMEM(((slots // chunks + 1) * feats, width), F32),
             VMEM((feats, slots, width), BF16),
             VMEM((feats, rows, width), I32),
             VMEM((rows, feats * width), BF16),

time: 210 us -> 210 us (level)
  no operation moved by 1% of the time
where the time goes in v5:
time: 210 us; the launch traced here: 209 us
  waiting for transfers between devices  71.1 us (34%)
  starting transfers between devices  64.4 us (31%)
  Pallas kernels  40.2 us (19%)
  other arithmetic  18.2 us (9%)
  local copies, waits for them, and re-layouts  14.3 us (7%)
    ppermute x3, waiting for transfers between devices, fetch(): return lax.ppermute(cut(source, *parts[which], tile), 'b', swap)  29.5 us
    pallas_call x3, Pallas kernels, multiply(): pl.pallas_call(functools.partial(multiply_kernel, (len(groups), count), s...  16.5 us
    pallas_call x2, Pallas kernels, pool(): pl.pallas_call(functools.partial(pool_kernel, groups, share, quarter, fea...  14.7 us
    ppermute x2, waiting for transfers between devices, shards(): far = lax.ppermute(mine, 'y', swap)  14.5 us
    unnamed x42, local copies, waits for them, and re-layouts  12.6 us
    ppermute x2, starting transfers between devices, shards(): in3 = lax.ppermute(near1, 'a', inward)  12.3 us
    all_to_all x2, starting transfers between devices, shards(): slots = lax.all_to_all(sent, ('a', 'b'), 0, 0, tiled=True)  10.7 us
    ppermute x2, waiting for transfers between devices, shards(): out3 = lax.ppermute(near0 + mid2, 'a', outward)  9.76 us
  transfers between devices with their start and end apart: 31, of which 15 were waited for; matrix products, arithmetic and copies ran while one was open for 10% of the time, Pallas kernels for 18%

profile of v5, /device:TPU:0, one launch (start us, length us, event | category | flops | bytes accessed | tf_op | source)
XLA Modules:
  0.0 208.5 jit_solution(8179900136259721061)
XLA Ops:
  2.3 3.0 %collective-permute-start.2 = (bf16[512,1024]{1,0:T(8,128)(2,1)S(1)}, bf16[512,1024]{1,0:T(8,128)(2,1)S(1)}, u32[]{:S(2)}, u32[]{:S(2)}) collective-permute-start(bf16[512,1024]{1,0:T(8,128)(2,1)S(1)} %cut.3), channel_id=1, source_target_pairs={{0,4},{4,0},{1,5},{5,1},{2,6},{6,2},{3,7},{7,3},{8,12},{12,8},{9,1... | collective-permute-start | bytes 3145736 | tf_op jit(solution)/shard_map/ppermute | solution.py:332
  5.4 7.6 %pool.2 = (bf16[2,2,112,512]{3,2,1,0:T(8,128)(2,1)S(1)}, bf16[2,2,96,512]{3,2,1,0:T(8,128)(2,1)}) custom-call(s32[1,8]{1,0:T(1,128)S(1)} %copy-done.18, s32[3]{0:T(128)S(1)} %get-tuple-element.79.spot_ref, s32[8,256]{1,0:T(8,128)S(1)} %get-tuple-element.78.length_ref, bf16[2048,16,128]{2,1,0:T(8,128)(2,1)} %items_ref.3), custom_call_target="tpu_custom_call" | custom-call | flops 1 | bytes 1 | tf_op jit(solution)/shard_map/pool/pallas_call | solution.py:112
  14.6 7.1 %pool.3 = (bf16[2,2,112,512]{3,2,1,0:T(8,128)(2,1)S(1)}, bf16[2,2,96,512]{3,2,1,0:T(8,128)(2,1)S(1)}) custom-call(s32[1,8]{1,0:T(1,128)S(1)} %copy-done.18, s32[3]{0:T(128)S(1)} %get-tuple-element.80.spot_ref, s32[8,256]{1,0:T(8,128)S(1)} %get-tuple-element.77.length_ref, bf16[2048,16,128]{2,1,0:T(8,128)(2,1)} %items_ref.3), custom_call_target="tpu_custom_call" | custom-call | flops 1 | bytes 1 | tf_op jit(solution)/shard_map/pool/pallas_call | solution.py:112
  21.7 3.3 %collective-permute-done = bf16[2,2,112,512]{3,2,1,0:T(8,128)(2,1)S(1)} collective-permute-done((bf16[2,2,112,512]{3,2,1,0:T(8,128)(2,1)S(1)}, bf16[2,2,112,512]{3,2,1,0:T(8,128)(2,1)S(1)}, u32[]{:S(2)}, u32[]{:S(2)}) %collective-permute-start) | collective-permute-done | bytes 458784 | tf_op jit(solution)/shard_map/ppermute | solution.py:348
  25.1 3.3 %collective-permute-done.2.refs_5_ = bf16[512,1024]{1,0:T(8,128)(2,1)S(1)} collective-permute-done((bf16[512,1024]{1,0:T(8,128)(2,1)S(1)}, bf16[512,1024]{1,0:T(8,128)(2,1)S(1)}, u32[]{:S(2)}, u32[]{:S(2)}) %collective-permute-start.2) | collective-permute-done | bytes 1048608 | tf_op jit(solution)/shard_map/ppermute | solution.py:332
  36.8 4.9 %all-to-all-start = ((bf16[8,112,512]{2,1,0:T(8,128)(2,1)}), bf16[8,112,512]{2,1,0:T(8,128)(2,1)S(1)}, u32[]{:S(2)}, u32[]{:S(2)}) async-start(bf16[8,112,512]{2,1,0:T(8,128)(2,1)} %bitcast.126), calls=%async_computation | async-start | bytes 1835008 | tf_op jit(solution)/shard_map/all_to_all | solution.py:373
  42.7 22.8 %collective-permute-done.9.refs_6_ = bf16[512,1024]{1,0:T(8,128)(2,1)S(1)} collective-permute-done((bf16[512,1024]{1,0:T(8,128)(2,1)}, bf16[512,1024]{1,0:T(8,128)(2,1)S(1)}, u32[]{:S(2)}, u32[]{:S(2)}) %collective-permute-start.9) | collective-permute-done | bytes 1048608 | tf_op jit(solution)/shard_map/ppermute | solution.py:332
  70.1 5.8 %all-to-all-start.1 = ((bf16[8,96,512]{2,1,0:T(8,128)(2,1)}), bf16[8,96,512]{2,1,0:T(8,128)(2,1)}, u32[]{:S(2)}, u32[]{:S(2)}) async-start(bf16[8,96,512]{2,1,0:T(8,128)(2,1)} %bitcast.127), calls=%async_computation.1 | async-start | bytes 1572864 | tf_op jit(solution)/shard_map/all_to_all | solution.py:373
  83.8 7.6 %collective-permute-done.4.refs_1_ = bf16[2,256,512]{2,1,0:T(8,128)(2,1)S(1)} collective-permute-done((bf16[2,256,512]{2,1,0:T(8,128)(2,1)S(1)}, bf16[2,256,512]{2,1,0:T(8,128)(2,1)S(1)}, u32[]{:S(2)}, u32[]{:S(2)}) %collective-permute-start.4) | collective-permute-done | bytes 524320 | tf_op jit(solution)/shard_map/ppermute | solution.py:387
  95.6 4.8 %multiply.3 = (bf16[256,1024]{1,0:T(8,128)(2,1)}, bf16[256,1024]{1,0:T(8,128)(2,1)}) custom-call(s32[4]{0:T(128)S(1)} %pad_add_fusion.spot_ref, s32[2]{0:T(128)S(1)} %get-tuple-element.68.place_ref, bf16[2,256,512]{2,1,0:T(8,128)(2,1)S(1)} %order.2.refs_0_, bf16[2,256,512]{2,1,0:T(8,128)(2,1)S(1)} %collective-permute-done.4.refs_1_, ...), custom_call_target="tpu_custom_call" | custom-call | flops 1 | bytes 1 | tf_op jit(solution)/shard_map/multiply/pallas_call | solution.py:246
  104.7 4.8 %all-to-all-start.2 = ((bf16[4,256,512]{2,1,0:T(8,128)(2,1)}), bf16[4,256,512]{2,1,0:T(8,128)(2,1)}, u32[]{:S(2)}, u32[]{:S(2)}) async-start(bf16[4,256,512]{2,1,0:T(8,128)(2,1)} %pad_maximum_fusion), calls=%async_computation.2 | async-start | bytes 2097152 | tf_op jit(solution)/shard_map/all_to_all | solution.py:409
  109.5 6.9 %collective-permute-done.11.refs_1_.refs_5_ = bf16[2,256,512]{2,1,0:T(8,128)(2,1)} collective-permute-done((bf16[2,256,512]{2,1,0:T(8,128)(2,1)S(1)}, bf16[2,256,512]{2,1,0:T(8,128)(2,1)}, u32[]{:S(2)}, u32[]{:S(2)}) %collective-permute-start.11) | collective-permute-done | bytes 524320 | tf_op jit(solution)/shard_map/ppermute | solution.py:387
  121.8 4.1 %multiply.4 = (bf16[256,1024]{1,0:T(8,128)(2,1)S(1)}, bf16[256,1024]{1,0:T(8,128)(2,1)S(1)}) custom-call(s32[4]{0:T(128)S(1)} %pad_add_fusion.spot_ref, s32[2]{0:T(128)S(1)} %get-tuple-element.68.place_ref, bf16[2,256,512]{2,1,0:T(8,128)(2,1)S(1)} %order.3.refs_0_.refs_4_, bf16[2,256,512]{2,1,0:T(8,128)(2,1)} %collective-permute-done.11.refs_1_.refs_5_, ...), custom_call_target="tpu_custom_call" | custom-call | flops 1 | bytes 1 | tf_op jit(solution)/shard_map/multiply/pallas_call | solution.py:246
  125.9 3.7 %collective-permute-start.21 = (bf16[256,1024]{1,0:T(8,128)(2,1)S(1)}, bf16[256,1024]{1,0:T(8,128)(2,1)S(1)}, u32[]{:S(2)}, u32[]{:S(2)}) collective-permute-start(bf16[256,1024]{1,0:T(8,128)(2,1)S(1)} %get-tuple-element.65), channel_id=1, source_target_pairs={{0,8},{24,16},{1,9},{25,17},{2,10},{26,18},{3,11},{27,19},{4,12},{... | collective-permute-start | bytes 1572872 | tf_op jit(solution)/shard_map/ppermute | solution.py:437
  129.6 3.4 %collective-permute-done.14.refs_9_ = bf16[1024,1024]{1,0:T(8,128)(2,1)} collective-permute-done((bf16[1024,1024]{1,0:T(8,128)(2,1)}, bf16[1024,1024]{1,0:T(8,128)(2,1)}, u32[]{:S(2)}, u32[]{:S(2)}) %collective-permute-start.14) | collective-permute-done | bytes 2097184 | tf_op jit(solution)/shard_map/ppermute | solution.py:332
  133.0 7.6 %multiply.5 = (bf16[256,1024]{1,0:T(8,128)(2,1)}, bf16[256,1024]{1,0:T(8,128)(2,1)S(1)}, bf16[256,1024]{1,0:T(8,128)(2,1)S(1)}, bf16[256,1024]{1,0:T(8,128)(2,1)S(1)}) custom-call(s32[4]{0:T(128)S(1)} %pad_add_fusion.spot_ref, s32[4]{0:T(128)S(1)} %pad_add_fusion.2.place_ref, bf16[2,256,512]{2,1,0:T(8,128)(2,1)S(1)} %order.2.refs_0_, ...), custom_call_target="tpu_custom_call" | custom-call | flops 1 | bytes 1 | tf_op jit(solution)/shard_map/multiply/pallas_call | solution.py:246
  141.4 4.2 %collective-permute-start.15 = (bf16[256,1024]{1,0:T(8,128)(2,1)S(1)}, bf16[256,1024]{1,0:T(8,128)(2,1)S(1)}, u32[]{:S(2)}, u32[]{:S(2)}) collective-permute-start(bf16[256,1024]{1,0:T(8,128)(2,1)S(1)} %get-tuple-element.60), channel_id=1, source_target_pairs={{0,8},{24,16},{1,9},{25,17},{2,10},{26,18},{3,11},{27,19},{4,12},{... | collective-permute-start | bytes 1572872 | tf_op jit(solution)/shard_map/ppermute | solution.py:449
  150.1 3.2 %collective-permute-start.19 = (bf16[256,1024]{1,0:T(8,128)(2,1)}, bf16[256,1024]{1,0:T(8,128)(2,1)}, u32[]{:S(2)}, u32[]{:S(2)}) collective-permute-start(bf16[256,1024]{1,0:T(8,128)(2,1)} %get-tuple-element.61), channel_id=1, source_target_pairs={{0,8},{24,16},{1,9},{25,17},{2,10},{26,18},{3,11},{27,19},{4,12},{... | collective-permute-start | bytes 1572872 | tf_op jit(solution)/shard_map/ppermute | solution.py:450
  153.3 4.6 %collective-permute-done.15 = bf16[256,1024]{1,0:T(8,128)(2,1)S(1)} collective-permute-done((bf16[256,1024]{1,0:T(8,128)(2,1)S(1)}, bf16[256,1024]{1,0:T(8,128)(2,1)S(1)}, u32[]{:S(2)}, u32[]{:S(2)}) %collective-permute-start.15) | collective-permute-done | bytes 524320 | tf_op jit(solution)/shard_map/ppermute | solution.py:449
  160.4 6.3 %collective-permute-start.24 = (bf16[256,1024]{1,0:T(8,128)(2,1)}, bf16[256,1024]{1,0:T(8,128)(2,1)S(1)}, u32[]{:S(2)}, u32[]{:S(2)}) collective-permute-start(bf16[256,1024]{1,0:T(8,128)(2,1)} %get-tuple-element.64.own_mid), channel_id=1, source_target_pairs={{0,8},{24,16},{1,9},{25,17},{2,10},{26,18},{3,11},{27,19},{4,12},{... | collective-permute-start | bytes 1572872 | tf_op jit(solution)/shard_map/ppermute | solution.py:379
  166.7 3.5 %all-to-all-start.3 = ((bf16[4,256,512]{2,1,0:T(8,128)(2,1)}), bf16[4,256,512]{2,1,0:T(8,128)(2,1)S(1)}, u32[]{:S(2)}, u32[]{:S(2)}) async-start(bf16[4,256,512]{2,1,0:T(8,128)(2,1)} %all-to-all-done.2), calls=%async_computation.3 | async-start | bytes 2097152 | tf_op jit(solution)/shard_map/all_to_all | solution.py:443
  174.0 6.0 %collective-permute-start.18 = (bf16[256,1024]{1,0:T(8,128)(2,1)S(1)}, bf16[256,1024]{1,0:T(8,128)(2,1)}, u32[]{:S(2)}, u32[]{:S(2)}) collective-permute-start(bf16[256,1024]{1,0:T(8,128)(2,1)S(1)} %copy-done.16), channel_id=1, source_target_pairs={{0,8},{24,16},{1,9},{25,17},{2,10},{26,18},{3,11},{27,19},{4,12},{... | collective-permute-start | bytes 1572872 | tf_op jit(solution)/shard_map/ppermute | solution.py:452
  193.1 3.7 %collective-permute-done.23.outer = bf16[256,1024]{1,0:T(8,128)(2,1)} collective-permute-done((bf16[256,1024]{1,0:T(8,128)(2,1)}, bf16[256,1024]{1,0:T(8,128)(2,1)}, u32[]{:S(2)}, u32[]{:S(2)}) %collective-permute-start.23) | collective-permute-done | bytes 524320 | tf_op jit(solution)/shard_map/ppermute | solution.py:441
  200.3 6.0 %collective-permute-done.17.outer = bf16[256,1024]{1,0:T(8,128)(2,1)} collective-permute-done((bf16[256,1024]{1,0:T(8,128)(2,1)}, bf16[256,1024]{1,0:T(8,128)(2,1)}, u32[]{:S(2)}, u32[]{:S(2)}) %collective-permute-start.17) | collective-permute-done | bytes 524320 | tf_op jit(solution)/shard_map/ppermute | solution.py:454
  (116 shorter events, 69.9 us)
Async XLA Ops:
  2.3 26.2 %collective-permute-start.2 = (bf16[512,1024]{1,0:T(8,128)(2,1)S(1)}, bf16[512,1024]{1,0:T(8,128)(2,1)S(1)}, u32[]{:S(2)}, u32[]{:S(2)}) collective-permute-start(bf16[512,1024]{1,0:T(8,128)(2,1)S(1)} %cut.3), channel_id=1, source_target_pairs={{0,4},{4,0},{1,5},{5,1},{2,6},{6,2},{3,7},{7,3},{8,12},{12,8},{9,1... | collective-permute-start | bytes 3145736 | tf_op jit(solution)/shard_map/ppermute | solution.py:332
  13.0 12.1 %collective-permute-start = (bf16[2,2,112,512]{3,2,1,0:T(8,128)(2,1)S(1)}, bf16[2,2,112,512]{3,2,1,0:T(8,128)(2,1)S(1)}, u32[]{:S(2)}, u32[]{:S(2)}) collective-permute-start(bf16[2,2,112,512]{3,2,1,0:T(8,128)(2,1)S(1)} %get-tuple-element.36), channel_id=1, source_target_pairs={{0,2},{2,0},{1,3},{3,1},{4,6},{6,4},{5,7},{7,5},{8,10},{10,8},{9,1... | collective-permute-start | bytes 1376264 | tf_op jit(solution)/shard_map/ppermute | solution.py:348
  29.2 12.5 %collective-permute-start.7 = (bf16[2,2,96,512]{3,2,1,0:T(8,128)(2,1)}, bf16[2,2,96,512]{3,2,1,0:T(8,128)(2,1)}, u32[]{:S(2)}, u32[]{:S(2)}) collective-permute-start(bf16[2,2,96,512]{3,2,1,0:T(8,128)(2,1)} %get-tuple-element.40), channel_id=1, source_target_pairs={{0,2},{2,0},{1,3},{3,1},{4,6},{6,4},{5,7},{7,5},{8,10},{10,8},{9,1... | collective-permute-start | bytes 1179656 | tf_op jit(solution)/shard_map/ppermute | solution.py:348
  32.0 33.6 %collective-permute-start.9 = (bf16[512,1024]{1,0:T(8,128)(2,1)}, bf16[512,1024]{1,0:T(8,128)(2,1)S(1)}, u32[]{:S(2)}, u32[]{:S(2)}) collective-permute-start(bf16[512,1024]{1,0:T(8,128)(2,1)} %cut.4), channel_id=1, source_target_pairs={{0,4},{4,0},{1,5},{5,1},{2,6},{6,2},{3,7},{7,3},{8,12},{12,8},{9,1... | collective-permute-start | bytes 3145736 | tf_op jit(solution)/shard_map/ppermute | solution.py:332
  36.8 33.3 %all-to-all-start = ((bf16[8,112,512]{2,1,0:T(8,128)(2,1)}), bf16[8,112,512]{2,1,0:T(8,128)(2,1)S(1)}, u32[]{:S(2)}, u32[]{:S(2)}) async-start(bf16[8,112,512]{2,1,0:T(8,128)(2,1)} %bitcast.126), calls=%async_computation | async-start | bytes 1835008 | tf_op jit(solution)/shard_map/all_to_all | solution.py:373
  42.6 23.0 %collective-permute-start.8 = (bf16[2,96,512]{2,1,0:T(8,128)(2,1)S(1)}, bf16[2,96,512]{2,1,0:T(8,128)(2,1)S(1)}, u32[]{:S(2)}, u32[]{:S(2)}) collective-permute-start(bf16[2,96,512]{2,1,0:T(8,128)(2,1)S(1)} %slice_bitcast_fusion.4), channel_id=1, source_target_pairs={{0,1},{1,0},{2,3},{3,2},{4,5},{5,4},{6,7},{7,6},{8,9},{9,8},{10,11... | collective-permute-start | bytes 589832 | tf_op jit(solution)/shard_map/ppermute | solution.py:353
  70.1 30.3 %all-to-all-start.1 = ((bf16[8,96,512]{2,1,0:T(8,128)(2,1)}), bf16[8,96,512]{2,1,0:T(8,128)(2,1)}, u32[]{:S(2)}, u32[]{:S(2)}) async-start(bf16[8,96,512]{2,1,0:T(8,128)(2,1)} %bitcast.127), calls=%async_computation.1 | async-start | bytes 1572864 | tf_op jit(solution)/shard_map/all_to_all | solution.py:373
  77.6 13.8 %collective-permute-start.4 = (bf16[2,256,512]{2,1,0:T(8,128)(2,1)S(1)}, bf16[2,256,512]{2,1,0:T(8,128)(2,1)S(1)}, u32[]{:S(2)}, u32[]{:S(2)}) collective-permute-start(bf16[2,256,512]{2,1,0:T(8,128)(2,1)S(1)} %order.2.refs_0_), channel_id=1, source_target_pairs={{0,2},{2,0},{1,3},{3,1},{4,6},{6,4},{5,7},{7,5},{8,10},{10,8},{9,1... | collective-permute-start | bytes 1572872 | tf_op jit(solution)/shard_map/ppermute | solution.py:387
  81.8 51.2 %collective-permute-start.14 = (bf16[1024,1024]{1,0:T(8,128)(2,1)}, bf16[1024,1024]{1,0:T(8,128)(2,1)}, u32[]{:S(2)}, u32[]{:S(2)}) collective-permute-start(bf16[1024,1024]{1,0:T(8,128)(2,1)} %cut.5), channel_id=1, source_target_pairs={{0,4},{4,0},{1,5},{5,1},{2,6},{6,2},{3,7},{7,3},{8,12},{12,8},{9,1... | collective-permute-start | bytes 6291464 | tf_op jit(solution)/shard_map/ppermute | solution.py:332
  102.2 14.3 %collective-permute-start.11 = (bf16[2,256,512]{2,1,0:T(8,128)(2,1)S(1)}, bf16[2,256,512]{2,1,0:T(8,128)(2,1)}, u32[]{:S(2)}, u32[]{:S(2)}) collective-permute-start(bf16[2,256,512]{2,1,0:T(8,128)(2,1)S(1)} %order.3.refs_0_.refs_4_), channel_id=1, source_target_pairs={{0,2},{2,0},{1,3},{3,1},{4,6},{6,4},{5,7},{7,5},{8,10},{10,8},{9,1... | collective-permute-start | bytes 1572872 | tf_op jit(solution)/shard_map/ppermute | solution.py:387
  104.7 62.0 %all-to-all-start.2 = ((bf16[4,256,512]{2,1,0:T(8,128)(2,1)}), bf16[4,256,512]{2,1,0:T(8,128)(2,1)}, u32[]{:S(2)}, u32[]{:S(2)}) async-start(bf16[4,256,512]{2,1,0:T(8,128)(2,1)} %pad_maximum_fusion), calls=%async_computation.2 | async-start | bytes 2097152 | tf_op jit(solution)/shard_map/all_to_all | solution.py:409
  125.9 21.8 %collective-permute-start.21 = (bf16[256,1024]{1,0:T(8,128)(2,1)S(1)}, bf16[256,1024]{1,0:T(8,128)(2,1)S(1)}, u32[]{:S(2)}, u32[]{:S(2)}) collective-permute-start(bf16[256,1024]{1,0:T(8,128)(2,1)S(1)} %get-tuple-element.65), channel_id=1, source_target_pairs={{0,8},{24,16},{1,9},{25,17},{2,10},{26,18},{3,11},{27,19},{4,12},{... | collective-permute-start | bytes 1572872 | tf_op jit(solution)/shard_map/ppermute | solution.py:437
  141.4 16.6 %collective-permute-start.15 = (bf16[256,1024]{1,0:T(8,128)(2,1)S(1)}, bf16[256,1024]{1,0:T(8,128)(2,1)S(1)}, u32[]{:S(2)}, u32[]{:S(2)}) collective-permute-start(bf16[256,1024]{1,0:T(8,128)(2,1)S(1)} %get-tuple-element.60), channel_id=1, source_target_pairs={{0,8},{24,16},{1,9},{25,17},{2,10},{26,18},{3,11},{27,19},{4,12},{... | collective-permute-start | bytes 1572872 | tf_op jit(solution)/shard_map/ppermute | solution.py:449
  145.6 24.7 %collective-permute-start.25 = (bf16[256,1024]{1,0:T(8,128)(2,1)}, bf16[256,1024]{1,0:T(8,128)(2,1)}, u32[]{:S(2)}, u32[]{:S(2)}) collective-permute-start(bf16[256,1024]{1,0:T(8,128)(2,1)} %get-tuple-element.66), channel_id=1, source_target_pairs={{0,8},{24,16},{1,9},{25,17},{2,10},{26,18},{3,11},{27,19},{4,12},{... | collective-permute-start | bytes 1572872 | tf_op jit(solution)/shard_map/ppermute | solution.py:378
  148.7 25.3 %collective-permute-start.22 = (bf16[256,1024]{1,0:T(8,128)(2,1)}, bf16[256,1024]{1,0:T(8,128)(2,1)}, u32[]{:S(2)}, u32[]{:S(2)}) collective-permute-start(bf16[256,1024]{1,0:T(8,128)(2,1)} %add.111), channel_id=1, source_target_pairs={{8,16},{16,8},{9,17},{17,9},{10,18},{18,10},{11,19},{19,11},{12,20... | collective-permute-start | bytes 1572872 | tf_op jit(solution)/shard_map/ppermute | solution.py:440
  150.1 32.0 %collective-permute-start.19 = (bf16[256,1024]{1,0:T(8,128)(2,1)}, bf16[256,1024]{1,0:T(8,128)(2,1)}, u32[]{:S(2)}, u32[]{:S(2)}) collective-permute-start(bf16[256,1024]{1,0:T(8,128)(2,1)} %get-tuple-element.61), channel_id=1, source_target_pairs={{0,8},{24,16},{1,9},{25,17},{2,10},{26,18},{3,11},{27,19},{4,12},{... | collective-permute-start | bytes 1572872 | tf_op jit(solution)/shard_map/ppermute | solution.py:450
  158.9 26.7 %collective-permute-start.16 = (bf16[256,1024]{1,0:T(8,128)(2,1)}, bf16[256,1024]{1,0:T(8,128)(2,1)}, u32[]{:S(2)}, u32[]{:S(2)}) collective-permute-start(bf16[256,1024]{1,0:T(8,128)(2,1)} %add.108), channel_id=1, source_target_pairs={{8,16},{16,8},{9,17},{17,9},{10,18},{18,10},{11,19},{19,11},{12,20... | collective-permute-start | bytes 1572872 | tf_op jit(solution)/shard_map/ppermute | solution.py:451
  160.4 31.3 %collective-permute-start.24 = (bf16[256,1024]{1,0:T(8,128)(2,1)}, bf16[256,1024]{1,0:T(8,128)(2,1)S(1)}, u32[]{:S(2)}, u32[]{:S(2)}) collective-permute-start(bf16[256,1024]{1,0:T(8,128)(2,1)} %get-tuple-element.64.own_mid), channel_id=1, source_target_pairs={{0,8},{24,16},{1,9},{25,17},{2,10},{26,18},{3,11},{27,19},{4,12},{... | collective-permute-start | bytes 1572872 | tf_op jit(solution)/shard_map/ppermute | solution.py:379
  166.7 30.1 %all-to-all-start.3 = ((bf16[4,256,512]{2,1,0:T(8,128)(2,1)}), bf16[4,256,512]{2,1,0:T(8,128)(2,1)S(1)}, u32[]{:S(2)}, u32[]{:S(2)}) async-start(bf16[4,256,512]{2,1,0:T(8,128)(2,1)} %all-to-all-done.2), calls=%async_computation.3 | async-start | bytes 2097152 | tf_op jit(solution)/shard_map/all_to_all | solution.py:443
  172.5 20.5 %collective-permute-start.26 = (bf16[256,1024]{1,0:T(8,128)(2,1)}, bf16[256,1024]{1,0:T(8,128)(2,1)}, u32[]{:S(2)}, u32[]{:S(2)}) collective-permute-start(bf16[256,1024]{1,0:T(8,128)(2,1)} %add.113), channel_id=1, source_target_pairs={{8,16},{16,8},{9,17},{17,9},{10,18},{18,10},{11,19},{19,11},{12,20... | collective-permute-start | bytes 1572872 | tf_op jit(solution)/shard_map/ppermute | solution.py:439
  174.0 26.2 %collective-permute-start.18 = (bf16[256,1024]{1,0:T(8,128)(2,1)S(1)}, bf16[256,1024]{1,0:T(8,128)(2,1)}, u32[]{:S(2)}, u32[]{:S(2)}) collective-permute-start(bf16[256,1024]{1,0:T(8,128)(2,1)S(1)} %copy-done.16), channel_id=1, source_target_pairs={{0,8},{24,16},{1,9},{25,17},{2,10},{26,18},{3,11},{27,19},{4,12},{... | collective-permute-start | bytes 1572872 | tf_op jit(solution)/shard_map/ppermute | solution.py:452
  182.1 14.7 %collective-permute-start.23 = (bf16[256,1024]{1,0:T(8,128)(2,1)}, bf16[256,1024]{1,0:T(8,128)(2,1)}, u32[]{:S(2)}, u32[]{:S(2)}) collective-permute-start(bf16[256,1024]{1,0:T(8,128)(2,1)} %add.112), channel_id=1, source_target_pairs={{8,0},{16,24},{9,1},{17,25},{10,2},{18,26},{11,3},{19,27},{12,4},{... | collective-permute-start | bytes 1572872 | tf_op jit(solution)/shard_map/ppermute | solution.py:441
  185.6 14.7 %collective-permute-start.20 = (bf16[256,1024]{1,0:T(8,128)(2,1)}, bf16[256,1024]{1,0:T(8,128)(2,1)}, u32[]{:S(2)}, u32[]{:S(2)}) collective-permute-start(bf16[256,1024]{1,0:T(8,128)(2,1)} %add.110), channel_id=1, source_target_pairs={{8,16},{16,8},{9,17},{17,9},{10,18},{18,10},{11,19},{19,11},{12,20... | collective-permute-start | bytes 1572872 | tf_op jit(solution)/shard_map/ppermute | solution.py:453
  191.7 14.5 %collective-permute-start.17 = (bf16[256,1024]{1,0:T(8,128)(2,1)}, bf16[256,1024]{1,0:T(8,128)(2,1)}, u32[]{:S(2)}, u32[]{:S(2)}) collective-permute-start(bf16[256,1024]{1,0:T(8,128)(2,1)} %add.109), channel_id=1, source_target_pairs={{8,0},{16,24},{9,1},{17,25},{10,2},{18,26},{11,3},{19,27},{12,4},{... | collective-permute-start | bytes 1572872 | tf_op jit(solution)/shard_map/ppermute | solution.py:454
  (28 other events, 243.2 us)
